TPU v7x, 32 devices: a whole 2x2x4 slice. The times are simulated.
32 devices in a mesh: ctx: 16 (over z, x, core), head: 2 (over y).
Axes of the slice: x: 2, y: 2, z: 4, core: 2. Of those that a mesh axis runs over, the one named last changes fastest.
Arguments:
- keys: bfloat16 [8192, 1024], P('ctx', 'head'), may hold values from -6 to 6
- values: bfloat16 [8192, 1024], P('ctx', 'head'), may hold values from -6 to 6
- rates: float32 [2, 8192], P('head', 'ctx'), may hold values from 0.05 to 1
- queries: bfloat16 [8192, 1024], P(('ctx', 'head')), may hold values from -6 to 6
- fast_weights: bfloat16 [2, 3, 512, 512], P('head'), may hold values from -4 to 4
- gate: bfloat16 [8192, 1024], P(('ctx', 'head')), may hold values from -6 to 6
- gain: float32 [1024], replicated, may hold values from 0.1 to 1.9
Outputs:
- layer_out: bfloat16 [8192, 1024], P(('ctx', 'head'))
- new_weights: bfloat16 [2, 3, 512, 512], P('head')
All inputs are finite; a program needn't handle non-finite values.
Results may differ from a plain program's by a relative error of at most 0.023.
Values may be sent and summed in bfloat16 or wider, within the bound.
No kernel may reach another device: no remote copies, remote signals or barrier semaphores. Data moves between devices by JAX's collectives and lax.ppermute only.
A program may use at most 64 MiB of HBM per device.

v0:
```python
import jax
import jax.numpy as jnp
from jax import lax
from jax.sharding import PartitionSpec as P

NS_STEPS = 5


coef_a = 3.4445
coef_b = -4.775
coef_c = 2.0315


def bmm(form, left, right):
    return jnp.einsum(form, left, right, preferred_element_type=jnp.float32)


def memory_read(query_rows, weight_set):
    scale = weight_set.shape[-1] ** (-0.5)
    r_one = bmm("thi,hij->thj", query_rows, weight_set[:, 0]) * scale
    r_three = bmm("thi,hij->thj", query_rows, weight_set[:, 1]) * scale
    hq = (jax.nn.silu(r_one) * r_three).astype(jnp.bfloat16)
    return (bmm("thj,hjc->thc", hq, weight_set[:, 2]) * scale).astype(jnp.bfloat16)


def poly_step(iterate_part, gram_part, square_part, whole):
    poly = (coef_b * gram_part.astype(jnp.float32) + coef_c * square_part).astype(jnp.bfloat16)
    return (coef_a * iterate_part.astype(jnp.float32) + bmm("hmrk,hmkc->hmrc", poly, whole)).astype(
        jnp.bfloat16
    )


def local(keys, values, rates, queries, fast_weights, gate, gain):
    heads_here = fast_weights.shape[0]
    width = fast_weights.shape[-1]
    scale = width ** (-0.5)
    step_size = 0.4 * jnp.sqrt(jnp.float32(width))
    tok_rows = keys.shape[0]
    key_rows = keys.reshape(tok_rows, heads_here, width)
    value_rows = values.reshape(tok_rows, heads_here, width)
    g_one = bmm("thi,hij->thj", key_rows, fast_weights[:, 0]) * scale
    g_three = bmm("thi,hij->thj", key_rows, fast_weights[:, 1]) * scale
    sig = jax.nn.sigmoid(g_one)
    hidden = (g_one * sig * g_three).astype(jnp.bfloat16)
    grad_out = (-(rates.T[:, :, None] * value_rows.astype(jnp.float32))).astype(jnp.bfloat16)
    d_two = bmm("thj,thc->hjc", hidden, grad_out) * scale
    d_hidden = bmm("thc,hjc->thj", grad_out, fast_weights[:, 2]) * scale
    dg_one = (d_hidden * g_three * sig * (1.0 + g_one * (1.0 - sig))).astype(jnp.bfloat16)
    dg_three = (d_hidden * (g_one * sig)).astype(jnp.bfloat16)
    d_one = bmm("thi,thj->hij", key_rows, dg_one) * scale
    d_three = bmm("thi,thj->hij", key_rows, dg_three) * scale
    partial_value = jnp.stack([d_one, d_three, d_two], axis=1)
    grads = lax.psum(partial_value.astype(jnp.bfloat16), "ctx").astype(jnp.float32)
    total = jnp.sum(grads * grads, axis=(2, 3), keepdims=True)
    iterate = (grads / (jnp.sqrt(total) + 1e-07)).astype(jnp.bfloat16)
    for step in range(NS_STEPS):
        gram = bmm("hmrc,hmkc->hmrk", iterate, iterate).astype(jnp.bfloat16)
        square = bmm("hmrk,hmkc->hmrc", gram, gram)
        iterate = poly_step(iterate, gram, square, iterate)
    new_weights = (
        fast_weights.astype(jnp.float32) - step_size * iterate.astype(jnp.float32)
    ).astype(jnp.bfloat16)
    query_rows = queries.shape[0]
    all_heads = queries.shape[1] // width
    query_heads = queries.reshape(query_rows, all_heads, width)
    every_weight = lax.all_gather(fast_weights, "head", axis=0, tiled=True)
    read = memory_read(query_heads, every_weight)
    read32 = read.astype(jnp.float32)
    mean_sq = jnp.mean(read32 * read32, axis=-1, keepdims=True)
    gate32 = gate.astype(jnp.float32).reshape(query_rows, all_heads, width)
    normed = (
        read32 * lax.rsqrt(mean_sq + 1e-06) * gain.reshape(all_heads, width) * jax.nn.silu(gate32)
    )
    return (normed.reshape(query_rows, all_heads * width).astype(jnp.bfloat16), new_weights)


def solution(mesh):
    in_specs = (
        P("ctx", "head"),
        P("ctx", "head"),
        P("head", "ctx"),
        P(("ctx", "head"), None),
        P("head", None, None, None),
        P(("ctx", "head"), None),
        P(),
    )
    out_specs = (P(("ctx", "head"), None), P("head", None, None, None))
    return jax.shard_map(local, mesh=mesh, in_specs=in_specs, out_specs=out_specs, check_vma=False)
```

profile of v0, /device:TPU:0, one launch (start us, length us, event | category | flops | bytes accessed | tf_op | source)
XLA Modules:
  0.0 182.4 jit_solution(7772904107537436653)
XLA Ops:
  8.0 0.0 copy-start
  8.0 0.0 copy-start.1
  8.0 0.0 all-reduce.2.cloned.1.call-start
  8.1 1.0 copy-done
  9.0 1.5 fusion.18
  10.5 0.0 copy-done.1
  10.5 0.0 copy-start.8
  10.5 0.0 copy-start.9
  10.6 0.4 fusion.17
  11.0 0.6 copy-done.8
  11.6 0.0 copy-done.9
  11.6 0.5 fusion.19
  12.1 0.7 fusion.32
  12.8 0.5 fusion.33
  13.4 0.8 fusion.34
  14.2 1.3 pad_maximum_fusion
  15.5 0.0 all-reduce.2.cloned.1.call-update
  15.5 0.0 all-gather.2.cloned.1.call-start
  15.6 1.6 copy.9
  17.2 0.0 all-gather.2.cloned.1.call-update
  17.2 0.0 copy-start.4
  17.2 1.6 copy.15
  18.8 0.0 copy-done.4
  18.8 0.0 copy-start.5
  18.8 0.0 copy-start.7
  18.8 0.2 copy.14
  19.0 0.8 copy-done.5
  19.8 1.0 copy.71
  20.8 0.0 copy-done.7
  20.9 93.5 %all-reduce.2.cloned.1.call-done = bf16[1,3,512,512]{2,3,1,0:T(8,128)(2,1)} async-done(((bf16[1,3,512,512]{2,3,1,0:T(8,128)(2,1)}), bf16[1,3,512,512]{2,3,1,0:T(8,128)(2,1)}) %all-reduce.2.cloned.1.call-update) | async-done | bytes 1572880 | tf_op jit(solution)/shard_map/psum | solution.py:53
  114.3 0.0 copy-start.3
  114.3 2.0 %fusion = f32[3]{0:T(128)S(1)} fusion(bf16[1,3,512,512]{2,3,1,0:T(8,128)(2,1)} %all-reduce.2.cloned.1.call-done), kind=kLoop, calls=%fused_computation.2 | loop fusion | flops 2359293 | bytes 1572876 | tf_op jit(solution)/shard_map/reduce_sum | solution.py:54
  116.4 0.0 copy-done.3
  116.4 2.4 %convolution_convert_fusion.4 = bf16[3,512,512]{2,1,0:T(8,128)(2,1)} fusion(bf16[1,3,512,512]{2,3,1,0:T(8,128)(2,1)S(1)} %copy-done.3, f32[3]{0:T(128)S(1)} %sqrt_add_fusion), kind=kOutput, calls=%fused_computation.24 | convolution fusion | flops 808452096 | bytes 3145740 | tf_op jit(solution)/shard_map/hmrc,hmkc->hmrk/dot_general | solution.py:15
  118.7 5.8 %fusion.6 = bf16[1,3,512,512]{2,3,1,0:T(8,128)(2,1)} fusion(bf16[3,512,512]{2,1,0:T(8,128)(2,1)} %convolution_convert_fusion.4, f32[3]{0:T(128)S(1)} %sqrt_add_fusion, bf16[1,3,512,512]{2,3,1,0:T(8,128)(2,1)S(1)} %copy-done.3), kind=kOutput, calls=%fused_computation.13 | convolution fusion | flops 1622409216 | bytes 4718604 | tf_op jit(solution)/shard_map/hmrk,hmkc->hmrc/dot_general | solution.py:15
  124.6 0.0 copy-start.10
  124.6 4.2 %convolution_convert_fusion.3 = bf16[3,512,512]{2,1,0:T(8,128)(2,1)} fusion(bf16[1,3,512,512]{2,3,1,0:T(8,128)(2,1)} %fusion.6), kind=kOutput, calls=%fused_computation.23 | convolution fusion | flops 806092800 | bytes 3145728 | tf_op jit(solution)/shard_map/hmrc,hmkc->hmrk/dot_general | solution.py:15
  128.8 0.0 copy-done.10
  128.8 5.7 %fusion.5 = bf16[1,3,512,512]{2,3,1,0:T(8,128)(2,1)} fusion(bf16[1,3,512,512]{2,3,1,0:T(8,128)(2,1)S(1)} %copy-done.10, bf16[3,512,512]{2,1,0:T(8,128)(2,1)} %convolution_convert_fusion.3), kind=kOutput, calls=%fused_computation.11 | convolution fusion | flops 1617690624 | bytes 4718592 | tf_op jit(solution)/shard_map/hmrk,hmkc->hmrc/dot_general | solution.py:15
  134.6 0.0 copy-start.11
  134.6 4.2 %convolution_convert_fusion.2 = bf16[3,512,512]{2,1,0:T(8,128)(2,1)} fusion(bf16[1,3,512,512]{2,3,1,0:T(8,128)(2,1)} %fusion.5), kind=kOutput, calls=%fused_computation.22 | convolution fusion | flops 806092800 | bytes 3145728 | tf_op jit(solution)/shard_map/hmrc,hmkc->hmrk/dot_general | solution.py:15
  138.8 0.0 copy-done.11
  138.8 5.7 %fusion.4 = bf16[1,3,512,512]{2,3,1,0:T(8,128)(2,1)} fusion(bf16[1,3,512,512]{2,3,1,0:T(8,128)(2,1)S(1)} %copy-done.11, bf16[3,512,512]{2,1,0:T(8,128)(2,1)} %convolution_convert_fusion.2), kind=kOutput, calls=%fused_computation.9 | convolution fusion | flops 1617690624 | bytes 4718592 | tf_op jit(solution)/shard_map/hmrk,hmkc->hmrc/dot_general | solution.py:15
  144.5 0.0 copy-start.12
  144.5 4.2 %convolution_convert_fusion.1 = bf16[3,512,512]{2,1,0:T(8,128)(2,1)} fusion(bf16[1,3,512,512]{2,3,1,0:T(8,128)(2,1)} %fusion.4), kind=kOutput, calls=%fused_computation.21 | convolution fusion | flops 806092800 | bytes 3145728 | tf_op jit(solution)/shard_map/hmrc,hmkc->hmrk/dot_general | solution.py:15
  148.7 0.0 copy-done.12
  148.8 5.7 %fusion.3 = bf16[1,3,512,512]{2,3,1,0:T(8,128)(2,1)} fusion(bf16[1,3,512,512]{2,3,1,0:T(8,128)(2,1)S(1)} %copy-done.12, bf16[3,512,512]{2,1,0:T(8,128)(2,1)} %convolution_convert_fusion.1), kind=kOutput, calls=%fused_computation.7 | convolution fusion | flops 1617690624 | bytes 4718592 | tf_op jit(solution)/shard_map/hmrk,hmkc->hmrc/dot_general | solution.py:15
  154.5 0.0 copy-start.2
  154.5 4.4 %convolution_convert_fusion = bf16[3,512,512]{2,1,0:T(8,128)(2,1)} fusion(bf16[1,3,512,512]{2,3,1,0:T(8,128)(2,1)} %fusion.3), kind=kOutput, calls=%fused_computation.20 | convolution fusion | flops 806092800 | bytes 3145728 | tf_op jit(solution)/shard_map/hmrc,hmkc->hmrk/dot_general | solution.py:15
  158.9 0.0 copy-done.2
  158.9 6.6 %subtract_convert_fusion = bf16[1,3,512,512]{2,3,1,0:T(8,128)(2,1)} fusion(bf16[1,3,512,512]{2,3,1,0:T(8,128)(2,1)S(1)} %copy-done.2, bf16[1,3,512,512]{2,3,1,0:T(8,128)(2,1)} %fusion.3, bf16[3,512,512]{2,1,0:T(8,128)(2,1)} %convolution_convert_fusion), kind=kOutput, calls=%fused_computation.14 | convolution fusion | flops 1621622784 | bytes 6291456 | tf_op jit(solution)/shard_map/hmrk,hmkc->hmrc/dot_general | solution.py:15
  165.5 0.0 copy-start.6
  165.5 2.6 %copy.43 = bf16[1,3,512,512]{3,2,1,0:T(8,128)(2,1)} copy(bf16[1,3,512,512]{2,3,1,0:T(8,128)(2,1)} %subtract_convert_fusion) | data formatting | bytes 3145728
  168.2 0.0 all-gather.2.cloned.1.call-done
  168.2 0.0 copy-done.6
  168.2 2.7 %fusion.22 = f32[256,2,512]{0,2,1:T(8,128)} fusion(bf16[256,2,512]{0,2,1:T(8,128)(2,1)S(1)} %bitcast.141, bf16[2,3,512,512]{2,3,0,1:T(8,128)(2,1)} %all-gather.2.cloned.1.call-done), kind=kOutput, calls=%fused_computation.50 | convolution fusion | flops 268697600 | bytes 2621440 | tf_op jit(solution)/shard_map/thi,hij->thj/dot_general | solution.py:15
  170.8 2.7 %multiply_reduce_fusion = (f32[256,2]{0,1:T(2,128)S(1)}, f32[256,2,512]{0,2,1:T(8,128)S(1)}) fusion(bf16[256,2,512]{0,2,1:T(8,128)(2,1)S(1)} %bitcast.142, bf16[2,3,512,512]{2,3,0,1:T(8,128)(2,1)} %all-gather.2.cloned.1.call-done, f32[256,2,512]{0,2,1:T(8,128)} %fusion.22), kind=kOutput, calls=%fused_computation.71 | convolution fusion | flops 540016128 | bytes 4720640 | tf_op jit(solution)/shard_map/thj,hjc->thc/dot_general | solution.py:15
  173.6 0.4 multiply_convert_fusion.3
  173.9 1.0 copy.42
  (3 shorter events, 0.0 us)
Async XLA Ops:
  8.0 1.0 copy-start
  8.0 2.5 %copy-start.1 = (bf16[1,3,512,512]{3,2,1,0:T(8,128)(2,1)S(1)}, bf16[1,3,512,512]{3,2,1,0:T(8,128)(2,1)}, u32[]{:S(2)}) copy-start(bf16[1,3,512,512]{3,2,1,0:T(8,128)(2,1)} %param.11) | copy-start | bytes 4718596
  8.0 106.3 %all-reduce.2.cloned.1.call-start = ((), (), s32[]{:S(2)}) async-start(), calls=%async_computation.1 | async-start | bytes 3145728 | tf_op jit(solution)/shard_map/psum | solution.py:53
  10.5 1.0 copy-start.8
  10.5 1.0 copy-start.9
  15.5 152.6 %all-gather.2.cloned.1.call-start = ((), (), s32[]{:S(2)}) async-start(), calls=%async_computation | async-start | bytes 4718592 | tf_op jit(solution)/shard_map/all_gather | solution.py:66
  17.2 1.6 copy-start.4
  18.8 1.0 copy-start.5
  18.8 2.0 %copy-start.7 = (f32[1024]{0:T(1024)S(1)}, f32[1024]{0:T(1024)}, u32[]{:S(2)}) copy-start(f32[1024]{0:T(1024)} %param.13) | copy-start | bytes 12292
  114.3 2.0 %copy-start.3 = (bf16[1,3,512,512]{2,3,1,0:T(8,128)(2,1)S(1)}, bf16[1,3,512,512]{2,3,1,0:T(8,128)(2,1)}, u32[]{:S(2)}) copy-start(bf16[1,3,512,512]{2,3,1,0:T(8,128)(2,1)} %all-reduce.2.cloned.1.call-done) | copy-start | bytes 4718596
  124.6 4.2 %copy-start.10 = (bf16[1,3,512,512]{2,3,1,0:T(8,128)(2,1)S(1)}, bf16[1,3,512,512]{2,3,1,0:T(8,128)(2,1)}, u32[]{:S(2)}) copy-start(bf16[1,3,512,512]{2,3,1,0:T(8,128)(2,1)} %fusion.6) | copy-start | bytes 4718596
  134.6 4.2 %copy-start.11 = (bf16[1,3,512,512]{2,3,1,0:T(8,128)(2,1)S(1)}, bf16[1,3,512,512]{2,3,1,0:T(8,128)(2,1)}, u32[]{:S(2)}) copy-start(bf16[1,3,512,512]{2,3,1,0:T(8,128)(2,1)} %fusion.5) | copy-start | bytes 4718596
  144.5 4.2 %copy-start.12 = (bf16[1,3,512,512]{2,3,1,0:T(8,128)(2,1)S(1)}, bf16[1,3,512,512]{2,3,1,0:T(8,128)(2,1)}, u32[]{:S(2)}) copy-start(bf16[1,3,512,512]{2,3,1,0:T(8,128)(2,1)} %fusion.4) | copy-start | bytes 4718596
  154.5 4.4 %copy-start.2 = (bf16[1,3,512,512]{2,3,1,0:T(8,128)(2,1)S(1)}, bf16[1,3,512,512]{2,3,1,0:T(8,128)(2,1)}, u32[]{:S(2)}) copy-start(bf16[1,3,512,512]{2,3,1,0:T(8,128)(2,1)} %copy.15) | copy-start | bytes 4718596
  165.5 2.6 %copy-start.6 = (bf16[256,1024]{0,1:T(8,128)(2,1)S(1)}, bf16[256,1024]{0,1:T(8,128)(2,1)}, u32[]{:S(2)}) copy-start(bf16[256,1024]{0,1:T(8,128)(2,1)} %copy.71) | copy-start | bytes 1572868
Sparse Core Ops, SparseCore 0:
  15.6 98.6 all-reduce.1
Sparse Core Ops, SparseCore 1:
  17.6 47.5 all-gather.1
where the time goes:
time: 183 us; the launch traced here: 182 us
  waiting for transfers between devices  93.5 us (51%)
  matrix products  59 us (32%)
  between operations  15.6 us (9%)
  local copies, waits for them, and re-layouts  10.5 us (6%)
  other arithmetic  3.75 us (2%)
    psum x1, waiting for transfers between devices, local(): lax.psum(partial_value.astype(jnp.bfloat16), 'ctx').astype(jnp.float32)  93.5 us
    dot_general x18, matrix products, bmm(): return jnp.einsum(form, left, right, preferred_element_type=jnp.float32)  59 us
    unnamed x30, local copies, waits for them, and re-layouts  9.26 us
  transfers between devices with their start and end apart: 2, of which 1 were waited for; matrix products, arithmetic and copies ran while one was open for 32% of the time, Pallas kernels for 0%

commit v1 on v0

v1 whole, which is shorter than its diff:
```python
import functools
import math

import jax
import jax.numpy as jnp
from jax import lax
from jax.experimental import pallas as pl
from jax.experimental.pallas import tpu as pltpu
from jax.sharding import PartitionSpec as P

NS_STEPS = 5
coef_a = 3.4445
coef_b = -4.775
coef_c = 2.0315
BF = jnp.bfloat16
F32 = jnp.float32
MIB = 1 << 20
ANY = pl.BlockSpec(memory_space=pl.ANY)
VM = pl.BlockSpec(memory_space=pltpu.VMEM)


def dot(left, right):
    return jnp.dot(left, right, preferred_element_type=F32)


def dot_nt(left, right):
    return lax.dot_general(left, right, (((1,), (1,)), ((), ())), preferred_element_type=F32)


def dot_tn(left, right):
    return lax.dot_general(left, right, (((0,), (0,)), ((), ())), preferred_element_type=F32)


def copies(pairs, sems):
    made = [pltpu.make_async_copy(src, dst, sems.at[i]) for i, (src, dst) in enumerate(pairs)]
    for copy in made:
        copy.start()
    return made


def quarter_id():
    return lax.axis_index("ctx") & 3


def put_pieces(whole, pieces):
    rows = whole.shape[0] // 4
    own = quarter_id()
    for r, piece in enumerate(pieces):
        at = pl.multiple_of((own ^ r) * rows, rows)
        piece[...] = whole[pl.ds(at, rows), :]


def take_pieces(pieces, whole):
    rows = whole.shape[0] // 4
    own = quarter_id()
    for r, piece in enumerate(pieces):
        at = pl.multiple_of((own ^ r) * rows, rows)
        whole[pl.ds(at, rows), :] = piece[...]


def grad_two_kernel(k_hbm, v_hbm, r_ref, w_hbm, *refs):
    pieces, (g1_ref, g3_ref, go_ref), (k, v, w1, w3, whole, sems) = refs[:4], refs[4:7], refs[7:]
    ck, c1, c3, cv = copies(
        [(k_hbm, k), (w_hbm.at[0, 0], w1), (w_hbm.at[0, 1], w3), (v_hbm, v)], sems
    )
    scale = w1.shape[-1] ** (-0.5)
    ck.wait()
    c1.wait()
    g1 = dot(k[...], w1[...]) * scale
    g1_ref[...] = g1
    c3.wait()
    g3 = dot(k[...], w3[...]) * scale
    g3_ref[...] = g3
    cv.wait()
    rate = jnp.broadcast_to(r_ref[...], (128, r_ref.shape[1])).T[:, :1]
    go = (-(rate * v[...].astype(F32))).astype(BF)
    go_ref[...] = go
    hidden = (g1 * jax.nn.sigmoid(g1) * g3).astype(BF)
    whole[...] = (dot_tn(hidden, go) * scale).astype(BF)
    put_pieces(whole, pieces)


def grad_one_kernel(k_ref, w_hbm, g1_ref, g3_ref, go_ref, *refs):
    one, three, (w2, dg1, dg3, whole, sems) = refs[:4], refs[4:8], refs[8:]
    (c2,) = copies([(w_hbm.at[0, 2], w2)], sems)
    scale = w2.shape[-1] ** (-0.5)
    c2.wait()
    dh = dot_nt(go_ref[...], w2[...]) * scale
    g1 = g1_ref[...]
    sig = jax.nn.sigmoid(g1)
    dg1[...] = (dh * g3_ref[...] * sig * (1.0 + g1 * (1.0 - sig))).astype(BF)
    dg3[...] = (dh * (g1 * sig)).astype(BF)
    k = k_ref[...]
    whole[...] = (dot_tn(k, dg1[...]) * scale).astype(BF)
    put_pieces(whole, one)
    whole[...] = (dot_tn(k, dg3[...]) * scale).astype(BF)
    put_pieces(whole, three)


def orthogonalize(grad):
    grad = grad.astype(F32)
    total = jnp.sum(grad * grad)
    x = (grad / (jnp.sqrt(total) + 1e-07)).astype(BF)
    for _ in range(NS_STEPS):
        gram = dot_nt(x, x).astype(BF)
        square = dot(gram, gram)
        poly = (coef_b * gram.astype(F32) + coef_c * square).astype(BF)
        x = (coef_a * x.astype(F32) + dot(poly, x)).astype(BF)
    return x


def updated(weight, x):
    step_size = 0.4 * math.sqrt(x.shape[-1])
    return (weight.astype(F32) - step_size * x.astype(F32)).astype(BF)


def first_update_kernel(p0, p2, p1, p3, w_hbm, o_ref, w, whole, sems):
    index = 2 * (1 - (lax.axis_index("ctx") & 1))
    (cw,) = copies([(w_hbm.at[0, index], w)], sems)
    take_pieces((p0, p1, p2, p3), whole)
    x = orthogonalize(whole[...])
    cw.wait()
    o_ref[...] = updated(w[...], x)


def last_update_kernel(p0, p1, p2, p3, w_hbm, mine, theirs, o_hbm, w, new, whole, sems):
    index = 2 * (1 - (lax.axis_index("ctx") & 1))
    cw, cm, ct = copies(
        [(w_hbm.at[0, 1], w), (mine, o_hbm.at[0, index]), (theirs, o_hbm.at[0, 2 - index])], sems
    )
    take_pieces((p0, p1, p2, p3), whole)
    x = orthogonalize(whole[...])
    cw.wait()
    new[...] = updated(w[...], x)
    cn = pltpu.make_async_copy(new, o_hbm.at[0, 1], sems.at[3])
    cn.start()
    cm.wait()
    ct.wait()
    cn.wait()


def read_kernel(w_hbm, *refs):
    count = (len(refs) - 4) // 2
    queries, reads, (w1, w3, w2, sems) = refs[:count], refs[count : 2 * count], refs[2 * count :]
    made = copies([(w_hbm.at[0, 0], w1), (w_hbm.at[0, 1], w3), (w_hbm.at[0, 2], w2)], sems)
    scale = w1.shape[-1] ** (-0.5)
    for copy in made:
        copy.wait()
    for q, out in zip(queries, reads):
        rows = q[...]
        r1 = dot(rows, w1[...]) * scale
        r3 = dot(rows, w3[...]) * scale
        hq = (r1 * jax.nn.sigmoid(r1) * r3).astype(BF)
        out[...] = (dot(hq, w2[...]) * scale).astype(BF)


def norm_kernel(heads, gate, gain, *refs):
    reads, out = refs[:heads], refs[heads]
    width = reads[0].shape[-1]
    me = lax.axis_index("head")
    for r, read in enumerate(reads):
        at = pl.multiple_of(lax.rem(me + r, heads) * width, width)
        x = read[...].astype(F32)
        mean = jnp.mean(x * x, axis=-1, keepdims=True)
        g = gate[:, pl.ds(at, width)].astype(F32)
        out[:, pl.ds(at, width)] = (
            x * lax.rsqrt(mean + 1e-06) * gain[:, pl.ds(at, width)] * (g * jax.nn.sigmoid(g))
        ).astype(BF)


def params(mib):
    return pltpu.CompilerParams(vmem_limit_bytes=mib * MIB)


def local(ctx, heads, keys, values, rates, queries, fast_weights, gate, gain):
    tok, width = keys.shape
    rows = width // 4
    piece = jax.ShapeDtypeStruct((rows, width), BF)
    bits = [1 << b for b in range(ctx.bit_length() - 1)]

    def swap(x, bit):
        return lax.ppermute(x, "ctx", [(i, i ^ bit) for i in range(ctx)])

    def turn(x, r):
        return lax.ppermute(x, "head", [(i, (i + r) % heads) for i in range(heads)])

    me = lax.axis_index("head")
    core = lax.axis_index("ctx") & 1

    def columns(r):
        return lax.dynamic_slice_in_dim(queries, lax.rem(me + r, heads) * width, width, 1)

    asked = [columns(0)] + [turn(columns(r), r) for r in range(1, heads)]

    mat = lambda dtype: pltpu.VMEM((width, width), dtype)
    tokens = lambda dtype: pltpu.VMEM((tok, width), dtype)
    outs = pl.pallas_call(
        grad_two_kernel,
        out_shape=[piece] * 4
        + [jax.ShapeDtypeStruct((tok, width), d) for d in (F32, F32, BF)],
        in_specs=[ANY, ANY, VM, ANY],
        out_specs=[VM] * 7,
        scratch_shapes=[tokens(BF), tokens(BF), mat(BF), mat(BF), mat(BF), pltpu.SemaphoreType.DMA((4,))],
        compiler_params=params(24),
    )(keys, values, rates, fast_weights)
    two, (g1, g3, go) = outs[:4], outs[4:]
    outs = pl.pallas_call(
        grad_one_kernel,
        out_shape=[piece] * 8,
        in_specs=[VM, ANY, VM, VM, VM],
        out_specs=[VM] * 8,
        scratch_shapes=[mat(BF), tokens(BF), tokens(BF), mat(BF), pltpu.SemaphoreType.DMA((1,))],
        compiler_params=params(24),
    )(keys, fast_weights, g1, g3, go)
    one, three = outs[:4], outs[4:]

    def add(x, y):
        return (x.astype(F32) + y.astype(F32)).astype(BF)

    def summed(p):
        far = swap(p[3], 1)
        near = swap(p[1], 1)
        give = add(p[2], far)
        keep = add(p[0], near)
        total = add(keep, swap(give, 2))
        for bit in bits[2:]:
            total = add(total, swap(total, bit))
        return total, swap(total, 2)

    two, one, three = summed(two), summed(one), summed(three)

    give = [jnp.where(core == 0, o, t) for o, t in zip(one, two)]
    keep = [jnp.where(core == 0, t, o) for o, t in zip(one, two)]
    got = [swap(x, 1) for x in give]
    matrix = jax.ShapeDtypeStruct((width, width), BF)
    mine = pl.pallas_call(
        first_update_kernel,
        out_shape=matrix,
        in_specs=[VM] * 4 + [ANY],
        out_specs=VM,
        scratch_shapes=[mat(BF), mat(BF), pltpu.SemaphoreType.DMA((1,))],
        compiler_params=params(16),
    )(*keep, *got, fast_weights)
    theirs = swap(mine, 1)
    others = [swap(x, 1) for x in three]
    new_weights = pl.pallas_call(
        last_update_kernel,
        out_shape=jax.ShapeDtypeStruct(fast_weights.shape, BF),
        in_specs=[VM] * 4 + [ANY] * 3,
        out_specs=ANY,
        scratch_shapes=[mat(BF), mat(BF), mat(BF), pltpu.SemaphoreType.DMA((4,))],
        compiler_params=params(16),
    )(three[0], others[0], three[1], others[1], fast_weights, mine, theirs)

    reads = pl.pallas_call(
        read_kernel,
        out_shape=[jax.ShapeDtypeStruct(x.shape, BF) for x in asked],
        in_specs=[ANY] + [VM] * heads,
        out_specs=[VM] * heads,
        scratch_shapes=[mat(BF)] * 3 + [pltpu.SemaphoreType.DMA((3,))],
        compiler_params=params(24),
    )(fast_weights, *asked)
    back = [reads[0]] + [turn(reads[r], heads - r) for r in range(1, heads)]
    layer_out = pl.pallas_call(
        functools.partial(norm_kernel, heads),
        out_shape=jax.ShapeDtypeStruct(queries.shape, BF),
        in_specs=[VM] * (2 + heads),
        out_specs=VM,
        compiler_params=params(16),
    )(gate, gain.reshape(1, -1), *back)
    return layer_out, new_weights


def solution(mesh):
    in_specs = (
        P("ctx", "head"),
        P("ctx", "head"),
        P("head", "ctx"),
        P(("ctx", "head"), None),
        P("head", None, None, None),
        P(("ctx", "head"), None),
        P(),
    )
    out_specs = (P(("ctx", "head"), None), P("head", None, None, None))
    body = functools.partial(local, mesh.shape["ctx"], mesh.shape["head"])
    return jax.shard_map(body, mesh=mesh, in_specs=in_specs, out_specs=out_specs, check_vma=False)
```

time: 183 us -> 70.1 us (0.38)
  waiting for transfers between devices: 93.5 us -> 22 us
  matrix products: 59 us -> 0 us
  starting transfers between devices: 0.08 us -> 24.1 us
  Pallas kernels: 0 us -> 18 us
  between operations: 15.6 us -> 1 us
  local copies, waits for them, and re-layouts: 10.5 us -> 4.23 us
  other arithmetic: 3.75 us -> 0.51 us
    psum x1 -> x0, waiting for transfers between devices: 93.5 us -> none  [local(): lax.psum(partial_value.astype(jnp.bfloat16), 'ctx').astype(jnp.float32)]
    dot_general x18 -> x0, matrix products: 59 us -> none  [bmm(): return jnp.einsum(form, left, right, preferred_element_type=jnp.float32)]
    ppermute x0 -> x25, starting transfers between devices: none -> 24.1 us  [the longest x23 19.9 us: swap(): return lax.ppermute(x, 'ctx', [(i, i ^ bit) for i in range(ctx)])]
    ppermute x0 -> x25, waiting for transfers between devices: none -> 22 us  [the longest x23 20.2 us: swap(): return lax.ppermute(x, 'ctx', [(i, i ^ bit) for i in range(ctx)])]
    pallas_call x0 -> x6, Pallas kernels: none -> 18 us  [the longest x1 6.55 us: local(): pl.pallas_call(last_update_kernel, out_shape=jax.ShapeDtypeStruct(fast_we...]
    unnamed x30 -> x16, local copies, waits for them, and re-layouts: 9.26 us -> 4.19 us
    reduce_sum x1 -> x0, other arithmetic: 2.02 us -> none  [local(): total = jnp.sum(grads * grads, axis=(2, 3), keepdims=True)]
  transfers between devices with their start and end apart: 2 -> 25, of which waited for: 1 -> 11; matrix products, arithmetic and copies ran while one was open for 32% -> 1% of each run, Pallas kernels for 0% -> 12%
where the time goes in v1:
time: 70.1 us; the launch traced here: 69.8 us
  starting transfers between devices  24.1 us (34%)
  waiting for transfers between devices  22 us (31%)
  Pallas kernels  18 us (26%)
  local copies, waits for them, and re-layouts  4.23 us (6%)
  between operations  1 us (1%)
    ppermute x23, waiting for transfers between devices, swap(): return lax.ppermute(x, 'ctx', [(i, i ^ bit) for i in range(ctx)])  20.2 us
    ppermute x23, starting transfers between devices, swap(): return lax.ppermute(x, 'ctx', [(i, i ^ bit) for i in range(ctx)])  19.9 us
    pallas_call x1, Pallas kernels, local(): pl.pallas_call(last_update_kernel, out_shape=jax.ShapeDtypeStruct(fast_we...  6.55 us
    pallas_call x1, Pallas kernels, local(): pl.pallas_call(first_update_kernel, out_shape=matrix, in_specs=[VM] * 4 +...  5.53 us
    unnamed x16, local copies, waits for them, and re-layouts  4.19 us
    ppermute x2, starting transfers between devices, turn(): return lax.ppermute(x, 'head', [(i, (i + r) % heads) for i in range(heads)])  4.16 us
    pallas_call x1, Pallas kernels, local(): pl.pallas_call(grad_two_kernel, out_shape=[piece] * 4 + [jax.ShapeDtypeSt...  1.85 us
    ppermute x2, waiting for transfers between devices, turn(): return lax.ppermute(x, 'head', [(i, (i + r) % heads) for i in range(heads)])  1.73 us
  transfers between devices with their start and end apart: 25, of which 11 were waited for; matrix products, arithmetic and copies ran while one was open for 1% of the time, Pallas kernels for 12%

profile of v1, /device:TPU:0, one launch (start us, length us, event | category | flops | bytes accessed | tf_op | source)
XLA Modules:
  0.0 69.8 jit_solution(9853342123486659368)
XLA Ops:
  0.6 0.0 copy-start
  0.6 1.4 %copy-done = bf16[1,3,512,512]{3,2,1,0:T(8,128)(2,1)S(1)} copy-done((bf16[1,3,512,512]{3,2,1,0:T(8,128)(2,1)S(1)}, bf16[1,3,512,512]{3,2,1,0:T(8,128)(2,1)}, u32[]{:S(2)}) %copy-start) | copy-done | bytes 1572888
  2.0 1.0 %copy-done.2 = bf16[512,512]{1,0:T(8,128)(2,1)S(1)} copy-done((bf16[512,512]{1,0:T(8,128)(2,1)S(1)}, bf16[512,512]{1,0:T(8,128)(2,1)}, u32[]{:S(2)}) %copy-start.2) | copy-done | bytes 524312
  3.1 1.0 %copy-done.4 = bf16[512,512]{1,0:T(8,128)(2,1)S(1)} copy-done((bf16[512,512]{1,0:T(8,128)(2,1)S(1)}, bf16[512,512]{1,0:T(8,128)(2,1)}, u32[]{:S(2)}) %copy-start.4) | copy-done | bytes 524312
  4.1 0.7 copy-done.6
  4.8 1.9 %shard_map.88 = (bf16[128,512]{1,0:T(8,128)(2,1)S(1)}, bf16[128,512]{1,0:T(8,128)(2,1)S(1)}, bf16[128,512]{1,0:T(8,128)(2,1)S(1)}, bf16[128,512]{1,0:T(8,128)(2,...) custom-call(bf16[512,512]{1,0:T(8,128)(2,1)S(1)} %copy-done.2, ...), custom_call_target="tpu_custom_call" | custom-call | tf_op jit(solution)/shard_map/pallas_call | solution.py:197
  6.7 0.0 copy-start.7
  6.7 1.5 %shard_map.89 = (bf16[128,512]{1,0:T(8,128)(2,1)S(1)}, bf16[128,512]{1,0:T(8,128)(2,1)S(1)}, bf16[128,512]{1,0:T(8,128)(2,1)S(1)}, bf16[128,512]{1,0:T(8,128)(2,...) custom-call(bf16[512,512]{1,0:T(8,128)(2,1)S(1)} %copy-done.2, ...), custom_call_target="tpu_custom_call" | custom-call | tf_op jit(solution)/shard_map/pallas_call | solution.py:207
  8.2 0.6 collective-permute-start.16
  8.8 0.1 collective-permute-start.15
  8.8 0.4 collective-permute-start.11
  9.3 0.1 collective-permute-start.10
  9.4 0.4 collective-permute-start.3
  9.8 0.0 collective-permute-done.16
  9.8 0.3 collective-permute-start.2
  10.2 0.2 collective-permute-done.11
  10.3 2.8 %collective-permute-start = (bf16[256,512]{1,0:T(8,128)(2,1)S(1)}, bf16[256,512]{1,0:T(8,128)(2,1)S(1)}, u32[]{:S(2)}, u32[]{:S(2)}) collective-permute-start(bf16[256,512]{1,0:T(8,128)(2,1)S(1)} %get-tuple-element.39), channel_id=1, source_target_pairs={{0,1},{1,0},{2,3},{3,2},{4,5},{5,4},{6,7},{7,6},{8,9},{9,8},{10,11... | collective-permute-start | bytes 786440 | tf_op jit(solution)/shard_map/ppermute | solution.py:185
  13.2 0.0 collective-permute-done.3
  13.2 1.6 %collective-permute-start.17 = (bf16[128,512]{1,0:T(8,128)(2,1)S(1)}, bf16[128,512]{1,0:T(8,128)(2,1)S(1)}, u32[]{:S(2)}, u32[]{:S(2)}) collective-permute-start(bf16[128,512]{1,0:T(8,128)(2,1)S(1)} %add_convert_fusion.3), channel_id=1, source_target_pairs={{0,4},{2,6},{4,0},{6,2},{8,12},{10,14},{12,8},{14,10},{16,20},{18,... | collective-permute-start | bytes 393224 | tf_op jit(solution)/shard_map/ppermute | solution.py:182
  14.8 0.0 collective-permute-done.15
  14.8 0.6 collective-permute-start.12
  15.4 4.2 %collective-permute-done.17 = bf16[128,512]{1,0:T(8,128)(2,1)S(1)} collective-permute-done((bf16[128,512]{1,0:T(8,128)(2,1)S(1)}, bf16[128,512]{1,0:T(8,128)(2,1)S(1)}, u32[]{:S(2)}, u32[]{:S(2)}) %collective-permute-start.17) | collective-permute-done | bytes 131104 | tf_op jit(solution)/shard_map/ppermute | solution.py:182
  19.6 1.5 %collective-permute-start.4 = (bf16[128,512]{1,0:T(8,128)(2,1)S(1)}, bf16[128,512]{1,0:T(8,128)(2,1)S(1)}, u32[]{:S(2)}, u32[]{:S(2)}) collective-permute-start(bf16[128,512]{1,0:T(8,128)(2,1)S(1)} %add_convert_fusion.13), channel_id=1, source_target_pairs={{0,4},{2,6},{4,0},{6,2},{8,12},{10,14},{12,8},{14,10},{16,20},{18,... | collective-permute-start | bytes 393224 | tf_op jit(solution)/shard_map/ppermute | solution.py:182
  21.1 0.1 add_convert_fusion.2
  21.2 0.0 collective-permute-done.10
  21.2 1.6 %collective-permute-start.18 = (bf16[128,512]{1,0:T(8,128)(2,1)S(1)}, bf16[128,512]{1,0:T(8,128)(2,1)S(1)}, u32[]{:S(2)}, u32[]{:S(2)}) collective-permute-start(bf16[128,512]{1,0:T(8,128)(2,1)S(1)} %add_convert_fusion.2), channel_id=1, source_target_pairs={{0,8},{2,10},{4,12},{6,14},{8,0},{10,2},{12,4},{14,6},{16,24},{18,... | collective-permute-start | bytes 393224 | tf_op jit(solution)/shard_map/ppermute | solution.py:182
  22.8 0.0 collective-permute-done.12
  22.8 0.1 add_convert_fusion.7
  22.9 1.2 %collective-permute-start.13 = (bf16[128,512]{1,0:T(8,128)(2,1)S(1)}, bf16[128,512]{1,0:T(8,128)(2,1)S(1)}, u32[]{:S(2)}, u32[]{:S(2)}) collective-permute-start(bf16[128,512]{1,0:T(8,128)(2,1)S(1)} %add_convert_fusion.7), channel_id=1, source_target_pairs={{0,8},{2,10},{4,12},{6,14},{8,0},{10,2},{12,4},{14,6},{16,24},{18,... | collective-permute-start | bytes 393224 | tf_op jit(solution)/shard_map/ppermute | solution.py:182
  24.1 2.1 %collective-permute-done.18 = bf16[128,512]{1,0:T(8,128)(2,1)S(1)} collective-permute-done((bf16[128,512]{1,0:T(8,128)(2,1)S(1)}, bf16[128,512]{1,0:T(8,128)(2,1)S(1)}, u32[]{:S(2)}, u32[]{:S(2)}) %collective-permute-start.18) | collective-permute-done | bytes 131104 | tf_op jit(solution)/shard_map/ppermute | solution.py:182
  26.3 0.0 copy-start.1
  26.3 3.5 %collective-permute-start.19 = (bf16[128,512]{1,0:T(8,128)(2,1)S(1)}, bf16[128,512]{1,0:T(8,128)(2,1)S(1)}, u32[]{:S(2)}, u32[]{:S(2)}) collective-permute-start(bf16[128,512]{1,0:T(8,128)(2,1)S(1)} %add_convert_fusion.1), channel_id=1, source_target_pairs={{0,16},{2,18},{4,20},{6,22},{8,24},{10,26},{12,28},{14,30},{16,0},... | collective-permute-start | bytes 393224 | tf_op jit(solution)/shard_map/ppermute | solution.py:182
  29.8 0.0 collective-permute-done.13
  29.8 2.8 %collective-permute-start.14 = (bf16[128,512]{1,0:T(8,128)(2,1)S(1)}, bf16[128,512]{1,0:T(8,128)(2,1)S(1)}, u32[]{:S(2)}, u32[]{:S(2)}) collective-permute-start(bf16[128,512]{1,0:T(8,128)(2,1)S(1)} %add_convert_fusion.6), channel_id=1, source_target_pairs={{0,16},{2,18},{4,20},{6,22},{8,24},{10,26},{12,28},{14,30},{16,0},... | collective-permute-start | bytes 393224 | tf_op jit(solution)/shard_map/ppermute | solution.py:182
  32.6 0.0 collective-permute-done.2
  32.6 0.0 collective-permute-done.4
  32.6 0.1 add_convert_fusion.12
  32.6 0.9 %collective-permute-start.5 = (bf16[128,512]{1,0:T(8,128)(2,1)S(1)}, bf16[128,512]{1,0:T(8,128)(2,1)S(1)}, u32[]{:S(2)}, u32[]{:S(2)}) collective-permute-start(bf16[128,512]{1,0:T(8,128)(2,1)S(1)} %add_convert_fusion.12), channel_id=1, source_target_pairs={{0,8},{2,10},{4,12},{6,14},{8,0},{10,2},{12,4},{14,6},{16,24},{18,... | collective-permute-start | bytes 393224 | tf_op jit(solution)/shard_map/ppermute | solution.py:182
  33.6 1.9 %collective-permute-done.19 = bf16[128,512]{1,0:T(8,128)(2,1)S(1)} collective-permute-done((bf16[128,512]{1,0:T(8,128)(2,1)S(1)}, bf16[128,512]{1,0:T(8,128)(2,1)S(1)}, u32[]{:S(2)}, u32[]{:S(2)}) %collective-permute-start.19) | collective-permute-done | bytes 131104 | tf_op jit(solution)/shard_map/ppermute | solution.py:182
  35.5 2.5 %collective-permute-done.14 = bf16[128,512]{1,0:T(8,128)(2,1)S(1)} collective-permute-done((bf16[128,512]{1,0:T(8,128)(2,1)S(1)}, bf16[128,512]{1,0:T(8,128)(2,1)S(1)}, u32[]{:S(2)}, u32[]{:S(2)}) %collective-permute-start.14) | collective-permute-done | bytes 131104 | tf_op jit(solution)/shard_map/ppermute | solution.py:182
  38.0 0.1 broadcast_select_fusion.1
  38.1 1.6 %collective-permute-start.20 = (bf16[128,512]{1,0:T(8,128)(2,1)S(1)}, bf16[128,512]{1,0:T(8,128)(2,1)S(1)}, u32[]{:S(2)}, u32[]{:S(2)}) collective-permute-start(bf16[128,512]{1,0:T(8,128)(2,1)S(1)} %get-tuple-element.38), channel_id=1, source_target_pairs={{0,4},{2,6},{4,0},{6,2},{8,12},{10,14},{12,8},{14,10},{16,20},{18,... | collective-permute-start | bytes 393224 | tf_op jit(solution)/shard_map/ppermute | solution.py:182
  39.7 0.5 collective-permute-start.21
  40.2 0.1 collective-permute-done.5
  40.3 0.5 collective-permute-start.6
  40.8 0.0 collective-permute-start.22
  40.8 2.3 %collective-permute-done.20 = bf16[128,512]{1,0:T(8,128)(2,1)S(1)} collective-permute-done((bf16[128,512]{1,0:T(8,128)(2,1)S(1)}, bf16[128,512]{1,0:T(8,128)(2,1)S(1)}, u32[]{:S(2)}, u32[]{:S(2)}) %collective-permute-start.20) | collective-permute-done | bytes 131104 | tf_op jit(solution)/shard_map/ppermute | solution.py:182
  43.1 1.5 %collective-permute-done.21 = bf16[128,512]{1,0:T(8,128)(2,1)S(1)} collective-permute-done((bf16[128,512]{1,0:T(8,128)(2,1)S(1)}, bf16[128,512]{1,0:T(8,128)(2,1)S(1)}, u32[]{:S(2)}, u32[]{:S(2)}) %collective-permute-start.21) | collective-permute-done | bytes 131104 | tf_op jit(solution)/shard_map/ppermute | solution.py:182
  44.7 0.1 collective-permute-start.23
  44.8 0.0 collective-permute-done.22.p1
  44.8 1.3 %collective-permute-done.23.p3 = bf16[128,512]{1,0:T(8,128)(2,1)S(1)} collective-permute-done((bf16[128,512]{1,0:T(8,128)(2,1)S(1)}, bf16[128,512]{1,0:T(8,128)(2,1)S(1)}, u32[]{:S(2)}, u32[]{:S(2)}) %collective-permute-start.23) | collective-permute-done | bytes 131104 | tf_op jit(solution)/shard_map/ppermute | solution.py:182
  46.1 5.5 %shard_map.90.mine = bf16[512,512]{1,0:T(8,128)(2,1)S(1)} custom-call(bf16[128,512]{1,0:T(8,128)(2,1)S(1)} %broadcast_select_fusion.3.p0, bf16[128,512]{1,0:T(8,128)(2,1)S(1)} %get-tuple-element.42.p2, bf16[128,512]{1,0:T(8,128)(2,1)S(1)} %collective-permute-done.22.p1, bf16[128,512]{1,0:T(8,128)(2,1)S(1)} %collective-permute-done.23.p3, ...), custom_call_target="tpu_custom_call" | custom-call | tf_op jit(solution)/shard_map/pallas_call | solution.py:236
  51.6 0.0 copy-start.3
  51.6 0.0 copy-start.5
  51.7 0.2 collective-permute-start.24
  51.9 0.0 collective-permute-done.refs_1_
  51.9 1.3 %shard_map.86 = (bf16[256,512]{1,0:T(8,128)(2,1)S(1)}, bf16[256,512]{1,0:T(8,128)(2,1)S(1)}) custom-call(bf16[1,3,512,512]{3,2,1,0:T(8,128)(2,1)S(1)} %copy-done.1, bf16[256,512]{1,0:T(8,128)(2,1)S(1)} %get-tuple-element.40.refs_0_, bf16[256,512]{1,0:T(8,128)(2,1)S(1)} %collective-permute-done.refs_1_), custom_call_target="tpu_custom_call" | custom-call | tf_op jit(solution)/shard_map/pallas_call | solution.py:255
  53.2 1.3 %collective-permute-start.1 = (bf16[256,512]{1,0:T(8,128)(2,1)S(1)}, bf16[256,512]{1,0:T(8,128)(2,1)S(1)}, u32[]{:S(2)}, u32[]{:S(2)}) collective-permute-start(bf16[256,512]{1,0:T(8,128)(2,1)S(1)} %get-tuple-element.20), channel_id=1, source_target_pairs={{0,1},{1,0},{2,3},{3,2},{4,5},{5,4},{6,7},{7,6},{8,9},{9,8},{10,11... | collective-permute-start | bytes 786440 | tf_op jit(solution)/shard_map/ppermute | solution.py:185
  54.5 0.0 collective-permute-done.6
  54.6 1.5 %collective-permute-start.8 = (bf16[128,512]{1,0:T(8,128)(2,1)S(1)}, bf16[128,512]{1,0:T(8,128)(2,1)S(1)}, u32[]{:S(2)}, u32[]{:S(2)}) collective-permute-start(bf16[128,512]{1,0:T(8,128)(2,1)S(1)} %add_convert_fusion.10.p0), channel_id=1, source_target_pairs={{0,4},{2,6},{4,0},{6,2},{8,12},{10,14},{12,8},{14,10},{16,20},{18,... | collective-permute-start | bytes 393224 | tf_op jit(solution)/shard_map/ppermute | solution.py:182
  56.0 4.1 %collective-permute-done.8.p2 = bf16[128,512]{1,0:T(8,128)(2,1)S(1)} collective-permute-done((bf16[128,512]{1,0:T(8,128)(2,1)S(1)}, bf16[128,512]{1,0:T(8,128)(2,1)S(1)}, u32[]{:S(2)}, u32[]{:S(2)}) %collective-permute-start.8) | collective-permute-done | bytes 131104 | tf_op jit(solution)/shard_map/ppermute | solution.py:182
  60.1 1.7 %collective-permute-done.1.refs_1_ = bf16[256,512]{1,0:T(8,128)(2,1)S(1)} collective-permute-done((bf16[256,512]{1,0:T(8,128)(2,1)S(1)}, bf16[256,512]{1,0:T(8,128)(2,1)S(1)}, u32[]{:S(2)}, u32[]{:S(2)}) %collective-permute-start.1) | collective-permute-done | bytes 262176 | tf_op jit(solution)/shard_map/ppermute | solution.py:185
  61.9 1.2 %shard_map.87 = bf16[256,1024]{1,0:T(8,128)(2,1)} custom-call(bf16[256,1024]{1,0:T(8,128)(2,1)S(1)} %copy-done.3, f32[1,1024]{1,0:T(1,128)S(1)} %bitcast.1, bf16[256,512]{1,0:T(8,128)(2,1)S(1)} %get-tuple-element.19.refs_0_, bf16[256,512]{1,0:T(8,128)(2,1)S(1)} %collective-permute-done.1.refs_1_), custom_call_target="tpu_custom_call" | custom-call | tf_op jit(solution)/shard_map/pallas_call | solution.py:264
  63.1 6.5 %shard_map.91 = bf16[1,3,512,512]{3,2,1,0:T(8,128)(2,1)} custom-call(bf16[128,512]{1,0:T(8,128)(2,1)S(1)} %add_convert_fusion.10.p0, bf16[128,512]{1,0:T(8,128)(2,1)S(1)} %collective-permute-done.7.p1, bf16[128,512]{1,0:T(8,128)(2,1)S(1)} %collective-permute-done.8.p2, bf16[128,512]{1,0:T(8,128)(2,1)S(1)} %collective-permute-done.9.p3, ...), custom_call_target="tpu_custom_call" | custom-call | tf_op jit(solution)/shard_map/pallas_call | solution.py:246
  (22 shorter events, 0.3 us)
Async XLA Ops:
  0.6 1.4 %copy-start = (bf16[1,3,512,512]{3,2,1,0:T(8,128)(2,1)S(1)}, bf16[1,3,512,512]{3,2,1,0:T(8,128)(2,1)}, u32[]{:S(2)}) copy-start(bf16[1,3,512,512]{3,2,1,0:T(8,128)(2,1)} %w_hbm.9) | copy-start | bytes 4718596
  2.0 1.0 %copy-start.2 = (bf16[512,512]{1,0:T(8,128)(2,1)S(1)}, bf16[512,512]{1,0:T(8,128)(2,1)}, u32[]{:S(2)}) copy-start(bf16[512,512]{1,0:T(8,128)(2,1)} %k_ref.1) | copy-start | bytes 1572868
  3.1 1.0 %copy-start.4 = (bf16[512,512]{1,0:T(8,128)(2,1)S(1)}, bf16[512,512]{1,0:T(8,128)(2,1)}, u32[]{:S(2)}) copy-start(bf16[512,512]{1,0:T(8,128)(2,1)} %v_hbm.1) | copy-start | bytes 1572868
  4.1 0.7 copy-start.6
  6.7 3.1 %copy-start.7 = (bf16[256,1024]{1,0:T(8,128)(2,1)S(1)}, bf16[256,1024]{1,0:T(8,128)(2,1)}, u32[]{:S(2)}) copy-start(bf16[256,1024]{1,0:T(8,128)(2,1)} %param.10) | copy-start | bytes 1572868
  8.2 1.6 %collective-permute-start.16 = (bf16[128,512]{1,0:T(8,128)(2,1)S(1)}, bf16[128,512]{1,0:T(8,128)(2,1)S(1)}, u32[]{:S(2)}, u32[]{:S(2)}) collective-permute-start(bf16[128,512]{1,0:T(8,128)(2,1)S(1)} %get-tuple-element.35), channel_id=1, source_target_pairs={{0,2},{2,0},{4,6},{6,4},{8,10},{10,8},{12,14},{14,12},{16,18},{18,... | collective-permute-start | bytes 393224 | tf_op jit(solution)/shard_map/ppermute | solution.py:182
  8.8 6.0 %collective-permute-start.15 = (bf16[128,512]{1,0:T(8,128)(2,1)S(1)}, bf16[128,512]{1,0:T(8,128)(2,1)S(1)}, u32[]{:S(2)}, u32[]{:S(2)}) collective-permute-start(bf16[128,512]{1,0:T(8,128)(2,1)S(1)} %get-tuple-element.33), channel_id=1, source_target_pairs={{0,2},{2,0},{4,6},{6,4},{8,10},{10,8},{12,14},{14,12},{16,18},{18,... | collective-permute-start | bytes 393224 | tf_op jit(solution)/shard_map/ppermute | solution.py:182
  8.8 1.5 %collective-permute-start.11 = (bf16[128,512]{1,0:T(8,128)(2,1)S(1)}, bf16[128,512]{1,0:T(8,128)(2,1)S(1)}, u32[]{:S(2)}, u32[]{:S(2)}) collective-permute-start(bf16[128,512]{1,0:T(8,128)(2,1)S(1)} %get-tuple-element.31), channel_id=1, source_target_pairs={{0,2},{2,0},{4,6},{6,4},{8,10},{10,8},{12,14},{14,12},{16,18},{18,... | collective-permute-start | bytes 393224 | tf_op jit(solution)/shard_map/ppermute | solution.py:182
  9.3 11.9 %collective-permute-start.10 = (bf16[128,512]{1,0:T(8,128)(2,1)S(1)}, bf16[128,512]{1,0:T(8,128)(2,1)S(1)}, u32[]{:S(2)}, u32[]{:S(2)}) collective-permute-start(bf16[128,512]{1,0:T(8,128)(2,1)S(1)} %get-tuple-element.29), channel_id=1, source_target_pairs={{0,2},{2,0},{4,6},{6,4},{8,10},{10,8},{12,14},{14,12},{16,18},{18,... | collective-permute-start | bytes 393224 | tf_op jit(solution)/shard_map/ppermute | solution.py:182
  9.4 3.8 %collective-permute-start.3 = (bf16[128,512]{1,0:T(8,128)(2,1)S(1)}, bf16[128,512]{1,0:T(8,128)(2,1)S(1)}, u32[]{:S(2)}, u32[]{:S(2)}) collective-permute-start(bf16[128,512]{1,0:T(8,128)(2,1)S(1)} %get-tuple-element.27), channel_id=1, source_target_pairs={{0,2},{2,0},{4,6},{6,4},{8,10},{10,8},{12,14},{14,12},{16,18},{18,... | collective-permute-start | bytes 393224 | tf_op jit(solution)/shard_map/ppermute | solution.py:182
  9.8 22.7 %collective-permute-start.2 = (bf16[128,512]{1,0:T(8,128)(2,1)S(1)}, bf16[128,512]{1,0:T(8,128)(2,1)S(1)}, u32[]{:S(2)}, u32[]{:S(2)}) collective-permute-start(bf16[128,512]{1,0:T(8,128)(2,1)S(1)} %get-tuple-element.25), channel_id=1, source_target_pairs={{0,2},{2,0},{4,6},{6,4},{8,10},{10,8},{12,14},{14,12},{16,18},{18,... | collective-permute-start | bytes 393224 | tf_op jit(solution)/shard_map/ppermute | solution.py:182
  10.3 41.6 %collective-permute-start = (bf16[256,512]{1,0:T(8,128)(2,1)S(1)}, bf16[256,512]{1,0:T(8,128)(2,1)S(1)}, u32[]{:S(2)}, u32[]{:S(2)}) collective-permute-start(bf16[256,512]{1,0:T(8,128)(2,1)S(1)} %get-tuple-element.39), channel_id=1, source_target_pairs={{0,1},{1,0},{2,3},{3,2},{4,5},{5,4},{6,7},{7,6},{8,9},{9,8},{10,11... | collective-permute-start | bytes 786440 | tf_op jit(solution)/shard_map/ppermute | solution.py:185
  13.2 6.4 %collective-permute-start.17 = (bf16[128,512]{1,0:T(8,128)(2,1)S(1)}, bf16[128,512]{1,0:T(8,128)(2,1)S(1)}, u32[]{:S(2)}, u32[]{:S(2)}) collective-permute-start(bf16[128,512]{1,0:T(8,128)(2,1)S(1)} %add_convert_fusion.3), channel_id=1, source_target_pairs={{0,4},{2,6},{4,0},{6,2},{8,12},{10,14},{12,8},{14,10},{16,20},{18,... | collective-permute-start | bytes 393224 | tf_op jit(solution)/shard_map/ppermute | solution.py:182
  14.8 8.0 %collective-permute-start.12 = (bf16[128,512]{1,0:T(8,128)(2,1)S(1)}, bf16[128,512]{1,0:T(8,128)(2,1)S(1)}, u32[]{:S(2)}, u32[]{:S(2)}) collective-permute-start(bf16[128,512]{1,0:T(8,128)(2,1)S(1)} %add_convert_fusion.8), channel_id=1, source_target_pairs={{0,4},{2,6},{4,0},{6,2},{8,12},{10,14},{12,8},{14,10},{16,20},{18,... | collective-permute-start | bytes 393224 | tf_op jit(solution)/shard_map/ppermute | solution.py:182
  19.6 12.9 %collective-permute-start.4 = (bf16[128,512]{1,0:T(8,128)(2,1)S(1)}, bf16[128,512]{1,0:T(8,128)(2,1)S(1)}, u32[]{:S(2)}, u32[]{:S(2)}) collective-permute-start(bf16[128,512]{1,0:T(8,128)(2,1)S(1)} %add_convert_fusion.13), channel_id=1, source_target_pairs={{0,4},{2,6},{4,0},{6,2},{8,12},{10,14},{12,8},{14,10},{16,20},{18,... | collective-permute-start | bytes 393224 | tf_op jit(solution)/shard_map/ppermute | solution.py:182
  21.2 5.0 %collective-permute-start.18 = (bf16[128,512]{1,0:T(8,128)(2,1)S(1)}, bf16[128,512]{1,0:T(8,128)(2,1)S(1)}, u32[]{:S(2)}, u32[]{:S(2)}) collective-permute-start(bf16[128,512]{1,0:T(8,128)(2,1)S(1)} %add_convert_fusion.2), channel_id=1, source_target_pairs={{0,8},{2,10},{4,12},{6,14},{8,0},{10,2},{12,4},{14,6},{16,24},{18,... | collective-permute-start | bytes 393224 | tf_op jit(solution)/shard_map/ppermute | solution.py:182
  22.9 6.9 %collective-permute-start.13 = (bf16[128,512]{1,0:T(8,128)(2,1)S(1)}, bf16[128,512]{1,0:T(8,128)(2,1)S(1)}, u32[]{:S(2)}, u32[]{:S(2)}) collective-permute-start(bf16[128,512]{1,0:T(8,128)(2,1)S(1)} %add_convert_fusion.7), channel_id=1, source_target_pairs={{0,8},{2,10},{4,12},{6,14},{8,0},{10,2},{12,4},{14,6},{16,24},{18,... | collective-permute-start | bytes 393224 | tf_op jit(solution)/shard_map/ppermute | solution.py:182
  26.3 19.8 %copy-start.1 = (bf16[1,3,512,512]{3,2,1,0:T(8,128)(2,1)S(1)}, bf16[1,3,512,512]{3,2,1,0:T(8,128)(2,1)}, u32[]{:S(2)}) copy-start(bf16[1,3,512,512]{3,2,1,0:T(8,128)(2,1)} %w_hbm.9) | copy-start | bytes 4718596
  26.3 9.2 %collective-permute-start.19 = (bf16[128,512]{1,0:T(8,128)(2,1)S(1)}, bf16[128,512]{1,0:T(8,128)(2,1)S(1)}, u32[]{:S(2)}, u32[]{:S(2)}) collective-permute-start(bf16[128,512]{1,0:T(8,128)(2,1)S(1)} %add_convert_fusion.1), channel_id=1, source_target_pairs={{0,16},{2,18},{4,20},{6,22},{8,24},{10,26},{12,28},{14,30},{16,0},... | collective-permute-start | bytes 393224 | tf_op jit(solution)/shard_map/ppermute | solution.py:182
  29.8 8.2 %collective-permute-start.14 = (bf16[128,512]{1,0:T(8,128)(2,1)S(1)}, bf16[128,512]{1,0:T(8,128)(2,1)S(1)}, u32[]{:S(2)}, u32[]{:S(2)}) collective-permute-start(bf16[128,512]{1,0:T(8,128)(2,1)S(1)} %add_convert_fusion.6), channel_id=1, source_target_pairs={{0,16},{2,18},{4,20},{6,22},{8,24},{10,26},{12,28},{14,30},{16,0},... | collective-permute-start | bytes 393224 | tf_op jit(solution)/shard_map/ppermute | solution.py:182
  32.6 7.7 %collective-permute-start.5 = (bf16[128,512]{1,0:T(8,128)(2,1)S(1)}, bf16[128,512]{1,0:T(8,128)(2,1)S(1)}, u32[]{:S(2)}, u32[]{:S(2)}) collective-permute-start(bf16[128,512]{1,0:T(8,128)(2,1)S(1)} %add_convert_fusion.12), channel_id=1, source_target_pairs={{0,8},{2,10},{4,12},{6,14},{8,0},{10,2},{12,4},{14,6},{16,24},{18,... | collective-permute-start | bytes 393224 | tf_op jit(solution)/shard_map/ppermute | solution.py:182
  38.1 5.0 %collective-permute-start.20 = (bf16[128,512]{1,0:T(8,128)(2,1)S(1)}, bf16[128,512]{1,0:T(8,128)(2,1)S(1)}, u32[]{:S(2)}, u32[]{:S(2)}) collective-permute-start(bf16[128,512]{1,0:T(8,128)(2,1)S(1)} %get-tuple-element.38), channel_id=1, source_target_pairs={{0,4},{2,6},{4,0},{6,2},{8,12},{10,14},{12,8},{14,10},{16,20},{18,... | collective-permute-start | bytes 393224 | tf_op jit(solution)/shard_map/ppermute | solution.py:182
  39.7 5.0 %collective-permute-start.21 = (bf16[128,512]{1,0:T(8,128)(2,1)S(1)}, bf16[128,512]{1,0:T(8,128)(2,1)S(1)}, u32[]{:S(2)}, u32[]{:S(2)}) collective-permute-start(bf16[128,512]{1,0:T(8,128)(2,1)S(1)} %get-tuple-element.37), channel_id=1, source_target_pairs={{0,4},{2,6},{4,0},{6,2},{8,12},{10,14},{12,8},{14,10},{16,20},{18,... | collective-permute-start | bytes 393224 | tf_op jit(solution)/shard_map/ppermute | solution.py:182
  40.3 14.2 %collective-permute-start.6 = (bf16[128,512]{1,0:T(8,128)(2,1)S(1)}, bf16[128,512]{1,0:T(8,128)(2,1)S(1)}, u32[]{:S(2)}, u32[]{:S(2)}) collective-permute-start(bf16[128,512]{1,0:T(8,128)(2,1)S(1)} %add_convert_fusion.11), channel_id=1, source_target_pairs={{0,16},{2,18},{4,20},{6,22},{8,24},{10,26},{12,28},{14,30},{16,0},... | collective-permute-start | bytes 393224 | tf_op jit(solution)/shard_map/ppermute | solution.py:182
  40.8 4.0 %collective-permute-start.22 = (bf16[128,512]{1,0:T(8,128)(2,1)S(1)}, bf16[128,512]{1,0:T(8,128)(2,1)S(1)}, u32[]{:S(2)}, u32[]{:S(2)}) collective-permute-start(bf16[128,512]{1,0:T(8,128)(2,1)S(1)} %get-tuple-element.36), channel_id=1, source_target_pairs={{0,2},{2,0},{4,6},{6,4},{8,10},{10,8},{12,14},{14,12},{16,18},{18,... | collective-permute-start | bytes 393224 | tf_op jit(solution)/shard_map/ppermute | solution.py:182
  44.7 1.4 %collective-permute-start.23 = (bf16[128,512]{1,0:T(8,128)(2,1)S(1)}, bf16[128,512]{1,0:T(8,128)(2,1)S(1)}, u32[]{:S(2)}, u32[]{:S(2)}) collective-permute-start(bf16[128,512]{1,0:T(8,128)(2,1)S(1)} %get-tuple-element.41), channel_id=1, source_target_pairs={{0,2},{2,0},{4,6},{6,4},{8,10},{10,8},{12,14},{14,12},{16,18},{18,... | collective-permute-start | bytes 393224 | tf_op jit(solution)/shard_map/ppermute | solution.py:182
  51.6 10.2 %copy-start.3 = (bf16[256,1024]{1,0:T(8,128)(2,1)S(1)}, bf16[256,1024]{1,0:T(8,128)(2,1)}, u32[]{:S(2)}) copy-start(bf16[256,1024]{1,0:T(8,128)(2,1)} %gate.1) | copy-start | bytes 1572868
  51.6 10.2 %copy-start.5 = (f32[1024]{0:T(1024)S(1)}, f32[1024]{0:T(1024)}, u32[]{:S(2)}) copy-start(f32[1024]{0:T(1024)} %param.13) | copy-start | bytes 12292
  51.7 11.4 %collective-permute-start.24 = (bf16[512,512]{1,0:T(8,128)(2,1)S(1)}, bf16[512,512]{1,0:T(8,128)(2,1)S(1)}, u32[]{:S(2)}, u32[]{:S(2)}) collective-permute-start(bf16[512,512]{1,0:T(8,128)(2,1)S(1)} %shard_map.90.mine), channel_id=1, source_target_pairs={{0,2},{2,0},{4,6},{6,4},{8,10},{10,8},{12,14},{14,12},{16,18},{18,... | collective-permute-start | bytes 1572872 | tf_op jit(solution)/shard_map/ppermute | solution.py:182
  53.2 8.6 %collective-permute-start.1 = (bf16[256,512]{1,0:T(8,128)(2,1)S(1)}, bf16[256,512]{1,0:T(8,128)(2,1)S(1)}, u32[]{:S(2)}, u32[]{:S(2)}) collective-permute-start(bf16[256,512]{1,0:T(8,128)(2,1)S(1)} %get-tuple-element.20), channel_id=1, source_target_pairs={{0,1},{1,0},{2,3},{3,2},{4,5},{5,4},{6,7},{7,6},{8,9},{9,8},{10,11... | collective-permute-start | bytes 786440 | tf_op jit(solution)/shard_map/ppermute | solution.py:185
  54.6 5.6 %collective-permute-start.8 = (bf16[128,512]{1,0:T(8,128)(2,1)S(1)}, bf16[128,512]{1,0:T(8,128)(2,1)S(1)}, u32[]{:S(2)}, u32[]{:S(2)}) collective-permute-start(bf16[128,512]{1,0:T(8,128)(2,1)S(1)} %add_convert_fusion.10.p0), channel_id=1, source_target_pairs={{0,4},{2,6},{4,0},{6,2},{8,12},{10,14},{12,8},{14,10},{16,20},{18,... | collective-permute-start | bytes 393224 | tf_op jit(solution)/shard_map/ppermute | solution.py:182
  56.0 7.0 %collective-permute-start.7 = (bf16[128,512]{1,0:T(8,128)(2,1)S(1)}, bf16[128,512]{1,0:T(8,128)(2,1)S(1)}, u32[]{:S(2)}, u32[]{:S(2)}) collective-permute-start(bf16[128,512]{1,0:T(8,128)(2,1)S(1)} %add_convert_fusion.10.p0), channel_id=1, source_target_pairs={{0,2},{2,0},{4,6},{6,4},{8,10},{10,8},{12,14},{14,12},{16,18},{18,... | collective-permute-start | bytes 393224 | tf_op jit(solution)/shard_map/ppermute | solution.py:182
  60.1 3.0 %collective-permute-start.9 = (bf16[128,512]{1,0:T(8,128)(2,1)S(1)}, bf16[128,512]{1,0:T(8,128)(2,1)S(1)}, u32[]{:S(2)}, u32[]{:S(2)}) collective-permute-start(bf16[128,512]{1,0:T(8,128)(2,1)S(1)} %collective-permute-done.8.p2), channel_id=1, source_target_pairs={{0,2},{2,0},{4,6},{6,4},{8,10},{10,8},{12,14},{14,12},{16,18},{18,... | collective-permute-start | bytes 393224 | tf_op jit(solution)/shard_map/ppermute | solution.py:182

commit v2 on v1

v2 whole, which is shorter than its diff:
```python
import functools
import math

import jax
import jax.numpy as jnp
from jax import lax
from jax.experimental import pallas as pl
from jax.experimental.pallas import tpu as pltpu
from jax.sharding import PartitionSpec as P


NS_STEPS = 5
coef_a = 3.4445
coef_b = -4.775
coef_c = 2.0315
PLANS = {'A': (0, 1, 2), 'B': (0, 2), 'C': (0, 1)}
BF = jnp.bfloat16
F32 = jnp.float32
MIB = 1 << 20
ANY = pl.BlockSpec(memory_space=pl.ANY)
HBM = pl.BlockSpec(memory_space=pltpu.HBM)
VM = pl.BlockSpec(memory_space=pltpu.VMEM)


def dot(left, right):
    return jnp.dot(left, right, preferred_element_type=F32)


def dot_nt(left, right):
    return lax.dot_general(left, right, (((1,), (1,)), ((), ())), preferred_element_type=F32)


def dot_tn(left, right):
    return lax.dot_general(left, right, (((0,), (0,)), ((), ())), preferred_element_type=F32)


def copies(pairs, sems):
    made = [pltpu.make_async_copy(src, dst, sems.at[i]) for i, (src, dst) in enumerate(pairs)]
    for copy in made:
        copy.start()
    return made


def blocks(whole, bits):
    index = lax.axis_index("ctx")
    own = sum(((index >> b) & 1) << i for i, b in enumerate(bits))
    parts = 1 << (len(bits) - 2)
    rows = whole.shape[0] // (4 * parts)
    for r in range(4):
        for e in range(parts):
            at = pl.multiple_of((own ^ (r | (e << 2))) * rows, rows)
            yield r, pl.ds(e * rows, rows), pl.ds(at, rows)


def put_pieces(whole, pieces, bits):
    for r, part, rows in blocks(whole, bits):
        pieces[r][part, :] = whole[rows, :]


def take_pieces(pieces, whole, bits):
    for r, part, rows in blocks(whole, bits):
        whole[rows, :] = pieces[r][part, :]


def grad_two_kernel(heads, k_hbm, v_hbm, r_hbm, w_hbm, q_hbm, *refs):
    pieces, (g1_ref, g3_ref, go_ref), asked = refs[:4], refs[4:7], refs[7 : 7 + heads]
    k, v, r_ref, w1, w3, whole, sems = refs[7 + heads :]
    width = w1.shape[-1]
    me = lax.axis_index("head")
    columns = []
    for r, out in enumerate(asked):
        at = pl.multiple_of(lax.rem(me + r, heads) * width, width)
        columns.append((q_hbm.at[:, pl.ds(at, width)], out))
    ck, c1, c3, cv, cr, *cq = copies(
        [(k_hbm, k), (w_hbm.at[0, 0], w1), (w_hbm.at[0, 1], w3), (v_hbm, v), (r_hbm, r_ref)]
        + columns,
        sems,
    )
    scale = w1.shape[-1] ** (-0.5)
    ck.wait()
    c1.wait()
    g1 = dot(k[...], w1[...]) * scale
    g1_ref[...] = g1
    c3.wait()
    g3 = dot(k[...], w3[...]) * scale
    g3_ref[...] = g3
    cv.wait()
    cr.wait()
    rate = jnp.broadcast_to(r_ref[...], (128, r_ref.shape[1])).T[:, :1]
    go = (-(rate * v[...].astype(F32))).astype(BF)
    go_ref[...] = go
    hidden = (g1 * jax.nn.sigmoid(g1) * g3).astype(BF)
    whole[...] = (dot_tn(hidden, go) * scale).astype(BF)
    put_pieces(whole, pieces, PLANS["A"])
    for copy in cq:
        copy.wait()


def grad_one_kernel(k_hbm, w_hbm, g1_ref, g3_ref, go_ref, *refs):
    one, three, (w2, k, dg1, dg3, whole, sems) = refs[:4], refs[4:8], refs[8:]
    c2, ck = copies([(w_hbm.at[0, 2], w2), (k_hbm, k)], sems)
    scale = w2.shape[-1] ** (-0.5)
    c2.wait()
    dh = dot_nt(go_ref[...], w2[...]) * scale
    g1 = g1_ref[...]
    sig = jax.nn.sigmoid(g1)
    dg1[...] = (dh * g3_ref[...] * sig * (1.0 + g1 * (1.0 - sig))).astype(BF)
    dg3[...] = (dh * (g1 * sig)).astype(BF)
    ck.wait()
    whole[...] = (dot_tn(k[...], dg1[...]) * scale).astype(BF)
    put_pieces(whole, one, PLANS["B"])
    whole[...] = (dot_tn(k[...], dg3[...]) * scale).astype(BF)
    put_pieces(whole, three, PLANS["C"])


def orthogonalize(grad):
    grad = grad.astype(F32)
    total = jnp.sum(grad * grad)
    x = (grad / (jnp.sqrt(total) + 1e-07)).astype(BF)
    for _ in range(NS_STEPS):
        gram = dot_nt(x, x).astype(BF)
        square = dot(gram, gram)
        poly = (coef_b * gram.astype(F32) + coef_c * square).astype(BF)
        x = (coef_a * x.astype(F32) + dot(poly, x)).astype(BF)
    return x


def updated(weight, x):
    step_size = 0.4 * math.sqrt(x.shape[-1])
    return (weight.astype(F32) - step_size * x.astype(F32)).astype(BF)


def first_update_kernel(p0, p2, p1, p3, w_hbm, o_ref, w, whole, sems):
    index = 2 * (1 - (lax.axis_index("ctx") & 1))
    (cw,) = copies([(w_hbm.at[0, index], w)], sems)
    pieces = (p0, p1, p2, p3)

    @pl.when(index == 2)
    def _():
        take_pieces(pieces, whole, PLANS["A"])

    @pl.when(index == 0)
    def _():
        take_pieces(pieces, whole, PLANS["B"])

    x = orthogonalize(whole[...])
    cw.wait()
    o_ref[...] = updated(w[...], x)


def last_update_kernel(p0, p1, p2, p3, w_hbm, mine, theirs, o_hbm, w, new, whole, sems):
    index = 2 * (1 - (lax.axis_index("ctx") & 1))
    cw, cm, ct = copies(
        [(w_hbm.at[0, 1], w), (mine, o_hbm.at[0, index]), (theirs, o_hbm.at[0, 2 - index])], sems
    )
    take_pieces((p0, p1, p2, p3), whole, PLANS["C"])
    x = orthogonalize(whole[...])
    cw.wait()
    new[...] = updated(w[...], x)
    cn = pltpu.make_async_copy(new, o_hbm.at[0, 1], sems.at[3])
    cn.start()
    cm.wait()
    ct.wait()
    cn.wait()


def read_kernel(w_hbm, *refs):
    count = (len(refs) - 4) // 2
    queries, reads, (w1, w3, w2, sems) = refs[:count], refs[count : 2 * count], refs[2 * count :]
    made = copies([(w_hbm.at[0, 0], w1), (w_hbm.at[0, 1], w3), (w_hbm.at[0, 2], w2)], sems)
    scale = w1.shape[-1] ** (-0.5)
    for copy in made:
        copy.wait()
    for q, out in zip(queries, reads):
        rows = q[...]
        r1 = dot(rows, w1[...]) * scale
        r3 = dot(rows, w3[...]) * scale
        hq = (r1 * jax.nn.sigmoid(r1) * r3).astype(BF)
        out[...] = (dot(hq, w2[...]) * scale).astype(BF)


def norm_kernel(heads, gate, gain, *refs):
    reads, out = refs[:heads], refs[heads]
    width = reads[0].shape[-1]
    me = lax.axis_index("head")
    for r, read in enumerate(reads):
        at = pl.multiple_of(lax.rem(me + r, heads) * width, width)
        x = read[...].astype(F32)
        mean = jnp.mean(x * x, axis=-1, keepdims=True)
        g = gate[:, pl.ds(at, width)].astype(F32)
        out[:, pl.ds(at, width)] = (
            x * lax.rsqrt(mean + 1e-06) * gain[:, pl.ds(at, width)] * (g * jax.nn.sigmoid(g))
        ).astype(BF)


def local(ctx, heads, keys, values, rates, queries, fast_weights, gate, gain):
    tok, width = keys.shape
    bits = range(ctx.bit_length() - 1)
    core = lax.axis_index("ctx") & 1
    piece = jax.ShapeDtypeStruct((width // 4, width), BF)
    matrix = jax.ShapeDtypeStruct((width, width), BF)
    mat = lambda dtype: pltpu.VMEM((width, width), dtype)
    tokens = lambda dtype: pltpu.VMEM((tok, width), dtype)
    sems = lambda n: pltpu.SemaphoreType.DMA((n,))

    hbm = lambda x: pltpu.with_memory_space_constraint(x, pltpu.HBM)

    def call(kernel, mib, **kw):
        def run(*args):
            return pl.pallas_call(
                kernel, compiler_params=pltpu.CompilerParams(vmem_limit_bytes=mib * MIB), **kw
            )(*args)

        return run

    def swap(x, bit):
        return lax.ppermute(x, "ctx", [(i, i ^ (1 << bit)) for i in range(ctx)])

    def turn(x, r):
        return lax.ppermute(x, "head", [(i, (i + r) % heads) for i in range(heads)])

    outs = call(
        functools.partial(grad_two_kernel, heads), 14,
        out_shape=[piece] * 4
        + [jax.ShapeDtypeStruct((tok, width), d) for d in (F32, F32, BF)]
        + [jax.ShapeDtypeStruct((queries.shape[0], width), BF)] * heads,
        in_specs=[HBM] * 5,
        out_specs=[VM] * (7 + heads),
        scratch_shapes=[
            tokens(BF), tokens(BF), pltpu.VMEM(rates.shape, F32), mat(BF), mat(BF), mat(BF), sems(5 + heads)
        ],
    )(hbm(keys), hbm(values), hbm(rates), hbm(fast_weights), hbm(queries))
    two, (g1, g3, go), columns = outs[:4], outs[4:7], outs[7:]
    asked = [columns[0]] + [turn(columns[r], r) for r in range(1, heads)]
    outs = call(
        grad_one_kernel, 12,
        out_shape=[piece] * 8,
        in_specs=[HBM, HBM, VM, VM, VM],
        out_specs=[VM] * 8,
        scratch_shapes=[mat(BF), tokens(BF), tokens(BF), tokens(BF), mat(BF), sems(2)],
    )(hbm(keys), hbm(fast_weights), g1, g3, go)
    one, three = outs[:4], outs[4:]

    def add(x, y):
        return (x.astype(F32) + y.astype(F32)).astype(BF)

    def summed(n, p):
        plan = PLANS[n]
        far = swap(p[3], 0)
        near = swap(p[1], 0)
        give = add(p[2], far)
        keep = add(p[0], near)
        total = add(keep, swap(give, plan[1]))
        if len(plan) == 3:
            half = total.shape[0] // 2
            total = add(total[:half], swap(total[half:], plan[2]))
        for bit in bits:
            if bit not in plan:
                total = add(total, swap(total, bit))
        if len(plan) == 3:
            total = jnp.concatenate([total, swap(total, plan[2])])
        return total, swap(total, plan[1])

    two, one, three = summed("A", two), summed("B", one), summed("C", three)

    give = [jnp.where(core == 0, o, t) for o, t in zip(one, two)]
    keep = [jnp.where(core == 0, t, o) for o, t in zip(one, two)]
    got = [swap(x, 0) for x in give]
    mine = call(
        first_update_kernel, 10,
        out_shape=matrix,
        in_specs=[VM] * 4 + [HBM],
        out_specs=VM,
        scratch_shapes=[mat(BF), mat(BF), sems(1)],
    )(*keep, *got, hbm(fast_weights))
    theirs = swap(mine, 0)
    others = [swap(x, 0) for x in three]
    new_weights = call(
        last_update_kernel, 10,
        out_shape=jax.ShapeDtypeStruct(fast_weights.shape, BF),
        in_specs=[VM] * 4 + [HBM, ANY, ANY],
        out_specs=HBM,
        scratch_shapes=[mat(BF), mat(BF), mat(BF), sems(4)],
    )(three[0], others[0], three[1], others[1], hbm(fast_weights), mine, theirs)

    reads = call(
        read_kernel, 12,
        out_shape=[jax.ShapeDtypeStruct(x.shape, BF) for x in asked],
        in_specs=[HBM] + [VM] * heads,
        out_specs=[VM] * heads,
        scratch_shapes=[mat(BF)] * 3 + [sems(3)],
    )(hbm(fast_weights), *asked)
    back = [reads[0]] + [turn(reads[r], heads - r) for r in range(1, heads)]
    layer_out = call(
        functools.partial(norm_kernel, heads), 8,
        out_shape=jax.ShapeDtypeStruct(queries.shape, BF),
        in_specs=[VM] * (2 + heads),
        out_specs=VM,
    )(gate, gain.reshape(1, -1), *back)
    return layer_out, new_weights


def solution(mesh):
    in_specs = (
        P("ctx", "head"),
        P("ctx", "head"),
        P("head", "ctx"),
        P(("ctx", "head"), None),
        P("head", None, None, None),
        P(("ctx", "head"), None),
        P(),
    )
    out_specs = (P(("ctx", "head"), None), P("head", None, None, None))

    def body(*args):
        return local(mesh.shape["ctx"], mesh.shape["head"], *args)

    return jax.shard_map(
        body, mesh=mesh, in_specs=in_specs, out_specs=out_specs, check_vma=False
    )
```

time: 70.1 us -> 72.7 us (1.037)
  local copies, waits for them, and re-layouts: 4.23 us -> 0.02 us
  Pallas kernels: 18 us -> 21.4 us
  waiting for transfers between devices: 22 us -> 25.2 us
    unnamed x16 -> x4, local copies, waits for them, and re-layouts: 4.19 us -> 0.01 us
    pallas_call x6, Pallas kernels: 18 us -> 21.4 us  [run(): pl.pallas_call(kernel, compiler_params=pltpu.CompilerParams(vmem_limit_by...]
    ppermute x23 -> x24, waiting for transfers between devices: 20.2 us -> 22.7 us  [swap(): return lax.ppermute(x, 'ctx', [(i, i ^ 1 << bit) for i in range(ctx)])]
    ppermute x23 -> x24, starting transfers between devices: 19.9 us -> 20.9 us  [swap(): return lax.ppermute(x, 'ctx', [(i, i ^ 1 << bit) for i in range(ctx)])]
    ppermute x2, waiting for transfers between devices: 1.73 us -> 2.47 us  [turn(): return lax.ppermute(x, 'head', [(i, (i + r) % heads) for i in range(heads)])]
  transfers between devices with their start and end apart: 25 -> 26, of which waited for: 11 -> 10; matrix products, arithmetic and copies ran while one was open for 1% -> 1% of each run, Pallas kernels for 12% -> 17%
where the time goes in v2:
time: 72.7 us; the launch traced here: 72.5 us
  waiting for transfers between devices  25.2 us (35%)
  starting transfers between devices  24.4 us (34%)
  Pallas kernels  21.4 us (29%)
  between operations  0.98 us (1%)
    ppermute x24, waiting for transfers between devices, swap(): return lax.ppermute(x, 'ctx', [(i, i ^ 1 << bit) for i in range(ctx)])  22.7 us
    pallas_call x6, Pallas kernels, run(): pl.pallas_call(kernel, compiler_params=pltpu.CompilerParams(vmem_limit_by...  21.4 us
    ppermute x24, starting transfers between devices, swap(): return lax.ppermute(x, 'ctx', [(i, i ^ 1 << bit) for i in range(ctx)])  20.9 us
    ppermute x2, starting transfers between devices, turn(): return lax.ppermute(x, 'head', [(i, (i + r) % heads) for i in range(heads)])  3.51 us
    ppermute x2, waiting for transfers between devices, turn(): return lax.ppermute(x, 'head', [(i, (i + r) % heads) for i in range(heads)])  2.47 us
  transfers between devices with their start and end apart: 26, of which 10 were waited for; matrix products, arithmetic and copies ran while one was open for 1% of the time, Pallas kernels for 17%

profile of v2, /device:TPU:0, one launch (start us, length us, event | category | flops | bytes accessed | tf_op | source)
XLA Modules:
  0.0 72.5 jit_solution(12432031832316447587)
XLA Ops:
  0.6 2.9 %shard_map.86 = (bf16[128,512]{1,0:T(8,128)(2,1)S(1)}, bf16[128,512]{1,0:T(8,128)(2,1)S(1)}, bf16[128,512]{1,0:T(8,128)(2,1)S(1)}, bf16[128,512]{1,0:T(8,128)(2,...) custom-call(bf16[512,512]{1,0:T(8,128)(2,1)} %k_hbm.3, ...), custom_call_target="tpu_custom_call" | custom-call | tf_op jit(solution)/shard_map/pallas_call | solution.py:210
  3.6 0.6 collective-permute-start.11
  4.1 0.1 collective-permute-start.10
  4.2 2.9 %collective-permute-start = (bf16[256,512]{1,0:T(8,128)(2,1)S(1)}, bf16[256,512]{1,0:T(8,128)(2,1)S(1)}, u32[]{:S(2)}, u32[]{:S(2)}) collective-permute-start(bf16[256,512]{1,0:T(8,128)(2,1)S(1)} %get-tuple-element.22), channel_id=1, source_target_pairs={{0,1},{1,0},{2,3},{3,2},{4,5},{5,4},{6,7},{7,6},{8,9},{9,8},{10,11... | collective-permute-start | bytes 786440 | tf_op jit(solution)/shard_map/ppermute | solution.py:220
  7.2 2.6 %shard_map.89 = (bf16[128,512]{1,0:T(8,128)(2,1)S(1)}, bf16[128,512]{1,0:T(8,128)(2,1)S(1)}, bf16[128,512]{1,0:T(8,128)(2,1)S(1)}, bf16[128,512]{1,0:T(8,128)(2,...) custom-call(bf16[512,512]{1,0:T(8,128)(2,1)} %k_hbm.3, ...), custom_call_target="tpu_custom_call" | custom-call | tf_op jit(solution)/shard_map/pallas_call | solution.py:210
  9.8 0.1 collective-permute-start.2
  9.8 0.5 collective-permute-start.3
  10.3 0.0 collective-permute-done.11
  10.3 0.1 collective-permute-start.17
  10.5 1.2 %collective-permute-done.17 = bf16[128,512]{1,0:T(8,128)(2,1)S(1)} collective-permute-done((bf16[128,512]{1,0:T(8,128)(2,1)S(1)}, bf16[128,512]{1,0:T(8,128)(2,1)S(1)}, u32[]{:S(2)}, u32[]{:S(2)}) %collective-permute-start.17) | collective-permute-done | bytes 131104 | tf_op jit(solution)/shard_map/ppermute | solution.py:217
  11.7 1.5 %collective-permute-start.12 = (bf16[128,512]{1,0:T(8,128)(2,1)S(1)}, bf16[128,512]{1,0:T(8,128)(2,1)S(1)}, u32[]{:S(2)}, u32[]{:S(2)}) collective-permute-start(bf16[128,512]{1,0:T(8,128)(2,1)S(1)} %add_convert_fusion.6), channel_id=1, source_target_pairs={{0,4},{2,6},{4,0},{6,2},{8,12},{10,14},{12,8},{14,10},{16,20},{18,... | collective-permute-start | bytes 393224 | tf_op jit(solution)/shard_map/ppermute | solution.py:217
  13.2 0.0 collective-permute-done.10
  13.2 0.1 collective-permute-start.16
  13.3 4.0 %collective-permute-done.12 = bf16[128,512]{1,0:T(8,128)(2,1)S(1)} collective-permute-done((bf16[128,512]{1,0:T(8,128)(2,1)S(1)}, bf16[128,512]{1,0:T(8,128)(2,1)S(1)}, u32[]{:S(2)}, u32[]{:S(2)}) %collective-permute-start.12) | collective-permute-done | bytes 131104 | tf_op jit(solution)/shard_map/ppermute | solution.py:217
  17.3 1.6 %collective-permute-start.18 = (bf16[128,512]{1,0:T(8,128)(2,1)S(1)}, bf16[128,512]{1,0:T(8,128)(2,1)S(1)}, u32[]{:S(2)}, u32[]{:S(2)}) collective-permute-start(bf16[128,512]{1,0:T(8,128)(2,1)S(1)} %add_convert_fusion.3), channel_id=1, source_target_pairs={{0,8},{2,10},{4,12},{6,14},{8,0},{10,2},{12,4},{14,6},{16,24},{18,... | collective-permute-start | bytes 393224 | tf_op jit(solution)/shard_map/ppermute | solution.py:217
  18.9 0.1 add_convert_fusion.5
  18.9 0.0 collective-permute-done.16
  18.9 0.5 collective-permute-start.13
  19.4 3.3 %collective-permute-done.18 = bf16[128,512]{1,0:T(8,128)(2,1)S(1)} collective-permute-done((bf16[128,512]{1,0:T(8,128)(2,1)S(1)}, bf16[128,512]{1,0:T(8,128)(2,1)S(1)}, u32[]{:S(2)}, u32[]{:S(2)}) %collective-permute-start.18) | collective-permute-done | bytes 131104 | tf_op jit(solution)/shard_map/ppermute | solution.py:217
  22.7 0.1 add_convert_fusion.2
  22.8 1.6 %collective-permute-start.19 = (bf16[128,512]{1,0:T(8,128)(2,1)S(1)}, bf16[128,512]{1,0:T(8,128)(2,1)S(1)}, u32[]{:S(2)}, u32[]{:S(2)}) collective-permute-start(bf16[128,512]{1,0:T(8,128)(2,1)S(1)} %add_convert_fusion.2), channel_id=1, source_target_pairs={{0,4},{2,6},{4,0},{6,2},{8,12},{10,14},{12,8},{14,10},{16,20},{18,... | collective-permute-start | bytes 393224 | tf_op jit(solution)/shard_map/ppermute | solution.py:217
  24.4 0.0 collective-permute-done.13
  24.4 2.7 %collective-permute-start.14 = (bf16[64,512]{1,0:T(8,128)(2,1)S(1)}, bf16[64,512]{1,0:T(8,128)(2,1)S(1)}, u32[]{:S(2)}, u32[]{:S(2)}) collective-permute-start(bf16[64,512]{1,0:T(8,128)(2,1)S(1)} %add_convert_fusion.14), channel_id=1, source_target_pairs={{0,16},{2,18},{4,20},{6,22},{8,24},{10,26},{12,28},{14,30},{16,0},... | collective-permute-start | bytes 196616 | tf_op jit(solution)/shard_map/ppermute | solution.py:217
  27.0 0.8 %collective-permute-done.19 = bf16[128,512]{1,0:T(8,128)(2,1)S(1)} collective-permute-done((bf16[128,512]{1,0:T(8,128)(2,1)S(1)}, bf16[128,512]{1,0:T(8,128)(2,1)S(1)}, u32[]{:S(2)}, u32[]{:S(2)}) %collective-permute-start.19) | collective-permute-done | bytes 131104 | tf_op jit(solution)/shard_map/ppermute | solution.py:217
  27.9 2.6 %collective-permute-start.20 = (bf16[128,512]{1,0:T(8,128)(2,1)S(1)}, bf16[128,512]{1,0:T(8,128)(2,1)S(1)}, u32[]{:S(2)}, u32[]{:S(2)}) collective-permute-start(bf16[128,512]{1,0:T(8,128)(2,1)S(1)} %add_convert_fusion.1), channel_id=1, source_target_pairs={{0,16},{2,18},{4,20},{6,22},{8,24},{10,26},{12,28},{14,30},{16,0},... | collective-permute-start | bytes 393224 | tf_op jit(solution)/shard_map/ppermute | solution.py:217
  30.5 1.6 %collective-permute-done.14 = bf16[64,512]{1,0:T(8,128)(2,1)S(1)} collective-permute-done((bf16[64,512]{1,0:T(8,128)(2,1)S(1)}, bf16[64,512]{1,0:T(8,128)(2,1)S(1)}, u32[]{:S(2)}, u32[]{:S(2)}) %collective-permute-start.14) | collective-permute-done | bytes 65568 | tf_op jit(solution)/shard_map/ppermute | solution.py:217
  32.2 0.1 collective-permute-start.15
  32.3 0.0 collective-permute-done.3
  32.3 1.5 %collective-permute-start.4 = (bf16[128,512]{1,0:T(8,128)(2,1)S(1)}, bf16[128,512]{1,0:T(8,128)(2,1)S(1)}, u32[]{:S(2)}, u32[]{:S(2)}) collective-permute-start(bf16[128,512]{1,0:T(8,128)(2,1)S(1)} %add_convert_fusion.11), channel_id=1, source_target_pairs={{0,4},{2,6},{4,0},{6,2},{8,12},{10,14},{12,8},{14,10},{16,20},{18,... | collective-permute-start | bytes 393224 | tf_op jit(solution)/shard_map/ppermute | solution.py:217
  33.8 3.4 %collective-permute-done.15 = bf16[64,512]{1,0:T(8,128)(2,1)S(1)} collective-permute-done((bf16[64,512]{1,0:T(8,128)(2,1)S(1)}, bf16[64,512]{1,0:T(8,128)(2,1)S(1)}, u32[]{:S(2)}, u32[]{:S(2)}) %collective-permute-start.15) | collective-permute-done | bytes 65568 | tf_op jit(solution)/shard_map/ppermute | solution.py:217
  37.2 0.0 collective-permute-done.20
  37.2 0.1 broadcast_select_fusion.1
  37.3 0.1 collective-permute-start.22
  37.4 1.5 %collective-permute-start.21 = (bf16[128,512]{1,0:T(8,128)(2,1)S(1)}, bf16[128,512]{1,0:T(8,128)(2,1)S(1)}, u32[]{:S(2)}, u32[]{:S(2)}) collective-permute-start(bf16[128,512]{1,0:T(8,128)(2,1)S(1)} %get-tuple-element.44), channel_id=1, source_target_pairs={{0,4},{2,6},{4,0},{6,2},{8,12},{10,14},{12,8},{14,10},{16,20},{18,... | collective-permute-start | bytes 393224 | tf_op jit(solution)/shard_map/ppermute | solution.py:217
  38.9 0.0 collective-permute-done.2
  38.9 0.0 collective-permute-done.4
  38.9 0.1 add_convert_fusion.10
  39.0 1.6 %collective-permute-start.5 = (bf16[128,512]{1,0:T(8,128)(2,1)S(1)}, bf16[128,512]{1,0:T(8,128)(2,1)S(1)}, u32[]{:S(2)}, u32[]{:S(2)}) collective-permute-start(bf16[128,512]{1,0:T(8,128)(2,1)S(1)} %add_convert_fusion.10), channel_id=1, source_target_pairs={{0,8},{2,10},{4,12},{6,14},{8,0},{10,2},{12,4},{14,6},{16,24},{18,... | collective-permute-start | bytes 393224 | tf_op jit(solution)/shard_map/ppermute | solution.py:217
  40.6 0.0 collective-permute-start.23
  40.6 1.9 %collective-permute-done.21 = bf16[128,512]{1,0:T(8,128)(2,1)S(1)} collective-permute-done((bf16[128,512]{1,0:T(8,128)(2,1)S(1)}, bf16[128,512]{1,0:T(8,128)(2,1)S(1)}, u32[]{:S(2)}, u32[]{:S(2)}) %collective-permute-start.21) | collective-permute-done | bytes 131104 | tf_op jit(solution)/shard_map/ppermute | solution.py:217
  42.5 0.0 collective-permute-done.22
  42.5 0.1 collective-permute-start.24
  42.6 1.4 %collective-permute-done.5 = bf16[128,512]{1,0:T(8,128)(2,1)S(1)} collective-permute-done((bf16[128,512]{1,0:T(8,128)(2,1)S(1)}, bf16[128,512]{1,0:T(8,128)(2,1)S(1)}, u32[]{:S(2)}, u32[]{:S(2)}) %collective-permute-start.5) | collective-permute-done | bytes 131104 | tf_op jit(solution)/shard_map/ppermute | solution.py:217
  44.0 3.6 %collective-permute-start.6 = (bf16[128,512]{1,0:T(8,128)(2,1)S(1)}, bf16[128,512]{1,0:T(8,128)(2,1)S(1)}, u32[]{:S(2)}, u32[]{:S(2)}) collective-permute-start(bf16[128,512]{1,0:T(8,128)(2,1)S(1)} %add_convert_fusion.9), channel_id=1, source_target_pairs={{0,16},{2,18},{4,20},{6,22},{8,24},{10,26},{12,28},{14,30},{16,0},... | collective-permute-start | bytes 393224 | tf_op jit(solution)/shard_map/ppermute | solution.py:217
  47.6 0.0 collective-permute-done.23.p1
  47.6 0.0 collective-permute-done.24.p3
  47.6 5.7 %shard_map.90.mine = bf16[512,512]{1,0:T(8,128)(2,1)S(1)} custom-call(bf16[128,512]{1,0:T(8,128)(2,1)S(1)} %get-tuple-element.45.p0, bf16[128,512]{1,0:T(8,128)(2,1)S(1)} %get-tuple-element.43.p2, bf16[128,512]{1,0:T(8,128)(2,1)S(1)} %collective-permute-done.23.p1, bf16[128,512]{1,0:T(8,128)(2,1)S(1)} %collective-permute-done.24.p3, ...), custom_call_target="tpu_custom_call" | custom-call | tf_op jit(solution)/shard_map/pallas_call | solution.py:210
  53.3 0.0 copy-start
  53.3 0.0 copy-start.1
  53.3 0.1 collective-permute-start.25
  53.4 0.0 collective-permute-done.refs_1_
  53.4 2.6 %shard_map.87 = (bf16[256,512]{1,0:T(8,128)(2,1)S(1)}, bf16[256,512]{1,0:T(8,128)(2,1)S(1)}) custom-call(bf16[1,3,512,512]{3,2,1,0:T(8,128)(2,1)} %w_hbm.9, bf16[256,512]{1,0:T(8,128)(2,1)S(1)} %get-tuple-element.21.refs_0_, bf16[256,512]{1,0:T(8,128)(2,1)S(1)} %collective-permute-done.refs_1_), custom_call_target="tpu_custom_call" | custom-call | tf_op jit(solution)/shard_map/pallas_call | solution.py:210
  56.1 0.6 collective-permute-start.1
  56.7 0.0 collective-permute-done.6
  56.7 0.6 collective-permute-start.8
  57.3 0.0 collective-permute-start.7
  57.3 5.0 %collective-permute-done.8.p2 = bf16[128,512]{1,0:T(8,128)(2,1)S(1)} collective-permute-done((bf16[128,512]{1,0:T(8,128)(2,1)S(1)}, bf16[128,512]{1,0:T(8,128)(2,1)S(1)}, u32[]{:S(2)}, u32[]{:S(2)}) %collective-permute-start.8) | collective-permute-done | bytes 131104 | tf_op jit(solution)/shard_map/ppermute | solution.py:217
  62.3 0.0 collective-permute-start.9
  62.3 2.5 %collective-permute-done.1.refs_1_ = bf16[256,512]{1,0:T(8,128)(2,1)S(1)} collective-permute-done((bf16[256,512]{1,0:T(8,128)(2,1)S(1)}, bf16[256,512]{1,0:T(8,128)(2,1)S(1)}, u32[]{:S(2)}, u32[]{:S(2)}) %collective-permute-start.1) | collective-permute-done | bytes 262176 | tf_op jit(solution)/shard_map/ppermute | solution.py:220
  64.8 1.2 %shard_map.88 = bf16[256,1024]{1,0:T(8,128)(2,1)} custom-call(bf16[256,1024]{1,0:T(8,128)(2,1)S(1)} %copy-done, f32[1,1024]{1,0:T(1,128)S(1)} %bitcast.1, bf16[256,512]{1,0:T(8,128)(2,1)S(1)} %get-tuple-element.23.refs_0_, bf16[256,512]{1,0:T(8,128)(2,1)S(1)} %collective-permute-done.1.refs_1_), custom_call_target="tpu_custom_call" | custom-call | tf_op jit(solution)/shard_map/pallas_call | solution.py:210
  66.0 0.0 collective-permute-done.7.p1
  66.0 0.0 collective-permute-done.9.p3
  66.0 0.0 collective-permute-done.25.theirs
  66.0 6.3 %shard_map.91 = bf16[1,3,512,512]{3,2,1,0:T(8,128)(2,1)} custom-call(bf16[128,512]{1,0:T(8,128)(2,1)S(1)} %add_convert_fusion.8.p0, bf16[128,512]{1,0:T(8,128)(2,1)S(1)} %collective-permute-done.7.p1, bf16[128,512]{1,0:T(8,128)(2,1)S(1)} %collective-permute-done.8.p2, bf16[128,512]{1,0:T(8,128)(2,1)S(1)} %collective-permute-done.9.p3, ...), custom_call_target="tpu_custom_call" | custom-call | tf_op jit(solution)/shard_map/pallas_call | solution.py:210
  (13 shorter events, 0.3 us)
Async XLA Ops:
  3.6 6.8 %collective-permute-start.11 = (bf16[128,512]{1,0:T(8,128)(2,1)S(1)}, bf16[128,512]{1,0:T(8,128)(2,1)S(1)}, u32[]{:S(2)}, u32[]{:S(2)}) collective-permute-start(bf16[128,512]{1,0:T(8,128)(2,1)S(1)} %get-tuple-element.35), channel_id=1, source_target_pairs={{0,2},{2,0},{4,6},{6,4},{8,10},{10,8},{12,14},{14,12},{16,18},{18,... | collective-permute-start | bytes 393224 | tf_op jit(solution)/shard_map/ppermute | solution.py:217
  4.1 9.1 %collective-permute-start.10 = (bf16[128,512]{1,0:T(8,128)(2,1)S(1)}, bf16[128,512]{1,0:T(8,128)(2,1)S(1)}, u32[]{:S(2)}, u32[]{:S(2)}) collective-permute-start(bf16[128,512]{1,0:T(8,128)(2,1)S(1)} %get-tuple-element.33), channel_id=1, source_target_pairs={{0,2},{2,0},{4,6},{6,4},{8,10},{10,8},{12,14},{14,12},{16,18},{18,... | collective-permute-start | bytes 393224 | tf_op jit(solution)/shard_map/ppermute | solution.py:217
  4.2 49.2 %collective-permute-start = (bf16[256,512]{1,0:T(8,128)(2,1)S(1)}, bf16[256,512]{1,0:T(8,128)(2,1)S(1)}, u32[]{:S(2)}, u32[]{:S(2)}) collective-permute-start(bf16[256,512]{1,0:T(8,128)(2,1)S(1)} %get-tuple-element.22), channel_id=1, source_target_pairs={{0,1},{1,0},{2,3},{3,2},{4,5},{5,4},{6,7},{7,6},{8,9},{9,8},{10,11... | collective-permute-start | bytes 786440 | tf_op jit(solution)/shard_map/ppermute | solution.py:220
  9.8 29.1 %collective-permute-start.2 = (bf16[128,512]{1,0:T(8,128)(2,1)S(1)}, bf16[128,512]{1,0:T(8,128)(2,1)S(1)}, u32[]{:S(2)}, u32[]{:S(2)}) collective-permute-start(bf16[128,512]{1,0:T(8,128)(2,1)S(1)} %get-tuple-element.29), channel_id=1, source_target_pairs={{0,2},{2,0},{4,6},{6,4},{8,10},{10,8},{12,14},{14,12},{16,18},{18,... | collective-permute-start | bytes 393224 | tf_op jit(solution)/shard_map/ppermute | solution.py:217
  9.8 22.5 %collective-permute-start.3 = (bf16[128,512]{1,0:T(8,128)(2,1)S(1)}, bf16[128,512]{1,0:T(8,128)(2,1)S(1)}, u32[]{:S(2)}, u32[]{:S(2)}) collective-permute-start(bf16[128,512]{1,0:T(8,128)(2,1)S(1)} %get-tuple-element.31), channel_id=1, source_target_pairs={{0,2},{2,0},{4,6},{6,4},{8,10},{10,8},{12,14},{14,12},{16,18},{18,... | collective-permute-start | bytes 393224 | tf_op jit(solution)/shard_map/ppermute | solution.py:217
  10.3 1.3 %collective-permute-start.17 = (bf16[128,512]{1,0:T(8,128)(2,1)S(1)}, bf16[128,512]{1,0:T(8,128)(2,1)S(1)}, u32[]{:S(2)}, u32[]{:S(2)}) collective-permute-start(bf16[128,512]{1,0:T(8,128)(2,1)S(1)} %get-tuple-element.39), channel_id=1, source_target_pairs={{0,2},{2,0},{4,6},{6,4},{8,10},{10,8},{12,14},{14,12},{16,18},{18,... | collective-permute-start | bytes 393224 | tf_op jit(solution)/shard_map/ppermute | solution.py:217
  11.7 5.6 %collective-permute-start.12 = (bf16[128,512]{1,0:T(8,128)(2,1)S(1)}, bf16[128,512]{1,0:T(8,128)(2,1)S(1)}, u32[]{:S(2)}, u32[]{:S(2)}) collective-permute-start(bf16[128,512]{1,0:T(8,128)(2,1)S(1)} %add_convert_fusion.6), channel_id=1, source_target_pairs={{0,4},{2,6},{4,0},{6,2},{8,12},{10,14},{12,8},{14,10},{16,20},{18,... | collective-permute-start | bytes 393224 | tf_op jit(solution)/shard_map/ppermute | solution.py:217
  13.2 5.7 %collective-permute-start.16 = (bf16[128,512]{1,0:T(8,128)(2,1)S(1)}, bf16[128,512]{1,0:T(8,128)(2,1)S(1)}, u32[]{:S(2)}, u32[]{:S(2)}) collective-permute-start(bf16[128,512]{1,0:T(8,128)(2,1)S(1)} %get-tuple-element.37), channel_id=1, source_target_pairs={{0,2},{2,0},{4,6},{6,4},{8,10},{10,8},{12,14},{14,12},{16,18},{18,... | collective-permute-start | bytes 393224 | tf_op jit(solution)/shard_map/ppermute | solution.py:217
  17.3 5.5 %collective-permute-start.18 = (bf16[128,512]{1,0:T(8,128)(2,1)S(1)}, bf16[128,512]{1,0:T(8,128)(2,1)S(1)}, u32[]{:S(2)}, u32[]{:S(2)}) collective-permute-start(bf16[128,512]{1,0:T(8,128)(2,1)S(1)} %add_convert_fusion.3), channel_id=1, source_target_pairs={{0,8},{2,10},{4,12},{6,14},{8,0},{10,2},{12,4},{14,6},{16,24},{18,... | collective-permute-start | bytes 393224 | tf_op jit(solution)/shard_map/ppermute | solution.py:217
  18.9 5.4 %collective-permute-start.13 = (bf16[64,512]{1,0:T(8,128)(2,1)S(1)}, bf16[64,512]{1,0:T(8,128)(2,1)S(1)}, u32[]{:S(2)}, u32[]{:S(2)}) collective-permute-start(bf16[64,512]{1,0:T(8,128)(2,1)S(1)} %slice.9), channel_id=1, source_target_pairs={{0,8},{2,10},{4,12},{6,14},{8,0},{10,2},{12,4},{14,6},{16,24},{18,... | collective-permute-start | bytes 196616 | tf_op jit(solution)/shard_map/ppermute | solution.py:217
  22.8 5.0 %collective-permute-start.19 = (bf16[128,512]{1,0:T(8,128)(2,1)S(1)}, bf16[128,512]{1,0:T(8,128)(2,1)S(1)}, u32[]{:S(2)}, u32[]{:S(2)}) collective-permute-start(bf16[128,512]{1,0:T(8,128)(2,1)S(1)} %add_convert_fusion.2), channel_id=1, source_target_pairs={{0,4},{2,6},{4,0},{6,2},{8,12},{10,14},{12,8},{14,10},{16,20},{18,... | collective-permute-start | bytes 393224 | tf_op jit(solution)/shard_map/ppermute | solution.py:217
  24.4 7.8 %collective-permute-start.14 = (bf16[64,512]{1,0:T(8,128)(2,1)S(1)}, bf16[64,512]{1,0:T(8,128)(2,1)S(1)}, u32[]{:S(2)}, u32[]{:S(2)}) collective-permute-start(bf16[64,512]{1,0:T(8,128)(2,1)S(1)} %add_convert_fusion.14), channel_id=1, source_target_pairs={{0,16},{2,18},{4,20},{6,22},{8,24},{10,26},{12,28},{14,30},{16,0},... | collective-permute-start | bytes 196616 | tf_op jit(solution)/shard_map/ppermute | solution.py:217
  27.9 9.4 %collective-permute-start.20 = (bf16[128,512]{1,0:T(8,128)(2,1)S(1)}, bf16[128,512]{1,0:T(8,128)(2,1)S(1)}, u32[]{:S(2)}, u32[]{:S(2)}) collective-permute-start(bf16[128,512]{1,0:T(8,128)(2,1)S(1)} %add_convert_fusion.1), channel_id=1, source_target_pairs={{0,16},{2,18},{4,20},{6,22},{8,24},{10,26},{12,28},{14,30},{16,0},... | collective-permute-start | bytes 393224 | tf_op jit(solution)/shard_map/ppermute | solution.py:217
  32.2 5.0 %collective-permute-start.15 = (bf16[64,512]{1,0:T(8,128)(2,1)S(1)}, bf16[64,512]{1,0:T(8,128)(2,1)S(1)}, u32[]{:S(2)}, u32[]{:S(2)}) collective-permute-start(bf16[64,512]{1,0:T(8,128)(2,1)S(1)} %add_convert_fusion.13), channel_id=1, source_target_pairs={{0,8},{2,10},{4,12},{6,14},{8,0},{10,2},{12,4},{14,6},{16,24},{18,... | collective-permute-start | bytes 196616 | tf_op jit(solution)/shard_map/ppermute | solution.py:217
  32.3 6.6 %collective-permute-start.4 = (bf16[128,512]{1,0:T(8,128)(2,1)S(1)}, bf16[128,512]{1,0:T(8,128)(2,1)S(1)}, u32[]{:S(2)}, u32[]{:S(2)}) collective-permute-start(bf16[128,512]{1,0:T(8,128)(2,1)S(1)} %add_convert_fusion.11), channel_id=1, source_target_pairs={{0,4},{2,6},{4,0},{6,2},{8,12},{10,14},{12,8},{14,10},{16,20},{18,... | collective-permute-start | bytes 393224 | tf_op jit(solution)/shard_map/ppermute | solution.py:217
  37.3 5.2 %collective-permute-start.22 = (bf16[128,512]{1,0:T(8,128)(2,1)S(1)}, bf16[128,512]{1,0:T(8,128)(2,1)S(1)}, u32[]{:S(2)}, u32[]{:S(2)}) collective-permute-start(bf16[128,512]{1,0:T(8,128)(2,1)S(1)} %get-tuple-element.41), channel_id=1, source_target_pairs={{0,8},{2,10},{4,12},{6,14},{8,0},{10,2},{12,4},{14,6},{16,24},{18,... | collective-permute-start | bytes 393224 | tf_op jit(solution)/shard_map/ppermute | solution.py:217
  37.4 5.0 %collective-permute-start.21 = (bf16[128,512]{1,0:T(8,128)(2,1)S(1)}, bf16[128,512]{1,0:T(8,128)(2,1)S(1)}, u32[]{:S(2)}, u32[]{:S(2)}) collective-permute-start(bf16[128,512]{1,0:T(8,128)(2,1)S(1)} %get-tuple-element.44), channel_id=1, source_target_pairs={{0,4},{2,6},{4,0},{6,2},{8,12},{10,14},{12,8},{14,10},{16,20},{18,... | collective-permute-start | bytes 393224 | tf_op jit(solution)/shard_map/ppermute | solution.py:217
  39.0 5.0 %collective-permute-start.5 = (bf16[128,512]{1,0:T(8,128)(2,1)S(1)}, bf16[128,512]{1,0:T(8,128)(2,1)S(1)}, u32[]{:S(2)}, u32[]{:S(2)}) collective-permute-start(bf16[128,512]{1,0:T(8,128)(2,1)S(1)} %add_convert_fusion.10), channel_id=1, source_target_pairs={{0,8},{2,10},{4,12},{6,14},{8,0},{10,2},{12,4},{14,6},{16,24},{18,... | collective-permute-start | bytes 393224 | tf_op jit(solution)/shard_map/ppermute | solution.py:217
  40.6 7.0 %collective-permute-start.23 = (bf16[128,512]{1,0:T(8,128)(2,1)S(1)}, bf16[128,512]{1,0:T(8,128)(2,1)S(1)}, u32[]{:S(2)}, u32[]{:S(2)}) collective-permute-start(bf16[128,512]{1,0:T(8,128)(2,1)S(1)} %get-tuple-element.40), channel_id=1, source_target_pairs={{0,2},{2,0},{4,6},{6,4},{8,10},{10,8},{12,14},{14,12},{16,18},{18,... | collective-permute-start | bytes 393224 | tf_op jit(solution)/shard_map/ppermute | solution.py:217
  42.5 5.1 %collective-permute-start.24 = (bf16[128,512]{1,0:T(8,128)(2,1)S(1)}, bf16[128,512]{1,0:T(8,128)(2,1)S(1)}, u32[]{:S(2)}, u32[]{:S(2)}) collective-permute-start(bf16[128,512]{1,0:T(8,128)(2,1)S(1)} %get-tuple-element.42), channel_id=1, source_target_pairs={{0,2},{2,0},{4,6},{6,4},{8,10},{10,8},{12,14},{14,12},{16,18},{18,... | collective-permute-start | bytes 393224 | tf_op jit(solution)/shard_map/ppermute | solution.py:217
  44.0 12.6 %collective-permute-start.6 = (bf16[128,512]{1,0:T(8,128)(2,1)S(1)}, bf16[128,512]{1,0:T(8,128)(2,1)S(1)}, u32[]{:S(2)}, u32[]{:S(2)}) collective-permute-start(bf16[128,512]{1,0:T(8,128)(2,1)S(1)} %add_convert_fusion.9), channel_id=1, source_target_pairs={{0,16},{2,18},{4,20},{6,22},{8,24},{10,26},{12,28},{14,30},{16,0},... | collective-permute-start | bytes 393224 | tf_op jit(solution)/shard_map/ppermute | solution.py:217
  53.3 11.5 %copy-start = (bf16[256,1024]{1,0:T(8,128)(2,1)S(1)}, bf16[256,1024]{1,0:T(8,128)(2,1)}, u32[]{:S(2)}) copy-start(bf16[256,1024]{1,0:T(8,128)(2,1)} %gate.1) | copy-start | bytes 1572868
  53.3 11.5 %copy-start.1 = (f32[1024]{0:T(1024)S(1)}, f32[1024]{0:T(1024)}, u32[]{:S(2)}) copy-start(f32[1024]{0:T(1024)} %param.13) | copy-start | bytes 12292
  53.3 12.7 %collective-permute-start.25 = (bf16[512,512]{1,0:T(8,128)(2,1)S(1)}, bf16[512,512]{1,0:T(8,128)(2,1)S(1)}, u32[]{:S(2)}, u32[]{:S(2)}) collective-permute-start(bf16[512,512]{1,0:T(8,128)(2,1)S(1)} %shard_map.90.mine), channel_id=1, source_target_pairs={{0,2},{2,0},{4,6},{6,4},{8,10},{10,8},{12,14},{14,12},{16,18},{18,... | collective-permute-start | bytes 1572872 | tf_op jit(solution)/shard_map/ppermute | solution.py:217
  56.1 8.7 %collective-permute-start.1 = (bf16[256,512]{1,0:T(8,128)(2,1)S(1)}, bf16[256,512]{1,0:T(8,128)(2,1)S(1)}, u32[]{:S(2)}, u32[]{:S(2)}) collective-permute-start(bf16[256,512]{1,0:T(8,128)(2,1)S(1)} %get-tuple-element.24), channel_id=1, source_target_pairs={{0,1},{1,0},{2,3},{3,2},{4,5},{5,4},{6,7},{7,6},{8,9},{9,8},{10,11... | collective-permute-start | bytes 786440 | tf_op jit(solution)/shard_map/ppermute | solution.py:220
  56.7 5.6 %collective-permute-start.8 = (bf16[128,512]{1,0:T(8,128)(2,1)S(1)}, bf16[128,512]{1,0:T(8,128)(2,1)S(1)}, u32[]{:S(2)}, u32[]{:S(2)}) collective-permute-start(bf16[128,512]{1,0:T(8,128)(2,1)S(1)} %add_convert_fusion.8.p0), channel_id=1, source_target_pairs={{0,4},{2,6},{4,0},{6,2},{8,12},{10,14},{12,8},{14,10},{16,20},{18,... | collective-permute-start | bytes 393224 | tf_op jit(solution)/shard_map/ppermute | solution.py:217
  57.3 8.7 %collective-permute-start.7 = (bf16[128,512]{1,0:T(8,128)(2,1)S(1)}, bf16[128,512]{1,0:T(8,128)(2,1)S(1)}, u32[]{:S(2)}, u32[]{:S(2)}) collective-permute-start(bf16[128,512]{1,0:T(8,128)(2,1)S(1)} %add_convert_fusion.8.p0), channel_id=1, source_target_pairs={{0,2},{2,0},{4,6},{6,4},{8,10},{10,8},{12,14},{14,12},{16,18},{18,... | collective-permute-start | bytes 393224 | tf_op jit(solution)/shard_map/ppermute | solution.py:217
  62.3 3.7 %collective-permute-start.9 = (bf16[128,512]{1,0:T(8,128)(2,1)S(1)}, bf16[128,512]{1,0:T(8,128)(2,1)S(1)}, u32[]{:S(2)}, u32[]{:S(2)}) collective-permute-start(bf16[128,512]{1,0:T(8,128)(2,1)S(1)} %collective-permute-done.8.p2), channel_id=1, source_target_pairs={{0,2},{2,0},{4,6},{6,4},{8,10},{10,8},{12,14},{14,12},{16,18},{18,... | collective-permute-start | bytes 393224 | tf_op jit(solution)/shard_map/ppermute | solution.py:217

commit v3 on v2

--- a/solution.py
+++ b/solution.py
@@ -13,7 +13,7 @@
 coef_a = 3.4445
 coef_b = -4.775
 coef_c = 2.0315
-PLANS = {'A': (0, 1, 2), 'B': (0, 2), 'C': (0, 1)}
+PLANS = {'A': (0, 1, 2), 'B': (0, 2, 1), 'C': (0, 1)}
 BF = jnp.bfloat16
 F32 = jnp.float32
 MIB = 1 << 20
@@ -63,8 +63,9 @@
 
 
 def grad_two_kernel(heads, k_hbm, v_hbm, r_hbm, w_hbm, q_hbm, *refs):
-    pieces, (g1_ref, g3_ref, go_ref), asked = refs[:4], refs[4:7], refs[7 : 7 + heads]
-    k, v, r_ref, w1, w3, whole, sems = refs[7 + heads :]
+    pieces, (g1_ref, g3_ref, go_ref), (k, w1, w3, w2) = refs[:4], refs[4:7], refs[7:11]
+    asked = refs[11 : 11 + heads]
+    v, r_ref, whole, sems = refs[11 + heads :]
     width = w1.shape[-1]
     me = lax.axis_index("head")
     columns = []
@@ -73,6 +74,7 @@
         columns.append((q_hbm.at[:, pl.ds(at, width)], out))
     ck, c1, c3, cv, cr, *cq = copies(
         [(k_hbm, k), (w_hbm.at[0, 0], w1), (w_hbm.at[0, 1], w3), (v_hbm, v), (r_hbm, r_ref)]
+        + [(w_hbm.at[0, 2], w2)]
         + columns,
         sems,
     )
@@ -96,33 +98,54 @@
         copy.wait()
 
 
-def grad_one_kernel(k_hbm, w_hbm, g1_ref, g3_ref, go_ref, *refs):
-    one, three, (w2, k, dg1, dg3, whole, sems) = refs[:4], refs[4:8], refs[8:]
-    c2, ck = copies([(w_hbm.at[0, 2], w2), (k_hbm, k)], sems)
+def grad_one_kernel(k, w2, g1_ref, g3_ref, go_ref, *refs):
+    one, three, (dg1, dg3, whole) = refs[:4], refs[4:8], refs[8:]
     scale = w2.shape[-1] ** (-0.5)
-    c2.wait()
     dh = dot_nt(go_ref[...], w2[...]) * scale
     g1 = g1_ref[...]
     sig = jax.nn.sigmoid(g1)
     dg1[...] = (dh * g3_ref[...] * sig * (1.0 + g1 * (1.0 - sig))).astype(BF)
     dg3[...] = (dh * (g1 * sig)).astype(BF)
-    ck.wait()
     whole[...] = (dot_tn(k[...], dg1[...]) * scale).astype(BF)
     put_pieces(whole, one, PLANS["B"])
     whole[...] = (dot_tn(k[...], dg3[...]) * scale).astype(BF)
     put_pieces(whole, three, PLANS["C"])
 
 
-def orthogonalize(grad):
+def normalized(grad):
     grad = grad.astype(F32)
     total = jnp.sum(grad * grad)
-    x = (grad / (jnp.sqrt(total) + 1e-07)).astype(BF)
+    return (grad / (jnp.sqrt(total) + 1e-07)).astype(BF)
+
+
+def polynomial(gram, square):
+    return (coef_b * gram.astype(F32) + coef_c * square).astype(BF)
+
+
+def step(x):
+    half = x.shape[0] // 2
+    x0, x1 = x[:half], x[half:]
+    cat = jnp.concatenate
+    a00 = dot_nt(x0, x0).astype(BF)
+    a01 = dot_nt(x0, x1).astype(BF)
+    a11 = dot_nt(x1, x1).astype(BF)
+    a0 = cat([a00, a01], 1)
+    a1 = cat([a01.T, a11], 1)
+    b00 = polynomial(a00, dot_nt(a0, a0))
+    b01 = polynomial(a01, dot_nt(a0, a1))
+    b11 = polynomial(a11, dot_nt(a1, a1))
+    b0 = cat([b00, b01], 1)
+    b1 = cat([b01.T, b11], 1)
+    y0 = (coef_a * x0.astype(F32) + dot(b0, x)).astype(BF)
+    y1 = (coef_a * x1.astype(F32) + dot(b1, x)).astype(BF)
+    return cat([y0, y1], 0)
+
+
+def orthogonalize(*grads):
+    xs = [normalized(grad) for grad in grads]
     for _ in range(NS_STEPS):
-        gram = dot_nt(x, x).astype(BF)
-        square = dot(gram, gram)
-        poly = (coef_b * gram.astype(F32) + coef_c * square).astype(BF)
-        x = (coef_a * x.astype(F32) + dot(poly, x)).astype(BF)
-    return x
+        xs = [step(x) for x in xs]
+    return xs
 
 
 def updated(weight, x):
@@ -130,57 +153,54 @@
     return (weight.astype(F32) - step_size * x.astype(F32)).astype(BF)
 
 
-def first_update_kernel(p0, p2, p1, p3, w_hbm, o_ref, w, whole, sems):
-    index = 2 * (1 - (lax.axis_index("ctx") & 1))
-    (cw,) = copies([(w_hbm.at[0, index], w)], sems)
+def first_update_kernel(p0, p1, p2, p3, w, o_ref, whole):
+    take_pieces((p0, p1, p2, p3), whole, PLANS["A"])
+    (x,) = orthogonalize(whole[...])
+    o_ref[...] = updated(w[...], x)
+
+
+def core():
+    return lax.axis_index("ctx") & 1
+
+
+def pair_update_kernel(p0, p2, p1, p3, w1, w3, o_ref, whole):
     pieces = (p0, p1, p2, p3)
 
-    @pl.when(index == 2)
-    def _():
-        take_pieces(pieces, whole, PLANS["A"])
-
-    @pl.when(index == 0)
+    @pl.when(core() == 0)
     def _():
         take_pieces(pieces, whole, PLANS["B"])
 
-    x = orthogonalize(whole[...])
-    cw.wait()
-    o_ref[...] = updated(w[...], x)
-
-
-def last_update_kernel(p0, p1, p2, p3, w_hbm, mine, theirs, o_hbm, w, new, whole, sems):
-    index = 2 * (1 - (lax.axis_index("ctx") & 1))
-    cw, cm, ct = copies(
-        [(w_hbm.at[0, 1], w), (mine, o_hbm.at[0, index]), (theirs, o_hbm.at[0, 2 - index])], sems
-    )
-    take_pieces((p0, p1, p2, p3), whole, PLANS["C"])
-    x = orthogonalize(whole[...])
-    cw.wait()
-    new[...] = updated(w[...], x)
-    cn = pltpu.make_async_copy(new, o_hbm.at[0, 1], sems.at[3])
-    cn.start()
-    cm.wait()
-    ct.wait()
-    cn.wait()
-
-
-def read_kernel(w_hbm, *refs):
-    count = (len(refs) - 4) // 2
-    queries, reads, (w1, w3, w2, sems) = refs[:count], refs[count : 2 * count], refs[2 * count :]
-    made = copies([(w_hbm.at[0, 0], w1), (w_hbm.at[0, 1], w3), (w_hbm.at[0, 2], w2)], sems)
+    @pl.when(core() == 1)
+    def _():
+        take_pieces(pieces, whole, PLANS["C"])
+
+    (x,) = orthogonalize(whole[...])
+    o_ref[...] = updated(jnp.where(core() == 0, w1[...], w3[...]), x)
+
+
+def last_kernel(theirs, partial, o_hbm, sems):
+    del partial
+    (copy,) = copies([(theirs, o_hbm.at[0, 1 - core()])], sems)
+    copy.wait()
+
+
+def read_kernel(heads, gate_hbm, gain_hbm, w1, w3, w2, *refs):
+    gate, gain, sems = refs[2 * heads :]
+    made = copies([(gate_hbm, gate), (gain_hbm, gain)], sems)
     scale = w1.shape[-1] ** (-0.5)
-    for copy in made:
-        copy.wait()
-    for q, out in zip(queries, reads):
+    for q, out in zip(refs[:heads], refs[heads : 2 * heads]):
         rows = q[...]
         r1 = dot(rows, w1[...]) * scale
         r3 = dot(rows, w3[...]) * scale
         hq = (r1 * jax.nn.sigmoid(r1) * r3).astype(BF)
         out[...] = (dot(hq, w2[...]) * scale).astype(BF)
-
-
-def norm_kernel(heads, gate, gain, *refs):
-    reads, out = refs[:heads], refs[heads]
+    for copy in made:
+        copy.wait()
+
+
+def norm_kernel(heads, gate, gain, mine, two, *refs):
+    reads, (out, o_hbm, sems) = refs[:heads], refs[heads:]
+    made = copies([(mine, o_hbm.at[0, core()]), (two, o_hbm.at[0, 2])], sems)
     width = reads[0].shape[-1]
     me = lax.axis_index("head")
     for r, read in enumerate(reads):
@@ -191,12 +211,13 @@
         out[:, pl.ds(at, width)] = (
             x * lax.rsqrt(mean + 1e-06) * gain[:, pl.ds(at, width)] * (g * jax.nn.sigmoid(g))
         ).astype(BF)
+    for copy in made:
+        copy.wait()
 
 
 def local(ctx, heads, keys, values, rates, queries, fast_weights, gate, gain):
     tok, width = keys.shape
     bits = range(ctx.bit_length() - 1)
-    core = lax.axis_index("ctx") & 1
     piece = jax.ShapeDtypeStruct((width // 4, width), BF)
     matrix = jax.ShapeDtypeStruct((width, width), BF)
     mat = lambda dtype: pltpu.VMEM((width, width), dtype)
@@ -223,22 +244,22 @@
         functools.partial(grad_two_kernel, heads), 14,
         out_shape=[piece] * 4
         + [jax.ShapeDtypeStruct((tok, width), d) for d in (F32, F32, BF)]
+        + [jax.ShapeDtypeStruct((tok, width), BF)]
+        + [matrix] * 3
         + [jax.ShapeDtypeStruct((queries.shape[0], width), BF)] * heads,
         in_specs=[HBM] * 5,
-        out_specs=[VM] * (7 + heads),
-        scratch_shapes=[
-            tokens(BF), tokens(BF), pltpu.VMEM(rates.shape, F32), mat(BF), mat(BF), mat(BF), sems(5 + heads)
-        ],
+        out_specs=[VM] * (11 + heads),
+        scratch_shapes=[tokens(BF), pltpu.VMEM(rates.shape, F32), mat(BF), sems(6 + heads)],
     )(hbm(keys), hbm(values), hbm(rates), hbm(fast_weights), hbm(queries))
-    two, (g1, g3, go), columns = outs[:4], outs[4:7], outs[7:]
+    two, (g1, g3, go), (k, w1, w3, w2), columns = outs[:4], outs[4:7], outs[7:11], outs[11:]
     asked = [columns[0]] + [turn(columns[r], r) for r in range(1, heads)]
     outs = call(
         grad_one_kernel, 12,
         out_shape=[piece] * 8,
-        in_specs=[HBM, HBM, VM, VM, VM],
+        in_specs=[VM] * 5,
         out_specs=[VM] * 8,
-        scratch_shapes=[mat(BF), tokens(BF), tokens(BF), tokens(BF), mat(BF), sems(2)],
-    )(hbm(keys), hbm(fast_weights), g1, g3, go)
+        scratch_shapes=[tokens(BF), tokens(BF), mat(BF)],
+    )(k, w2, g1, g3, go)
     one, three = outs[:4], outs[4:]
 
     def add(x, y):
@@ -263,40 +284,57 @@
 
     two, one, three = summed("A", two), summed("B", one), summed("C", three)
 
-    give = [jnp.where(core == 0, o, t) for o, t in zip(one, two)]
-    keep = [jnp.where(core == 0, t, o) for o, t in zip(one, two)]
+    def gathered(own):
+        other = [swap(x, 0) for x in own]
+        return own[0], other[0], own[1], other[1]
+
+    new_two = call(
+        first_update_kernel, 10,
+        out_shape=matrix,
+        in_specs=[VM] * 5,
+        out_specs=VM,
+        scratch_shapes=[mat(BF)],
+    )(*gathered(two), w2)
+    give = [jnp.where(core() == 0, c, b) for b, c in zip(one, three)]
+    keep = [jnp.where(core() == 0, b, c) for b, c in zip(one, three)]
     got = [swap(x, 0) for x in give]
     mine = call(
-        first_update_kernel, 10,
+        pair_update_kernel, 10,
         out_shape=matrix,
-        in_specs=[VM] * 4 + [HBM],
+        in_specs=[VM] * 6,
         out_specs=VM,
-        scratch_shapes=[mat(BF), mat(BF), sems(1)],
-    )(*keep, *got, hbm(fast_weights))
+        scratch_shapes=[mat(BF)],
+    )(*keep, *got, w1, w3)
     theirs = swap(mine, 0)
-    others = [swap(x, 0) for x in three]
+
+    gains = gain.reshape(1, -1)
+    *reads, gate_here, gain_here = call(
+        functools.partial(read_kernel, heads), 12,
+        out_shape=[jax.ShapeDtypeStruct(x.shape, BF) for x in asked]
+        + [jax.ShapeDtypeStruct(x.shape, x.dtype) for x in (gate, gains)],
+        in_specs=[HBM] * 2 + [VM] * (3 + heads),
+        out_specs=[VM] * (heads + 2),
+        scratch_shapes=[sems(2)],
+    )(hbm(gate), hbm(gains), w1, w3, w2, *asked)
+    back = [reads[0]] + [turn(reads[r], heads - r) for r in range(1, heads)]
+    layer_out, new_weights = call(
+        functools.partial(norm_kernel, heads), 8,
+        out_shape=[
+            jax.ShapeDtypeStruct(queries.shape, BF),
+            jax.ShapeDtypeStruct(fast_weights.shape, BF),
+        ],
+        in_specs=[VM] * (4 + heads),
+        out_specs=[VM, HBM],
+        scratch_shapes=[sems(2)],
+    )(gate_here, gain_here, mine, new_two, *back)
     new_weights = call(
-        last_update_kernel, 10,
+        last_kernel, 4,
         out_shape=jax.ShapeDtypeStruct(fast_weights.shape, BF),
-        in_specs=[VM] * 4 + [HBM, ANY, ANY],
+        in_specs=[VM, HBM],
         out_specs=HBM,
-        scratch_shapes=[mat(BF), mat(BF), mat(BF), sems(4)],
-    )(three[0], others[0], three[1], others[1], hbm(fast_weights), mine, theirs)
-
-    reads = call(
-        read_kernel, 12,
-        out_shape=[jax.ShapeDtypeStruct(x.shape, BF) for x in asked],
-        in_specs=[HBM] + [VM] * heads,
-        out_specs=[VM] * heads,
-        scratch_shapes=[mat(BF)] * 3 + [sems(3)],
-    )(hbm(fast_weights), *asked)
-    back = [reads[0]] + [turn(reads[r], heads - r) for r in range(1, heads)]
-    layer_out = call(
-        functools.partial(norm_kernel, heads), 8,
-        out_shape=jax.ShapeDtypeStruct(queries.shape, BF),
-        in_specs=[VM] * (2 + heads),
-        out_specs=VM,
-    )(gate, gain.reshape(1, -1), *back)
+        scratch_shapes=[sems(1)],
+        input_output_aliases={1: 0},
+    )(theirs, new_weights)
     return layer_out, new_weights
 
 

time: 72.7 us -> 70.4 us (0.968)
  waiting for transfers between devices: 25.2 us -> 17.4 us
  other arithmetic: 0.5 us -> 5.01 us
  starting transfers between devices: 24.4 us -> 26.4 us
  Pallas kernels: 21.4 us -> 20.3 us
    ppermute x24 -> x25, waiting for transfers between devices: 22.7 us -> 17.4 us  [swap(): return lax.ppermute(x, 'ctx', [(i, i ^ 1 << bit) for i in range(ctx)])]
    convert_element_type x11, other arithmetic: 0.39 us -> 4.89 us  [add(): return (x.astype(F32) + y.astype(F32)).astype(BF)]
    ppermute x24 -> x25, starting transfers between devices: 20.9 us -> 24.3 us  [swap(): return lax.ppermute(x, 'ctx', [(i, i ^ 1 << bit) for i in range(ctx)])]
    ppermute x2, waiting for transfers between devices: 2.47 us -> 0.01 us  [turn(): return lax.ppermute(x, 'head', [(i, (i + r) % heads) for i in range(heads)])]
    ppermute x2, starting transfers between devices: 3.51 us -> 2.1 us  [turn(): return lax.ppermute(x, 'head', [(i, (i + r) % heads) for i in range(heads)])]
    pallas_call x6 -> x7, Pallas kernels: 21.4 us -> 20.3 us  [run(): pl.pallas_call(kernel, compiler_params=pltpu.CompilerParams(vmem_limit_by...]
  transfers between devices with their start and end apart: 26 -> 27, of which waited for: 10 -> 12; matrix products, arithmetic and copies ran while one was open for 1% -> 7% of each run, Pallas kernels for 17% -> 21%
where the time goes in v3:
time: 70.4 us; the launch traced here: 70.2 us
  starting transfers between devices  26.4 us (38%)
  Pallas kernels  20.3 us (29%)
  waiting for transfers between devices  17.4 us (25%)
  other arithmetic  5.01 us (7%)
  between operations  1 us (1%)
    ppermute x25, starting transfers between devices, swap(): return lax.ppermute(x, 'ctx', [(i, i ^ 1 << bit) for i in range(ctx)])  24.3 us
    pallas_call x7, Pallas kernels, run(): pl.pallas_call(kernel, compiler_params=pltpu.CompilerParams(vmem_limit_by...  20.3 us
    ppermute x25, waiting for transfers between devices, swap(): return lax.ppermute(x, 'ctx', [(i, i ^ 1 << bit) for i in range(ctx)])  17.4 us
    convert_element_type x11, other arithmetic, add(): return (x.astype(F32) + y.astype(F32)).astype(BF)  4.89 us
    ppermute x2, starting transfers between devices, turn(): return lax.ppermute(x, 'head', [(i, (i + r) % heads) for i in range(heads)])  2.1 us
  transfers between devices with their start and end apart: 27, of which 12 were waited for; matrix products, arithmetic and copies ran while one was open for 7% of the time, Pallas kernels for 21%

profile of v3, /device:TPU:0, one launch (start us, length us, event | category | flops | bytes accessed | tf_op | source)
XLA Modules:
  0.0 70.2 jit_solution(15444332117905572212)
XLA Ops:
  0.6 3.0 %shard_map.86 = (bf16[128,512]{1,0:T(8,128)(2,1)S(1)}, bf16[128,512]{1,0:T(8,128)(2,1)S(1)}, bf16[128,512]{1,0:T(8,128)(2,1)S(1)}, bf16[128,512]{1,0:T(8,128)(2,...) custom-call(bf16[512,512]{1,0:T(8,128)(2,1)} %k_hbm.1, ...), custom_call_target="tpu_custom_call" | custom-call | tf_op jit(solution)/shard_map/pallas_call | solution.py:231
  3.6 1.9 %shard_map.88 = (bf16[128,512]{1,0:T(8,128)(2,1)S(1)}, bf16[128,512]{1,0:T(8,128)(2,1)S(1)}, bf16[128,512]{1,0:T(8,128)(2,1)S(1)}, bf16[128,512]{1,0:T(8,128)(2,...) custom-call(bf16[512,512]{1,0:T(8,128)(2,1)S(1)} %get-tuple-element., ...), custom_call_target="tpu_custom_call" | custom-call | tf_op jit(solution)/shard_map/pallas_call | solution.py:231
  5.5 0.5 collective-permute-start.2
  6.0 0.0 collective-permute-start.17
  6.0 0.5 collective-permute-start.16
  6.5 0.0 collective-permute-start.8
  6.5 0.5 collective-permute-start.7
  7.0 0.3 collective-permute-done.2
  7.3 0.4 collective-permute-start.1
  7.7 0.9 %add_convert_fusion.9 = bf16[128,512]{1,0:T(8,128)(2,1)S(1)} fusion(bf16[128,512]{1,0:T(8,128)(2,1)} %collective-permute-done.2, bf16[128,512]{1,0:T(8,128)(2,1)S(1)} %get-tuple-element.42), kind=kLoop, calls=%fused_computation.9 | loop fusion | flops 262144 | bytes 393216 | tf_op jit(solution)/shard_map/convert_element_type | solution.py:266
  8.6 0.0 collective-permute-done.8
  8.6 2.8 %collective-permute-start.3 = (bf16[128,512]{1,0:T(8,128)(2,1)S(1)}, bf16[128,512]{1,0:T(8,128)(2,1)S(1)}, u32[]{:S(2)}, u32[]{:S(2)}) collective-permute-start(bf16[128,512]{1,0:T(8,128)(2,1)S(1)} %add_convert_fusion.9), channel_id=1, source_target_pairs={{0,8},{2,10},{4,12},{6,14},{8,0},{10,2},{12,4},{14,6},{16,24},{18,... | collective-permute-start | bytes 393224 | tf_op jit(solution)/shard_map/ppermute | solution.py:238
  11.4 0.9 %add_convert_fusion.6 = bf16[128,512]{1,0:T(8,128)(2,1)S(1)} fusion(bf16[128,512]{1,0:T(8,128)(2,1)} %collective-permute-done.8, bf16[128,512]{1,0:T(8,128)(2,1)S(1)} %get-tuple-element.46), kind=kLoop, calls=%fused_computation.6 | loop fusion | flops 262144 | bytes 393216 | tf_op jit(solution)/shard_map/convert_element_type | solution.py:266
  12.3 0.0 collective-permute-done.1
  12.3 1.6 %collective-permute-start.9 = (bf16[128,512]{1,0:T(8,128)(2,1)S(1)}, bf16[128,512]{1,0:T(8,128)(2,1)S(1)}, u32[]{:S(2)}, u32[]{:S(2)}) collective-permute-start(bf16[128,512]{1,0:T(8,128)(2,1)S(1)} %add_convert_fusion.6), channel_id=1, source_target_pairs={{0,4},{2,6},{4,0},{6,2},{8,12},{10,14},{12,8},{14,10},{16,20},{18,... | collective-permute-start | bytes 393224 | tf_op jit(solution)/shard_map/ppermute | solution.py:238
  13.9 1.5 %collective-permute-done.3 = bf16[128,512]{1,0:T(8,128)(2,1)S(1)} collective-permute-done((bf16[128,512]{1,0:T(8,128)(2,1)S(1)}, bf16[128,512]{1,0:T(8,128)(2,1)S(1)}, u32[]{:S(2)}, u32[]{:S(2)}) %collective-permute-start.3) | collective-permute-done | bytes 131104 | tf_op jit(solution)/shard_map/ppermute | solution.py:238
  15.4 0.1 add_convert_fusion.8
  15.5 1.7 %collective-permute-start.4 = (bf16[64,512]{1,0:T(8,128)(2,1)S(1)}, bf16[64,512]{1,0:T(8,128)(2,1)S(1)}, u32[]{:S(2)}, u32[]{:S(2)}) collective-permute-start(bf16[64,512]{1,0:T(8,128)(2,1)S(1)} %slice.17), channel_id=1, source_target_pairs={{0,4},{2,6},{4,0},{6,2},{8,12},{10,14},{12,8},{14,10},{16,20},{18,... | collective-permute-start | bytes 196616 | tf_op jit(solution)/shard_map/ppermute | solution.py:238
  17.2 0.0 collective-permute-done.7
  17.2 0.7 collective-permute-done.9
  17.9 1.0 %add_convert_fusion.5 = bf16[128,512]{1,0:T(8,128)(2,1)S(1)} fusion(bf16[128,512]{1,0:T(8,128)(2,1)S(1)} %collective-permute-done.9, bf16[128,512]{1,0:T(8,128)(2,1)} %collective-permute-done.7, bf16[128,512]{1,0:T(8,128)(2,1)S(1)} %get-tuple-element.44), kind=kLoop, calls=%fused_computation.5 | loop fusion | flops 524288 | bytes 524288 | tf_op jit(solution)/shard_map/convert_element_type | solution.py:266
  18.8 1.0 %collective-permute-start.10 = (bf16[128,512]{1,0:T(8,128)(2,1)S(1)}, bf16[128,512]{1,0:T(8,128)(2,1)S(1)}, u32[]{:S(2)}, u32[]{:S(2)}) collective-permute-start(bf16[128,512]{1,0:T(8,128)(2,1)S(1)} %add_convert_fusion.5), channel_id=1, source_target_pairs={{0,8},{2,10},{4,12},{6,14},{8,0},{10,2},{12,4},{14,6},{16,24},{18,... | collective-permute-start | bytes 393224 | tf_op jit(solution)/shard_map/ppermute | solution.py:238
  19.8 0.0 collective-permute-done.4
  19.8 2.8 %collective-permute-start.5 = (bf16[64,512]{1,0:T(8,128)(2,1)S(1)}, bf16[64,512]{1,0:T(8,128)(2,1)S(1)}, u32[]{:S(2)}, u32[]{:S(2)}) collective-permute-start(bf16[64,512]{1,0:T(8,128)(2,1)S(1)} %add_convert_fusion.14), channel_id=1, source_target_pairs={{0,16},{2,18},{4,20},{6,22},{8,24},{10,26},{12,28},{14,30},{16,0},... | collective-permute-start | bytes 196616 | tf_op jit(solution)/shard_map/ppermute | solution.py:238
  22.7 1.8 %collective-permute-done.10 = bf16[128,512]{1,0:T(8,128)(2,1)S(1)} collective-permute-done((bf16[128,512]{1,0:T(8,128)(2,1)S(1)}, bf16[128,512]{1,0:T(8,128)(2,1)S(1)}, u32[]{:S(2)}, u32[]{:S(2)}) %collective-permute-start.10) | collective-permute-done | bytes 131104 | tf_op jit(solution)/shard_map/ppermute | solution.py:238
  24.5 2.8 %collective-permute-start.11 = (bf16[128,512]{1,0:T(8,128)(2,1)S(1)}, bf16[128,512]{1,0:T(8,128)(2,1)S(1)}, u32[]{:S(2)}, u32[]{:S(2)}) collective-permute-start(bf16[128,512]{1,0:T(8,128)(2,1)S(1)} %add_convert_fusion.4), channel_id=1, source_target_pairs={{0,16},{2,18},{4,20},{6,22},{8,24},{10,26},{12,28},{14,30},{16,0},... | collective-permute-start | bytes 393224 | tf_op jit(solution)/shard_map/ppermute | solution.py:238
  27.3 0.0 collective-permute-done.5
  27.3 2.0 %collective-permute-start.6 = (bf16[64,512]{1,0:T(8,128)(2,1)S(1)}, bf16[64,512]{1,0:T(8,128)(2,1)S(1)}, u32[]{:S(2)}, u32[]{:S(2)}) collective-permute-start(bf16[64,512]{1,0:T(8,128)(2,1)S(1)} %add_convert_fusion.13), channel_id=1, source_target_pairs={{0,4},{2,6},{4,0},{6,2},{8,12},{10,14},{12,8},{14,10},{16,20},{18,... | collective-permute-start | bytes 196616 | tf_op jit(solution)/shard_map/ppermute | solution.py:238
  29.3 0.0 collective-permute-done.17
  29.3 0.9 %add_convert_fusion.1 = bf16[128,512]{1,0:T(8,128)(2,1)S(1)} fusion(bf16[128,512]{1,0:T(8,128)(2,1)} %collective-permute-done.17, bf16[128,512]{1,0:T(8,128)(2,1)S(1)} %get-tuple-element.50), kind=kLoop, calls=%fused_computation.1 | loop fusion | flops 262144 | bytes 393216 | tf_op jit(solution)/shard_map/convert_element_type | solution.py:266
  30.3 0.2 collective-permute-start.18
  30.4 1.2 %collective-permute-done.6 = bf16[64,512]{1,0:T(8,128)(2,1)S(1)} collective-permute-done((bf16[64,512]{1,0:T(8,128)(2,1)S(1)}, bf16[64,512]{1,0:T(8,128)(2,1)S(1)}, u32[]{:S(2)}, u32[]{:S(2)}) %collective-permute-start.6) | collective-permute-done | bytes 65568 | tf_op jit(solution)/shard_map/ppermute | solution.py:238
  31.7 0.2 collective-permute-done.11
  31.9 0.1 broadcast_select_fusion.1
  31.9 2.0 %collective-permute-start.13 = (bf16[128,512]{1,0:T(8,128)(2,1)S(1)}, bf16[128,512]{1,0:T(8,128)(2,1)S(1)}, u32[]{:S(2)}, u32[]{:S(2)}) collective-permute-start(bf16[128,512]{1,0:T(8,128)(2,1)S(1)} %get-tuple-element.57), channel_id=1, source_target_pairs={{0,4},{2,6},{4,0},{6,2},{8,12},{10,14},{12,8},{14,10},{16,20},{18,... | collective-permute-start | bytes 393224 | tf_op jit(solution)/shard_map/ppermute | solution.py:238
  34.0 1.5 %collective-permute-start.12 = (bf16[128,512]{1,0:T(8,128)(2,1)S(1)}, bf16[128,512]{1,0:T(8,128)(2,1)S(1)}, u32[]{:S(2)}, u32[]{:S(2)}) collective-permute-start(bf16[128,512]{1,0:T(8,128)(2,1)S(1)} %get-tuple-element.60), channel_id=1, source_target_pairs={{0,8},{2,10},{4,12},{6,14},{8,0},{10,2},{12,4},{14,6},{16,24},{18,... | collective-permute-start | bytes 393224 | tf_op jit(solution)/shard_map/ppermute | solution.py:238
  35.4 0.0 collective-permute-done.16
  35.4 1.2 %collective-permute-done.18 = bf16[128,512]{1,0:T(8,128)(2,1)S(1)} collective-permute-done((bf16[128,512]{1,0:T(8,128)(2,1)S(1)}, bf16[128,512]{1,0:T(8,128)(2,1)S(1)}, u32[]{:S(2)}, u32[]{:S(2)}) %collective-permute-start.18) | collective-permute-done | bytes 131104 | tf_op jit(solution)/shard_map/ppermute | solution.py:238
  36.7 1.0 %add_convert_fusion = bf16[128,512]{1,0:T(8,128)(2,1)S(1)} fusion(bf16[128,512]{1,0:T(8,128)(2,1)S(1)} %collective-permute-done.18, bf16[128,512]{1,0:T(8,128)(2,1)} %collective-permute-done.16, bf16[128,512]{1,0:T(8,128)(2,1)S(1)} %get-tuple-element.48), kind=kLoop, calls=%fused_computation | loop fusion | flops 524288 | bytes 524288 | tf_op jit(solution)/shard_map/convert_element_type | solution.py:266
  37.6 0.1 collective-permute-start.19
  37.7 0.1 collective-permute-start.14
  37.8 1.2 %collective-permute-done.12 = bf16[128,512]{1,0:T(8,128)(2,1)S(1)} collective-permute-done((bf16[128,512]{1,0:T(8,128)(2,1)S(1)}, bf16[128,512]{1,0:T(8,128)(2,1)S(1)}, u32[]{:S(2)}, u32[]{:S(2)}) %collective-permute-start.12) | collective-permute-done | bytes 131104 | tf_op jit(solution)/shard_map/ppermute | solution.py:238
  39.0 0.0 collective-permute-done.13
  39.1 0.1 collective-permute-start.15
  39.1 2.8 %collective-permute-done.19 = bf16[64,512]{1,0:T(8,128)(2,1)S(1)} collective-permute-done((bf16[64,512]{1,0:T(8,128)(2,1)S(1)}, bf16[64,512]{1,0:T(8,128)(2,1)S(1)}, u32[]{:S(2)}, u32[]{:S(2)}) %collective-permute-start.19) | collective-permute-done | bytes 65568 | tf_op jit(solution)/shard_map/ppermute | solution.py:238
  42.0 1.8 %collective-permute-start.20 = (bf16[64,512]{1,0:T(8,128)(2,1)S(1)}, bf16[64,512]{1,0:T(8,128)(2,1)S(1)}, u32[]{:S(2)}, u32[]{:S(2)}) collective-permute-start(bf16[64,512]{1,0:T(8,128)(2,1)S(1)} %add_convert_fusion.12), channel_id=1, source_target_pairs={{0,16},{2,18},{4,20},{6,22},{8,24},{10,26},{12,28},{14,30},{16,0},... | collective-permute-start | bytes 196616 | tf_op jit(solution)/shard_map/ppermute | solution.py:238
  43.8 1.5 %collective-permute-start = (bf16[256,512]{1,0:T(8,128)(2,1)S(1)}, bf16[256,512]{1,0:T(8,128)(2,1)S(1)}, u32[]{:S(2)}, u32[]{:S(2)}) collective-permute-start(bf16[256,512]{1,0:T(8,128)(2,1)S(1)} %get-tuple-element.33), channel_id=1, source_target_pairs={{0,1},{1,0},{2,3},{3,2},{4,5},{5,4},{6,7},{7,6},{8,9},{9,8},{10,11... | collective-permute-start | bytes 786440 | tf_op jit(solution)/shard_map/ppermute | solution.py:241
  45.3 5.5 %shard_map.89.mine = bf16[512,512]{1,0:T(8,128)(2,1)S(1)} custom-call(bf16[128,512]{1,0:T(8,128)(2,1)S(1)} %get-tuple-element.61.p0, bf16[128,512]{1,0:T(8,128)(2,1)S(1)} %get-tuple-element.59.p2, bf16[128,512]{1,0:T(8,128)(2,1)S(1)} %collective-permute-done.14.p1, bf16[128,512]{1,0:T(8,128)(2,1)S(1)} %collective-permute-done.15.p3, ...), custom_call_target="tpu_custom_call" | custom-call | tf_op jit(solution)/shard_map/pallas_call | solution.py:231
  50.8 0.1 collective-permute-start.26
  51.0 1.3 %collective-permute-start.21 = (bf16[64,512]{1,0:T(8,128)(2,1)S(1)}, bf16[64,512]{1,0:T(8,128)(2,1)S(1)}, u32[]{:S(2)}, u32[]{:S(2)}) collective-permute-start(bf16[64,512]{1,0:T(8,128)(2,1)S(1)} %add_convert_fusion.11), channel_id=1, source_target_pairs={{0,8},{2,10},{4,12},{6,14},{8,0},{10,2},{12,4},{14,6},{16,24},{18,... | collective-permute-start | bytes 196616 | tf_op jit(solution)/shard_map/ppermute | solution.py:238
  52.3 3.2 %collective-permute-done.21 = bf16[64,512]{1,0:T(8,128)(2,1)S(1)} collective-permute-done((bf16[64,512]{1,0:T(8,128)(2,1)S(1)}, bf16[64,512]{1,0:T(8,128)(2,1)S(1)}, u32[]{:S(2)}, u32[]{:S(2)}) %collective-permute-start.21) | collective-permute-done | bytes 65568 | tf_op jit(solution)/shard_map/ppermute | solution.py:238
  55.5 0.8 %collective-permute-start.23 = (bf16[128,512]{1,0:T(8,128)(2,1)S(1)}, bf16[128,512]{1,0:T(8,128)(2,1)S(1)}, u32[]{:S(2)}, u32[]{:S(2)}) collective-permute-start(bf16[128,512]{1,0:T(8,128)(2,1)S(1)} %pad_maximum_fusion.1.p0), channel_id=1, source_target_pairs={{0,4},{2,6},{4,0},{6,2},{8,12},{10,14},{12,8},{14,10},{16,20},{18,... | collective-permute-start | bytes 393224 | tf_op jit(solution)/shard_map/ppermute | solution.py:238
  56.3 0.0 collective-permute-done.refs_1_
  56.3 1.9 %shard_map.87 = (bf16[256,512]{1,0:T(8,128)(2,1)S(1)}, bf16[256,512]{1,0:T(8,128)(2,1)S(1)}, bf16[256,1024]{1,0:T(8,128)(2,1)S(1)}, f32[1,1024]{1,0:T(1,128)S(1)}) custom-call(bf16[256,1024]{1,0:T(8,128)(2,1)} %gate_hbm.1, f32[1,1024]{1,0:T(1,128)} %bitcast.1, bf16[512,512]{1,0:T(8,128)(2,1)S(1)} %get-tuple-element.29.w1, ...), custom_call_target="tpu_custom_call" | custom-call | tf_op jit(solution)/shard_map/pallas_call | solution.py:231
  58.2 0.6 collective-permute-start.25
  58.8 1.8 %collective-permute-done.23.p2 = bf16[128,512]{1,0:T(8,128)(2,1)S(1)} collective-permute-done((bf16[128,512]{1,0:T(8,128)(2,1)S(1)}, bf16[128,512]{1,0:T(8,128)(2,1)S(1)}, u32[]{:S(2)}, u32[]{:S(2)}) %collective-permute-start.23) | collective-permute-done | bytes 131104 | tf_op jit(solution)/shard_map/ppermute | solution.py:238
  60.6 0.0 collective-permute-start.24
  60.6 0.0 collective-permute-done.22.p1
  60.6 1.3 %collective-permute-done.24.p3 = bf16[128,512]{1,0:T(8,128)(2,1)S(1)} collective-permute-done((bf16[128,512]{1,0:T(8,128)(2,1)S(1)}, bf16[128,512]{1,0:T(8,128)(2,1)S(1)}, u32[]{:S(2)}, u32[]{:S(2)}) %collective-permute-start.24) | collective-permute-done | bytes 131104 | tf_op jit(solution)/shard_map/ppermute | solution.py:238
  62.0 5.4 %shard_map.90.two = bf16[512,512]{1,0:T(8,128)(2,1)S(1)} custom-call(bf16[128,512]{1,0:T(8,128)(2,1)S(1)} %pad_maximum_fusion.1.p0, bf16[128,512]{1,0:T(8,128)(2,1)S(1)} %collective-permute-done.22.p1, bf16[128,512]{1,0:T(8,128)(2,1)S(1)} %collective-permute-done.23.p2, bf16[128,512]{1,0:T(8,128)(2,1)S(1)} %collective-permute-done.24.p3, ...), custom_call_target="tpu_custom_call" | custom-call | tf_op jit(solution)/shard_map/pallas_call | solution.py:231
  67.3 0.0 collective-permute-done.25.refs_1_
  67.3 1.9 %shard_map.91 = (bf16[256,1024]{1,0:T(8,128)(2,1)}, bf16[1,3,512,512]{3,2,1,0:T(8,128)(2,1)}) custom-call(bf16[256,1024]{1,0:T(8,128)(2,1)S(1)} %get-tuple-element.34.gate, f32[1,1024]{1,0:T(1,128)S(1)} %get-tuple-element.35.gain, bf16[512,512]{1,0:T(8,128)(2,1)S(1)} %shard_map.89.mine, bf16[512,512]{1,0:T(8,128)(2,1)S(1)} %shard_map.90.two, ...), custom_call_target="tpu_custom_call" | custom-call | tf_op jit(solution)/shard_map/pallas_call | solution.py:231
  69.2 0.0 collective-permute-done.26.theirs
  69.2 0.8 %shard_map.92 = bf16[1,3,512,512]{3,2,1,0:T(8,128)(2,1)} custom-call(bf16[512,512]{1,0:T(8,128)(2,1)S(1)} %collective-permute-done.26.theirs, bf16[1,3,512,512]{3,2,1,0:T(8,128)(2,1)} %get-tuple-element.55.partial), custom_call_target="tpu_custom_call", output_to_operand_aliasing={{}: (1, {})} | custom-call | tf_op jit(solution)/shard_map/pallas_call | solution.py:231
  (14 shorter events, 0.2 us)
Async XLA Ops:
  5.5 1.8 %collective-permute-start.2 = (bf16[128,512]{1,0:T(8,128)(2,1)}, bf16[128,512]{1,0:T(8,128)(2,1)}, u32[]{:S(2)}, u32[]{:S(2)}) collective-permute-start(bf16[128,512]{1,0:T(8,128)(2,1)} %get-tuple-element.43), channel_id=1, source_target_pairs={{0,2},{2,0},{4,6},{6,4},{8,10},{10,8},{12,14},{14,12},{16,18},{18,... | collective-permute-start | bytes 393224 | tf_op jit(solution)/shard_map/ppermute | solution.py:238
  6.0 23.4 %collective-permute-start.17 = (bf16[128,512]{1,0:T(8,128)(2,1)S(1)}, bf16[128,512]{1,0:T(8,128)(2,1)}, u32[]{:S(2)}, u32[]{:S(2)}) collective-permute-start(bf16[128,512]{1,0:T(8,128)(2,1)S(1)} %get-tuple-element.51), channel_id=1, source_target_pairs={{0,2},{2,0},{4,6},{6,4},{8,10},{10,8},{12,14},{14,12},{16,18},{18,... | collective-permute-start | bytes 393224 | tf_op jit(solution)/shard_map/ppermute | solution.py:238
  6.0 29.5 %collective-permute-start.16 = (bf16[128,512]{1,0:T(8,128)(2,1)S(1)}, bf16[128,512]{1,0:T(8,128)(2,1)}, u32[]{:S(2)}, u32[]{:S(2)}) collective-permute-start(bf16[128,512]{1,0:T(8,128)(2,1)S(1)} %get-tuple-element.49), channel_id=1, source_target_pairs={{0,2},{2,0},{4,6},{6,4},{8,10},{10,8},{12,14},{14,12},{16,18},{18,... | collective-permute-start | bytes 393224 | tf_op jit(solution)/shard_map/ppermute | solution.py:238
  6.5 2.1 %collective-permute-start.8 = (bf16[128,512]{1,0:T(8,128)(2,1)S(1)}, bf16[128,512]{1,0:T(8,128)(2,1)}, u32[]{:S(2)}, u32[]{:S(2)}) collective-permute-start(bf16[128,512]{1,0:T(8,128)(2,1)S(1)} %get-tuple-element.47), channel_id=1, source_target_pairs={{0,2},{2,0},{4,6},{6,4},{8,10},{10,8},{12,14},{14,12},{16,18},{18,... | collective-permute-start | bytes 393224 | tf_op jit(solution)/shard_map/ppermute | solution.py:238
  6.5 10.7 %collective-permute-start.7 = (bf16[128,512]{1,0:T(8,128)(2,1)S(1)}, bf16[128,512]{1,0:T(8,128)(2,1)}, u32[]{:S(2)}, u32[]{:S(2)}) collective-permute-start(bf16[128,512]{1,0:T(8,128)(2,1)S(1)} %get-tuple-element.45), channel_id=1, source_target_pairs={{0,2},{2,0},{4,6},{6,4},{8,10},{10,8},{12,14},{14,12},{16,18},{18,... | collective-permute-start | bytes 393224 | tf_op jit(solution)/shard_map/ppermute | solution.py:238
  7.3 5.0 %collective-permute-start.1 = (bf16[128,512]{1,0:T(8,128)(2,1)S(1)}, bf16[128,512]{1,0:T(8,128)(2,1)S(1)}, u32[]{:S(2)}, u32[]{:S(2)}) collective-permute-start(bf16[128,512]{1,0:T(8,128)(2,1)S(1)} %get-tuple-element.41), channel_id=1, source_target_pairs={{0,2},{2,0},{4,6},{6,4},{8,10},{10,8},{12,14},{14,12},{16,18},{18,... | collective-permute-start | bytes 393224 | tf_op jit(solution)/shard_map/ppermute | solution.py:238
  8.6 6.8 %collective-permute-start.3 = (bf16[128,512]{1,0:T(8,128)(2,1)S(1)}, bf16[128,512]{1,0:T(8,128)(2,1)S(1)}, u32[]{:S(2)}, u32[]{:S(2)}) collective-permute-start(bf16[128,512]{1,0:T(8,128)(2,1)S(1)} %add_convert_fusion.9), channel_id=1, source_target_pairs={{0,8},{2,10},{4,12},{6,14},{8,0},{10,2},{12,4},{14,6},{16,24},{18,... | collective-permute-start | bytes 393224 | tf_op jit(solution)/shard_map/ppermute | solution.py:238
  12.3 5.5 %collective-permute-start.9 = (bf16[128,512]{1,0:T(8,128)(2,1)S(1)}, bf16[128,512]{1,0:T(8,128)(2,1)S(1)}, u32[]{:S(2)}, u32[]{:S(2)}) collective-permute-start(bf16[128,512]{1,0:T(8,128)(2,1)S(1)} %add_convert_fusion.6), channel_id=1, source_target_pairs={{0,4},{2,6},{4,0},{6,2},{8,12},{10,14},{12,8},{14,10},{16,20},{18,... | collective-permute-start | bytes 393224 | tf_op jit(solution)/shard_map/ppermute | solution.py:238
  15.5 4.3 %collective-permute-start.4 = (bf16[64,512]{1,0:T(8,128)(2,1)S(1)}, bf16[64,512]{1,0:T(8,128)(2,1)S(1)}, u32[]{:S(2)}, u32[]{:S(2)}) collective-permute-start(bf16[64,512]{1,0:T(8,128)(2,1)S(1)} %slice.17), channel_id=1, source_target_pairs={{0,4},{2,6},{4,0},{6,2},{8,12},{10,14},{12,8},{14,10},{16,20},{18,... | collective-permute-start | bytes 196616 | tf_op jit(solution)/shard_map/ppermute | solution.py:238
  18.8 5.6 %collective-permute-start.10 = (bf16[128,512]{1,0:T(8,128)(2,1)S(1)}, bf16[128,512]{1,0:T(8,128)(2,1)S(1)}, u32[]{:S(2)}, u32[]{:S(2)}) collective-permute-start(bf16[128,512]{1,0:T(8,128)(2,1)S(1)} %add_convert_fusion.5), channel_id=1, source_target_pairs={{0,8},{2,10},{4,12},{6,14},{8,0},{10,2},{12,4},{14,6},{16,24},{18,... | collective-permute-start | bytes 393224 | tf_op jit(solution)/shard_map/ppermute | solution.py:238
  19.8 7.5 %collective-permute-start.5 = (bf16[64,512]{1,0:T(8,128)(2,1)S(1)}, bf16[64,512]{1,0:T(8,128)(2,1)S(1)}, u32[]{:S(2)}, u32[]{:S(2)}) collective-permute-start(bf16[64,512]{1,0:T(8,128)(2,1)S(1)} %add_convert_fusion.14), channel_id=1, source_target_pairs={{0,16},{2,18},{4,20},{6,22},{8,24},{10,26},{12,28},{14,30},{16,0},... | collective-permute-start | bytes 196616 | tf_op jit(solution)/shard_map/ppermute | solution.py:238
  24.5 7.4 %collective-permute-start.11 = (bf16[128,512]{1,0:T(8,128)(2,1)S(1)}, bf16[128,512]{1,0:T(8,128)(2,1)S(1)}, u32[]{:S(2)}, u32[]{:S(2)}) collective-permute-start(bf16[128,512]{1,0:T(8,128)(2,1)S(1)} %add_convert_fusion.4), channel_id=1, source_target_pairs={{0,16},{2,18},{4,20},{6,22},{8,24},{10,26},{12,28},{14,30},{16,0},... | collective-permute-start | bytes 393224 | tf_op jit(solution)/shard_map/ppermute | solution.py:238
  27.3 4.3 %collective-permute-start.6 = (bf16[64,512]{1,0:T(8,128)(2,1)S(1)}, bf16[64,512]{1,0:T(8,128)(2,1)S(1)}, u32[]{:S(2)}, u32[]{:S(2)}) collective-permute-start(bf16[64,512]{1,0:T(8,128)(2,1)S(1)} %add_convert_fusion.13), channel_id=1, source_target_pairs={{0,4},{2,6},{4,0},{6,2},{8,12},{10,14},{12,8},{14,10},{16,20},{18,... | collective-permute-start | bytes 196616 | tf_op jit(solution)/shard_map/ppermute | solution.py:238
  30.3 6.4 %collective-permute-start.18 = (bf16[128,512]{1,0:T(8,128)(2,1)S(1)}, bf16[128,512]{1,0:T(8,128)(2,1)S(1)}, u32[]{:S(2)}, u32[]{:S(2)}) collective-permute-start(bf16[128,512]{1,0:T(8,128)(2,1)S(1)} %add_convert_fusion.1), channel_id=1, source_target_pairs={{0,4},{2,6},{4,0},{6,2},{8,12},{10,14},{12,8},{14,10},{16,20},{18,... | collective-permute-start | bytes 393224 | tf_op jit(solution)/shard_map/ppermute | solution.py:238
  31.9 7.1 %collective-permute-start.13 = (bf16[128,512]{1,0:T(8,128)(2,1)S(1)}, bf16[128,512]{1,0:T(8,128)(2,1)S(1)}, u32[]{:S(2)}, u32[]{:S(2)}) collective-permute-start(bf16[128,512]{1,0:T(8,128)(2,1)S(1)} %get-tuple-element.57), channel_id=1, source_target_pairs={{0,4},{2,6},{4,0},{6,2},{8,12},{10,14},{12,8},{14,10},{16,20},{18,... | collective-permute-start | bytes 393224 | tf_op jit(solution)/shard_map/ppermute | solution.py:238
  34.0 5.1 %collective-permute-start.12 = (bf16[128,512]{1,0:T(8,128)(2,1)S(1)}, bf16[128,512]{1,0:T(8,128)(2,1)S(1)}, u32[]{:S(2)}, u32[]{:S(2)}) collective-permute-start(bf16[128,512]{1,0:T(8,128)(2,1)S(1)} %get-tuple-element.60), channel_id=1, source_target_pairs={{0,8},{2,10},{4,12},{6,14},{8,0},{10,2},{12,4},{14,6},{16,24},{18,... | collective-permute-start | bytes 393224 | tf_op jit(solution)/shard_map/ppermute | solution.py:238
  37.6 4.3 %collective-permute-start.19 = (bf16[64,512]{1,0:T(8,128)(2,1)S(1)}, bf16[64,512]{1,0:T(8,128)(2,1)S(1)}, u32[]{:S(2)}, u32[]{:S(2)}) collective-permute-start(bf16[64,512]{1,0:T(8,128)(2,1)S(1)} %slice.19), channel_id=1, source_target_pairs={{0,8},{2,10},{4,12},{6,14},{8,0},{10,2},{12,4},{14,6},{16,24},{18,... | collective-permute-start | bytes 196616 | tf_op jit(solution)/shard_map/ppermute | solution.py:238
  37.7 7.6 %collective-permute-start.14 = (bf16[128,512]{1,0:T(8,128)(2,1)S(1)}, bf16[128,512]{1,0:T(8,128)(2,1)S(1)}, u32[]{:S(2)}, u32[]{:S(2)}) collective-permute-start(bf16[128,512]{1,0:T(8,128)(2,1)S(1)} %get-tuple-element.56), channel_id=1, source_target_pairs={{0,2},{2,0},{4,6},{6,4},{8,10},{10,8},{12,14},{14,12},{16,18},{18,... | collective-permute-start | bytes 393224 | tf_op jit(solution)/shard_map/ppermute | solution.py:238
  39.1 6.2 %collective-permute-start.15 = (bf16[128,512]{1,0:T(8,128)(2,1)S(1)}, bf16[128,512]{1,0:T(8,128)(2,1)S(1)}, u32[]{:S(2)}, u32[]{:S(2)}) collective-permute-start(bf16[128,512]{1,0:T(8,128)(2,1)S(1)} %get-tuple-element.58), channel_id=1, source_target_pairs={{0,2},{2,0},{4,6},{6,4},{8,10},{10,8},{12,14},{14,12},{16,18},{18,... | collective-permute-start | bytes 393224 | tf_op jit(solution)/shard_map/ppermute | solution.py:238
  42.0 8.9 %collective-permute-start.20 = (bf16[64,512]{1,0:T(8,128)(2,1)S(1)}, bf16[64,512]{1,0:T(8,128)(2,1)S(1)}, u32[]{:S(2)}, u32[]{:S(2)}) collective-permute-start(bf16[64,512]{1,0:T(8,128)(2,1)S(1)} %add_convert_fusion.12), channel_id=1, source_target_pairs={{0,16},{2,18},{4,20},{6,22},{8,24},{10,26},{12,28},{14,30},{16,0},... | collective-permute-start | bytes 196616 | tf_op jit(solution)/shard_map/ppermute | solution.py:238
  43.8 12.5 %collective-permute-start = (bf16[256,512]{1,0:T(8,128)(2,1)S(1)}, bf16[256,512]{1,0:T(8,128)(2,1)S(1)}, u32[]{:S(2)}, u32[]{:S(2)}) collective-permute-start(bf16[256,512]{1,0:T(8,128)(2,1)S(1)} %get-tuple-element.33), channel_id=1, source_target_pairs={{0,1},{1,0},{2,3},{3,2},{4,5},{5,4},{6,7},{7,6},{8,9},{9,8},{10,11... | collective-permute-start | bytes 786440 | tf_op jit(solution)/shard_map/ppermute | solution.py:241
  50.8 18.4 %collective-permute-start.26 = (bf16[512,512]{1,0:T(8,128)(2,1)S(1)}, bf16[512,512]{1,0:T(8,128)(2,1)S(1)}, u32[]{:S(2)}, u32[]{:S(2)}) collective-permute-start(bf16[512,512]{1,0:T(8,128)(2,1)S(1)} %shard_map.89.mine), channel_id=1, source_target_pairs={{0,2},{2,0},{4,6},{6,4},{8,10},{10,8},{12,14},{14,12},{16,18},{18,... | collective-permute-start | bytes 1572872 | tf_op jit(solution)/shard_map/ppermute | solution.py:238
  51.0 4.5 %collective-permute-start.21 = (bf16[64,512]{1,0:T(8,128)(2,1)S(1)}, bf16[64,512]{1,0:T(8,128)(2,1)S(1)}, u32[]{:S(2)}, u32[]{:S(2)}) collective-permute-start(bf16[64,512]{1,0:T(8,128)(2,1)S(1)} %add_convert_fusion.11), channel_id=1, source_target_pairs={{0,8},{2,10},{4,12},{6,14},{8,0},{10,2},{12,4},{14,6},{16,24},{18,... | collective-permute-start | bytes 196616 | tf_op jit(solution)/shard_map/ppermute | solution.py:238
  55.5 5.1 %collective-permute-start.23 = (bf16[128,512]{1,0:T(8,128)(2,1)S(1)}, bf16[128,512]{1,0:T(8,128)(2,1)S(1)}, u32[]{:S(2)}, u32[]{:S(2)}) collective-permute-start(bf16[128,512]{1,0:T(8,128)(2,1)S(1)} %pad_maximum_fusion.1.p0), channel_id=1, source_target_pairs={{0,4},{2,6},{4,0},{6,2},{8,12},{10,14},{12,8},{14,10},{16,20},{18,... | collective-permute-start | bytes 393224 | tf_op jit(solution)/shard_map/ppermute | solution.py:238
  58.2 9.1 %collective-permute-start.25 = (bf16[256,512]{1,0:T(8,128)(2,1)S(1)}, bf16[256,512]{1,0:T(8,128)(2,1)S(1)}, u32[]{:S(2)}, u32[]{:S(2)}) collective-permute-start(bf16[256,512]{1,0:T(8,128)(2,1)S(1)} %get-tuple-element.53), channel_id=1, source_target_pairs={{0,1},{1,0},{2,3},{3,2},{4,5},{5,4},{6,7},{7,6},{8,9},{9,8},{10,11... | collective-permute-start | bytes 786440 | tf_op jit(solution)/shard_map/ppermute | solution.py:241
  58.8 1.8 %collective-permute-start.22 = (bf16[128,512]{1,0:T(8,128)(2,1)S(1)}, bf16[128,512]{1,0:T(8,128)(2,1)S(1)}, u32[]{:S(2)}, u32[]{:S(2)}) collective-permute-start(bf16[128,512]{1,0:T(8,128)(2,1)S(1)} %pad_maximum_fusion.1.p0), channel_id=1, source_target_pairs={{0,2},{2,0},{4,6},{6,4},{8,10},{10,8},{12,14},{14,12},{16,18},{18,... | collective-permute-start | bytes 393224 | tf_op jit(solution)/shard_map/ppermute | solution.py:238
  60.6 1.3 %collective-permute-start.24 = (bf16[128,512]{1,0:T(8,128)(2,1)S(1)}, bf16[128,512]{1,0:T(8,128)(2,1)S(1)}, u32[]{:S(2)}, u32[]{:S(2)}) collective-permute-start(bf16[128,512]{1,0:T(8,128)(2,1)S(1)} %collective-permute-done.23.p2), channel_id=1, source_target_pairs={{0,2},{2,0},{4,6},{6,4},{8,10},{10,8},{12,14},{14,12},{16,18},{18,... | collective-permute-start | bytes 393224 | tf_op jit(solution)/shard_map/ppermute | solution.py:238

commit v4 on v3

--- a/solution.py
+++ b/solution.py
@@ -52,9 +52,11 @@
             yield r, pl.ds(e * rows, rows), pl.ds(at, rows)
 
 
-def put_pieces(whole, pieces, bits):
+def put_pieces(whole, halves, bits):
+    quarter = whole.shape[0] // 4
     for r, part, rows in blocks(whole, bits):
-        pieces[r][part, :] = whole[rows, :]
+        half = halves[r & 1].at[pl.ds((r >> 1) * quarter, quarter), :]
+        half[part, :] = whole[rows, :]
 
 
 def take_pieces(pieces, whole, bits):
@@ -62,50 +64,60 @@
         whole[rows, :] = pieces[r][part, :]
 
 
+def token_spans(tokens):
+    return [slice(0, tokens // 2), slice(tokens // 2, tokens)]
+
+
 def grad_two_kernel(heads, k_hbm, v_hbm, r_hbm, w_hbm, q_hbm, *refs):
-    pieces, (g1_ref, g3_ref, go_ref), (k, w1, w3, w2) = refs[:4], refs[4:7], refs[7:11]
-    asked = refs[11 : 11 + heads]
-    v, r_ref, whole, sems = refs[11 + heads :]
+    halves, (g1_ref, g3_ref, go_ref), (k, w2) = refs[:2], refs[2:5], refs[5:7]
+    asked = refs[7 : 7 + heads]
+    v, r_ref, w1, w3, whole, sems = refs[7 + heads :]
     width = w1.shape[-1]
     me = lax.axis_index("head")
     columns = []
     for r, out in enumerate(asked):
         at = pl.multiple_of(lax.rem(me + r, heads) * width, width)
         columns.append((q_hbm.at[:, pl.ds(at, width)], out))
-    ck, c1, c3, cv, cr, *cq = copies(
-        [(k_hbm, k), (w_hbm.at[0, 0], w1), (w_hbm.at[0, 1], w3), (v_hbm, v), (r_hbm, r_ref)]
-        + [(w_hbm.at[0, 2], w2)]
-        + columns,
-        sems,
+    ck, c1, c3, cv, cr = copies(
+        [(k_hbm, k), (w_hbm.at[0, 0], w1), (w_hbm.at[0, 1], w3), (v_hbm, v), (r_hbm, r_ref)], sems
     )
     scale = w1.shape[-1] ** (-0.5)
     ck.wait()
     c1.wait()
-    g1 = dot(k[...], w1[...]) * scale
-    g1_ref[...] = g1
+    later = copies([(w_hbm.at[0, 2], w2)] + columns, sems.at[pl.ds(5, 1 + heads)])
+    spans = token_spans(k.shape[0])
+    g1 = []
+    for rows in spans:
+        g1.append(dot(k[rows, :], w1[...]) * scale)
+        g1_ref[rows, :] = g1[-1]
     c3.wait()
-    g3 = dot(k[...], w3[...]) * scale
-    g3_ref[...] = g3
     cv.wait()
     cr.wait()
     rate = jnp.broadcast_to(r_ref[...], (128, r_ref.shape[1])).T[:, :1]
-    go = (-(rate * v[...].astype(F32))).astype(BF)
-    go_ref[...] = go
-    hidden = (g1 * jax.nn.sigmoid(g1) * g3).astype(BF)
-    whole[...] = (dot_tn(hidden, go) * scale).astype(BF)
-    put_pieces(whole, pieces, PLANS["A"])
-    for copy in cq:
+    total = None
+    for rows, one in zip(spans, g1):
+        three = dot(k[rows, :], w3[...]) * scale
+        g3_ref[rows, :] = three
+        go = (-(rate[rows, :] * v[rows, :].astype(F32))).astype(BF)
+        go_ref[rows, :] = go
+        hidden = (one * jax.nn.sigmoid(one) * three).astype(BF)
+        part = dot_tn(hidden, go)
+        total = part if total is None else total + part
+    whole[...] = (total * scale).astype(BF)
+    put_pieces(whole, halves, PLANS["A"])
+    for copy in later:
         copy.wait()
 
 
 def grad_one_kernel(k, w2, g1_ref, g3_ref, go_ref, *refs):
-    one, three, (dg1, dg3, whole) = refs[:4], refs[4:8], refs[8:]
+    one, three, (dg1, dg3, whole) = refs[:2], refs[2:4], refs[4:]
     scale = w2.shape[-1] ** (-0.5)
-    dh = dot_nt(go_ref[...], w2[...]) * scale
-    g1 = g1_ref[...]
-    sig = jax.nn.sigmoid(g1)
-    dg1[...] = (dh * g3_ref[...] * sig * (1.0 + g1 * (1.0 - sig))).astype(BF)
-    dg3[...] = (dh * (g1 * sig)).astype(BF)
+    for rows in token_spans(k.shape[0]):
+        dh = dot_nt(go_ref[rows, :], w2[...]) * scale
+        g1 = g1_ref[rows, :]
+        sig = jax.nn.sigmoid(g1)
+        dg1[rows, :] = (dh * g3_ref[rows, :] * sig * (1.0 + g1 * (1.0 - sig))).astype(BF)
+        dg3[rows, :] = (dh * (g1 * sig)).astype(BF)
     whole[...] = (dot_tn(k[...], dg1[...]) * scale).astype(BF)
     put_pieces(whole, one, PLANS["B"])
     whole[...] = (dot_tn(k[...], dg3[...]) * scale).astype(BF)
@@ -153,17 +165,22 @@
     return (weight.astype(F32) - step_size * x.astype(F32)).astype(BF)
 
 
-def first_update_kernel(p0, p1, p2, p3, w, o_ref, whole):
+def first_update_kernel(p0, p1, p2, p3, w_hbm, gate_hbm, gain_hbm, o_ref, gate, gain, w, whole, sems):
+    cw, *made = copies([(w_hbm.at[0, 2], w), (gate_hbm, gate), (gain_hbm, gain)], sems)
     take_pieces((p0, p1, p2, p3), whole, PLANS["A"])
     (x,) = orthogonalize(whole[...])
+    cw.wait()
     o_ref[...] = updated(w[...], x)
+    for copy in made:
+        copy.wait()
 
 
 def core():
     return lax.axis_index("ctx") & 1
 
 
-def pair_update_kernel(p0, p2, p1, p3, w1, w3, o_ref, whole):
+def pair_update_kernel(p0, p2, p1, p3, w_hbm, o_ref, w, whole, sems):
+    (cw,) = copies([(w_hbm.at[0, core()], w)], sems)
     pieces = (p0, p1, p2, p3)
 
     @pl.when(core() == 0)
@@ -175,7 +192,8 @@
         take_pieces(pieces, whole, PLANS["C"])
 
     (x,) = orthogonalize(whole[...])
-    o_ref[...] = updated(jnp.where(core() == 0, w1[...], w3[...]), x)
+    cw.wait()
+    o_ref[...] = updated(w[...], x)
 
 
 def last_kernel(theirs, partial, o_hbm, sems):
@@ -184,18 +202,18 @@
     copy.wait()
 
 
-def read_kernel(heads, gate_hbm, gain_hbm, w1, w3, w2, *refs):
-    gate, gain, sems = refs[2 * heads :]
-    made = copies([(gate_hbm, gate), (gain_hbm, gain)], sems)
+def read_kernel(heads, w_hbm, *refs):
+    queries, reads, (w1, w3, w2, sems) = refs[:heads], refs[heads : 2 * heads], refs[2 * heads :]
+    c1, c3, c2 = copies([(w_hbm.at[0, i], w) for i, w in enumerate((w1, w3, w2))], sems)
     scale = w1.shape[-1] ** (-0.5)
-    for q, out in zip(refs[:heads], refs[heads : 2 * heads]):
-        rows = q[...]
-        r1 = dot(rows, w1[...]) * scale
-        r3 = dot(rows, w3[...]) * scale
-        hq = (r1 * jax.nn.sigmoid(r1) * r3).astype(BF)
-        out[...] = (dot(hq, w2[...]) * scale).astype(BF)
-    for copy in made:
-        copy.wait()
+    c1.wait()
+    r1 = [dot(q[...], w1[...]) * scale for q in queries]
+    c3.wait()
+    r3 = [dot(q[...], w3[...]) * scale for q in queries]
+    hq = [(a * jax.nn.sigmoid(a) * b).astype(BF) for a, b in zip(r1, r3)]
+    c2.wait()
+    for h, out in zip(hq, reads):
+        out[...] = (dot(h, w2[...]) * scale).astype(BF)
 
 
 def norm_kernel(heads, gate, gain, mine, two, *refs):
@@ -218,7 +236,7 @@
 def local(ctx, heads, keys, values, rates, queries, fast_weights, gate, gain):
     tok, width = keys.shape
     bits = range(ctx.bit_length() - 1)
-    piece = jax.ShapeDtypeStruct((width // 4, width), BF)
+    halves = jax.ShapeDtypeStruct((width // 2, width), BF)
     matrix = jax.ShapeDtypeStruct((width, width), BF)
     mat = lambda dtype: pltpu.VMEM((width, width), dtype)
     tokens = lambda dtype: pltpu.VMEM((tok, width), dtype)
@@ -242,44 +260,51 @@
 
     outs = call(
         functools.partial(grad_two_kernel, heads), 14,
-        out_shape=[piece] * 4
+        out_shape=[halves] * 2
         + [jax.ShapeDtypeStruct((tok, width), d) for d in (F32, F32, BF)]
         + [jax.ShapeDtypeStruct((tok, width), BF)]
-        + [matrix] * 3
+        + [matrix]
         + [jax.ShapeDtypeStruct((queries.shape[0], width), BF)] * heads,
         in_specs=[HBM] * 5,
-        out_specs=[VM] * (11 + heads),
-        scratch_shapes=[tokens(BF), pltpu.VMEM(rates.shape, F32), mat(BF), sems(6 + heads)],
+        out_specs=[VM] * (7 + heads),
+        scratch_shapes=[tokens(BF), pltpu.VMEM(rates.shape, F32), mat(BF), mat(BF), mat(BF), sems(6 + heads)],
     )(hbm(keys), hbm(values), hbm(rates), hbm(fast_weights), hbm(queries))
-    two, (g1, g3, go), (k, w1, w3, w2), columns = outs[:4], outs[4:7], outs[7:11], outs[11:]
+    two, (g1, g3, go), (k, w2), columns = outs[:2], outs[2:5], outs[5:7], outs[7:]
     asked = [columns[0]] + [turn(columns[r], r) for r in range(1, heads)]
     outs = call(
         grad_one_kernel, 12,
-        out_shape=[piece] * 8,
+        out_shape=[halves] * 4,
         in_specs=[VM] * 5,
-        out_specs=[VM] * 8,
+        out_specs=[VM] * 4,
         scratch_shapes=[tokens(BF), tokens(BF), mat(BF)],
     )(k, w2, g1, g3, go)
-    one, three = outs[:4], outs[4:]
+    one, three = outs[:2], outs[2:]
 
     def add(x, y):
         return (x.astype(F32) + y.astype(F32)).astype(BF)
 
     def summed(n, p):
         plan = PLANS[n]
-        far = swap(p[3], 0)
-        near = swap(p[1], 0)
-        give = add(p[2], far)
-        keep = add(p[0], near)
-        total = add(keep, swap(give, plan[1]))
+        keep, send = p
+        got = swap(send, 0)
+        quarter = width // 4
+
+        give = add(keep[quarter:], got[quarter:])
+        total, got = add(keep[:quarter], got[:quarter]), swap(give, plan[1])
         if len(plan) == 3:
-            half = total.shape[0] // 2
-            total = add(total[:half], swap(total[half:], plan[2]))
+            half = quarter // 2
+            give = add(total[half:], got[half:])
+            total, got = add(total[:half], got[:half]), swap(give, plan[2])
         for bit in bits:
             if bit not in plan:
-                total = add(total, swap(total, bit))
+                total = add(total, got)
+                got = swap(total, bit)
         if len(plan) == 3:
-            total = jnp.concatenate([total, swap(total, plan[2])])
+            total = add(total, got)
+            got = swap(total, plan[2])
+            total = jnp.concatenate([total, got])
+        else:
+            total = add(total, got)
         return total, swap(total, plan[1])
 
     two, one, three = summed("A", two), summed("B", one), summed("C", three)
@@ -288,34 +313,35 @@
         other = [swap(x, 0) for x in own]
         return own[0], other[0], own[1], other[1]
 
-    new_two = call(
+    gains = gain.reshape(1, -1)
+    new_two, gate_here, gain_here = call(
         first_update_kernel, 10,
-        out_shape=matrix,
-        in_specs=[VM] * 5,
-        out_specs=VM,
-        scratch_shapes=[mat(BF)],
-    )(*gathered(two), w2)
-    give = [jnp.where(core() == 0, c, b) for b, c in zip(one, three)]
-    keep = [jnp.where(core() == 0, b, c) for b, c in zip(one, three)]
-    got = [swap(x, 0) for x in give]
+        out_shape=[matrix] + [jax.ShapeDtypeStruct(x.shape, x.dtype) for x in (gate, gains)],
+        in_specs=[VM] * 4 + [HBM] * 3,
+        out_specs=[VM] * 3,
+        scratch_shapes=[mat(BF), mat(BF), sems(3)],
+    )(*gathered(two), hbm(fast_weights), hbm(gate), hbm(gains))
+    keep, got = [], []
+    for b, c in zip(one, three):
+        keep.append(jnp.where(core() == 0, b, c))
+        give = lax.select_n(jnp.broadcast_to(core() == 0, b.shape), b, c)
+        got.append(swap(give, 0))
     mine = call(
         pair_update_kernel, 10,
         out_shape=matrix,
-        in_specs=[VM] * 6,
+        in_specs=[VM] * 4 + [HBM],
         out_specs=VM,
-        scratch_shapes=[mat(BF)],
-    )(*keep, *got, w1, w3)
+        scratch_shapes=[mat(BF), mat(BF), sems(1)],
+    )(*keep, *got, hbm(fast_weights))
     theirs = swap(mine, 0)
 
-    gains = gain.reshape(1, -1)
-    *reads, gate_here, gain_here = call(
+    reads = call(
         functools.partial(read_kernel, heads), 12,
-        out_shape=[jax.ShapeDtypeStruct(x.shape, BF) for x in asked]
-        + [jax.ShapeDtypeStruct(x.shape, x.dtype) for x in (gate, gains)],
-        in_specs=[HBM] * 2 + [VM] * (3 + heads),
-        out_specs=[VM] * (heads + 2),
-        scratch_shapes=[sems(2)],
-    )(hbm(gate), hbm(gains), w1, w3, w2, *asked)
+        out_shape=[jax.ShapeDtypeStruct(x.shape, BF) for x in asked],
+        in_specs=[HBM] + [VM] * heads,
+        out_specs=[VM] * heads,
+        scratch_shapes=[mat(BF)] * 3 + [sems(3)],
+    )(hbm(fast_weights), *asked)
     back = [reads[0]] + [turn(reads[r], heads - r) for r in range(1, heads)]
     layer_out, new_weights = call(
         functools.partial(norm_kernel, heads), 8,

time: 70.4 us -> 69.3 us (0.984)
  waiting for transfers between devices: 17.4 us -> 22.8 us
  other arithmetic: 5.01 us -> 0.51 us
  starting transfers between devices: 26.4 us -> 24.4 us
    ppermute x25 -> x22, waiting for transfers between devices: 17.4 us -> 22.8 us  [swap(): return lax.ppermute(x, 'ctx', [(i, i ^ 1 << bit) for i in range(ctx)])]
    convert_element_type x11, other arithmetic: 4.89 us -> 0.38 us  [add(): return (x.astype(F32) + y.astype(F32)).astype(BF)]
    ppermute x25 -> x22, starting transfers between devices: 24.3 us -> 22.3 us  [swap(): return lax.ppermute(x, 'ctx', [(i, i ^ 1 << bit) for i in range(ctx)])]
  transfers between devices with their start and end apart: 27 -> 24, of which waited for: 12 -> 12; matrix products, arithmetic and copies ran while one was open for 7% -> 1% of each run, Pallas kernels for 21% -> 22%
where the time goes in v4:
time: 69.3 us; the launch traced here: 69.2 us
  starting transfers between devices  24.4 us (35%)
  waiting for transfers between devices  22.8 us (33%)
  Pallas kernels  20.5 us (30%)
  between operations  0.96 us (1%)
    ppermute x22, waiting for transfers between devices, swap(): return lax.ppermute(x, 'ctx', [(i, i ^ 1 << bit) for i in range(ctx)])  22.8 us
    ppermute x22, starting transfers between devices, swap(): return lax.ppermute(x, 'ctx', [(i, i ^ 1 << bit) for i in range(ctx)])  22.3 us
    pallas_call x7, Pallas kernels, run(): pl.pallas_call(kernel, compiler_params=pltpu.CompilerParams(vmem_limit_by...  20.5 us
    ppermute x2, starting transfers between devices, turn(): return lax.ppermute(x, 'head', [(i, (i + r) % heads) for i in range(heads)])  2.08 us
  transfers between devices with their start and end apart: 24, of which 12 were waited for; matrix products, arithmetic and copies ran while one was open for 1% of the time, Pallas kernels for 22%

profile of v4, /device:TPU:0, one launch (start us, length us, event | category | flops | bytes accessed | tf_op | source)
XLA Modules:
  0.0 69.2 jit_solution(11057012320212280236)
XLA Ops:
  0.6 2.9 %shard_map.86 = (bf16[256,512]{1,0:T(8,128)(2,1)S(1)}, bf16[256,512]{1,0:T(8,128)(2,1)S(1)}, f32[512,512]{1,0:T(8,128)S(1)}, f32[512,512]{1,0:T(8,128)S(1)}, bf1...) custom-call(bf16[512,512]{1,0:T(8,128)(2,1)} %k_hbm.1, ...), custom_call_target="tpu_custom_call" | custom-call | tf_op jit(solution)/shard_map/pallas_call | solution.py:249
  3.5 1.3 %shard_map.88 = (bf16[256,512]{1,0:T(8,128)(2,1)S(1)}, bf16[256,512]{1,0:T(8,128)(2,1)S(1)}, bf16[256,512]{1,0:T(8,128)(2,1)S(1)}, bf16[256,512]{1,0:T(8,128)(2,1)S(1)}) custom-call(bf16[512,512]{1,0:T(8,128)(2,1)S(1)} %get-tuple-element.26.k, bf16[512,512]{1,0:T(8,128)(2,1)S(1)} %get-tuple-element.27.w2, f32[512,512]{1,0:T(8,128)S(1)} %get-tuple-element.28.g1_ref, ...), custom_call_target="tpu_custom_call" | custom-call | tf_op jit(solution)/shard_map/pallas_call | solution.py:249
  4.8 0.6 collective-permute-start.8
  5.4 1.2 %collective-permute-done.8 = bf16[256,512]{1,0:T(8,128)(2,1)S(1)} collective-permute-done((bf16[256,512]{1,0:T(8,128)(2,1)S(1)}, bf16[256,512]{1,0:T(8,128)(2,1)S(1)}, u32[]{:S(2)}, u32[]{:S(2)}) %collective-permute-start.8) | collective-permute-done | bytes 262176 | tf_op jit(solution)/shard_map/ppermute | solution.py:256
  6.6 0.1 add_convert_fusion.6
  6.6 3.0 %collective-permute-start.9 = (bf16[128,512]{1,0:T(8,128)(2,1)S(1)}, bf16[128,512]{1,0:T(8,128)(2,1)S(1)}, u32[]{:S(2)}, u32[]{:S(2)}) collective-permute-start(bf16[128,512]{1,0:T(8,128)(2,1)S(1)} %get-tuple-element.45), channel_id=1, source_target_pairs={{0,8},{2,10},{4,12},{6,14},{8,0},{10,2},{12,4},{14,6},{16,24},{18,... | collective-permute-start | bytes 393224 | tf_op jit(solution)/shard_map/ppermute | solution.py:256
  9.6 0.0 collective-permute-start.13
  9.6 0.5 collective-permute-start
  10.1 3.3 %collective-permute-done.9 = bf16[128,512]{1,0:T(8,128)(2,1)S(1)} collective-permute-done((bf16[128,512]{1,0:T(8,128)(2,1)S(1)}, bf16[128,512]{1,0:T(8,128)(2,1)S(1)}, u32[]{:S(2)}, u32[]{:S(2)}) %collective-permute-start.9) | collective-permute-done | bytes 131104 | tf_op jit(solution)/shard_map/ppermute | solution.py:256
  13.4 1.7 %collective-permute-start.10 = (bf16[64,512]{1,0:T(8,128)(2,1)S(1)}, bf16[64,512]{1,0:T(8,128)(2,1)S(1)}, u32[]{:S(2)}, u32[]{:S(2)}) collective-permute-start(bf16[64,512]{1,0:T(8,128)(2,1)S(1)} %add_convert_fusion.11), channel_id=1, source_target_pairs={{0,4},{2,6},{4,0},{6,2},{8,12},{10,14},{12,8},{14,10},{16,20},{18,... | collective-permute-start | bytes 196616 | tf_op jit(solution)/shard_map/ppermute | solution.py:256
  15.2 0.0 collective-permute-done.13
  15.2 0.4 collective-permute-start.14
  15.6 2.8 %collective-permute-done.10 = bf16[64,512]{1,0:T(8,128)(2,1)S(1)} collective-permute-done((bf16[64,512]{1,0:T(8,128)(2,1)S(1)}, bf16[64,512]{1,0:T(8,128)(2,1)S(1)}, u32[]{:S(2)}, u32[]{:S(2)}) %collective-permute-start.10) | collective-permute-done | bytes 65568 | tf_op jit(solution)/shard_map/ppermute | solution.py:256
  18.5 2.8 %collective-permute-start.11 = (bf16[64,512]{1,0:T(8,128)(2,1)S(1)}, bf16[64,512]{1,0:T(8,128)(2,1)S(1)}, u32[]{:S(2)}, u32[]{:S(2)}) collective-permute-start(bf16[64,512]{1,0:T(8,128)(2,1)S(1)} %add_convert_fusion.10), channel_id=1, source_target_pairs={{0,16},{2,18},{4,20},{6,22},{8,24},{10,26},{12,28},{14,30},{16,0},... | collective-permute-start | bytes 196616 | tf_op jit(solution)/shard_map/ppermute | solution.py:256
  21.3 0.0 collective-permute-done.14
  21.3 0.1 add_convert_fusion.2
  21.4 1.6 %collective-permute-start.15 = (bf16[128,512]{1,0:T(8,128)(2,1)S(1)}, bf16[128,512]{1,0:T(8,128)(2,1)S(1)}, u32[]{:S(2)}, u32[]{:S(2)}) collective-permute-start(bf16[128,512]{1,0:T(8,128)(2,1)S(1)} %add_convert_fusion.2), channel_id=1, source_target_pairs={{0,8},{2,10},{4,12},{6,14},{8,0},{10,2},{12,4},{14,6},{16,24},{18,... | collective-permute-start | bytes 393224 | tf_op jit(solution)/shard_map/ppermute | solution.py:256
  23.0 0.8 %collective-permute-done.11 = bf16[64,512]{1,0:T(8,128)(2,1)S(1)} collective-permute-done((bf16[64,512]{1,0:T(8,128)(2,1)S(1)}, bf16[64,512]{1,0:T(8,128)(2,1)S(1)}, u32[]{:S(2)}, u32[]{:S(2)}) %collective-permute-start.11) | collective-permute-done | bytes 65568 | tf_op jit(solution)/shard_map/ppermute | solution.py:256
  23.9 1.3 %collective-permute-start.12 = (bf16[64,512]{1,0:T(8,128)(2,1)S(1)}, bf16[64,512]{1,0:T(8,128)(2,1)S(1)}, u32[]{:S(2)}, u32[]{:S(2)}) collective-permute-start(bf16[64,512]{1,0:T(8,128)(2,1)S(1)} %add_convert_fusion.9), channel_id=1, source_target_pairs={{0,4},{2,6},{4,0},{6,2},{8,12},{10,14},{12,8},{14,10},{16,20},{18,... | collective-permute-start | bytes 196616 | tf_op jit(solution)/shard_map/ppermute | solution.py:256
  25.2 1.2 %collective-permute-done.15 = bf16[128,512]{1,0:T(8,128)(2,1)S(1)} collective-permute-done((bf16[128,512]{1,0:T(8,128)(2,1)S(1)}, bf16[128,512]{1,0:T(8,128)(2,1)S(1)}, u32[]{:S(2)}, u32[]{:S(2)}) %collective-permute-start.15) | collective-permute-done | bytes 131104 | tf_op jit(solution)/shard_map/ppermute | solution.py:256
  26.5 1.7 %collective-permute-start.16 = (bf16[128,512]{1,0:T(8,128)(2,1)S(1)}, bf16[128,512]{1,0:T(8,128)(2,1)S(1)}, u32[]{:S(2)}, u32[]{:S(2)}) collective-permute-start(bf16[128,512]{1,0:T(8,128)(2,1)S(1)} %add_convert_fusion.1), channel_id=1, source_target_pairs={{0,16},{2,18},{4,20},{6,22},{8,24},{10,26},{12,28},{14,30},{16,0},... | collective-permute-start | bytes 393224 | tf_op jit(solution)/shard_map/ppermute | solution.py:256
  28.2 0.0 collective-permute-done
  28.2 0.1 add_convert_fusion.8
  28.2 0.9 %collective-permute-start.1 = (bf16[128,512]{1,0:T(8,128)(2,1)S(1)}, bf16[128,512]{1,0:T(8,128)(2,1)S(1)}, u32[]{:S(2)}, u32[]{:S(2)}) collective-permute-start(bf16[128,512]{1,0:T(8,128)(2,1)S(1)} %get-tuple-element.47), channel_id=1, source_target_pairs={{0,4},{2,6},{4,0},{6,2},{8,12},{10,14},{12,8},{14,10},{16,20},{18,... | collective-permute-start | bytes 393224 | tf_op jit(solution)/shard_map/ppermute | solution.py:256
  29.2 0.0 collective-permute-done.12
  29.2 4.7 %collective-permute-done.16 = bf16[128,512]{1,0:T(8,128)(2,1)S(1)} collective-permute-done((bf16[128,512]{1,0:T(8,128)(2,1)S(1)}, bf16[128,512]{1,0:T(8,128)(2,1)S(1)}, u32[]{:S(2)}, u32[]{:S(2)}) %collective-permute-start.16) | collective-permute-done | bytes 131104 | tf_op jit(solution)/shard_map/ppermute | solution.py:256
  33.9 0.1 broadcast_select_fusion.1
  34.0 1.2 %collective-permute-start.18 = (bf16[128,512]{1,0:T(8,128)(2,1)S(1)}, bf16[128,512]{1,0:T(8,128)(2,1)S(1)}, u32[]{:S(2)}, u32[]{:S(2)}) collective-permute-start(bf16[128,512]{1,0:T(8,128)(2,1)S(1)} %get-tuple-element.43), channel_id=1, source_target_pairs={{0,4},{2,6},{4,0},{6,2},{8,12},{10,14},{12,8},{14,10},{16,20},{18,... | collective-permute-start | bytes 393224 | tf_op jit(solution)/shard_map/ppermute | solution.py:256
  35.2 0.3 collective-permute-start.17
  35.5 0.0 collective-permute-done.1
  35.5 1.9 %collective-permute-start.2 = (bf16[64,512]{1,0:T(8,128)(2,1)S(1)}, bf16[64,512]{1,0:T(8,128)(2,1)S(1)}, u32[]{:S(2)}, u32[]{:S(2)}) collective-permute-start(bf16[64,512]{1,0:T(8,128)(2,1)S(1)} %add_convert_fusion.15), channel_id=1, source_target_pairs={{0,8},{2,10},{4,12},{6,14},{8,0},{10,2},{12,4},{14,6},{16,24},{18,... | collective-permute-start | bytes 196616 | tf_op jit(solution)/shard_map/ppermute | solution.py:256
  37.4 0.0 collective-permute-start.19
  37.4 2.8 %collective-permute-done.17 = bf16[128,512]{1,0:T(8,128)(2,1)S(1)} collective-permute-done((bf16[128,512]{1,0:T(8,128)(2,1)S(1)}, bf16[128,512]{1,0:T(8,128)(2,1)S(1)}, u32[]{:S(2)}, u32[]{:S(2)}) %collective-permute-start.17) | collective-permute-done | bytes 131104 | tf_op jit(solution)/shard_map/ppermute | solution.py:256
  40.2 0.0 collective-permute-done.18
  40.3 0.1 collective-permute-start.20
  40.3 0.6 collective-permute-done.2
  41.0 1.5 %collective-permute-start.3 = (bf16[64,512]{1,0:T(8,128)(2,1)S(1)}, bf16[64,512]{1,0:T(8,128)(2,1)S(1)}, u32[]{:S(2)}, u32[]{:S(2)}) collective-permute-start(bf16[64,512]{1,0:T(8,128)(2,1)S(1)} %add_convert_fusion.14), channel_id=1, source_target_pairs={{0,16},{2,18},{4,20},{6,22},{8,24},{10,26},{12,28},{14,30},{16,0},... | collective-permute-start | bytes 196616 | tf_op jit(solution)/shard_map/ppermute | solution.py:256
  42.5 1.5 %collective-permute-start.21 = (bf16[256,512]{1,0:T(8,128)(2,1)S(1)}, bf16[256,512]{1,0:T(8,128)(2,1)S(1)}, u32[]{:S(2)}, u32[]{:S(2)}) collective-permute-start(bf16[256,512]{1,0:T(8,128)(2,1)S(1)} %get-tuple-element.37), channel_id=1, source_target_pairs={{0,1},{1,0},{2,3},{3,2},{4,5},{5,4},{6,7},{7,6},{8,9},{9,8},{10,11... | collective-permute-start | bytes 786440 | tf_op jit(solution)/shard_map/ppermute | solution.py:259
  44.0 0.0 collective-permute-done.19.p1
  44.0 0.0 collective-permute-done.20.p3
  44.0 5.7 %shard_map.89.mine = bf16[512,512]{1,0:T(8,128)(2,1)S(1)} custom-call(bf16[128,512]{1,0:T(8,128)(2,1)S(1)} %get-tuple-element.51.p0, bf16[128,512]{1,0:T(8,128)(2,1)S(1)} %get-tuple-element.49.p2, bf16[128,512]{1,0:T(8,128)(2,1)S(1)} %collective-permute-done.19.p1, bf16[128,512]{1,0:T(8,128)(2,1)S(1)} %collective-permute-done.20.p3, ...), custom_call_target="tpu_custom_call" | custom-call | tf_op jit(solution)/shard_map/pallas_call | solution.py:249
  49.7 0.1 collective-permute-start.23
  49.7 0.0 collective-permute-done.3
  49.8 1.4 %collective-permute-start.4 = (bf16[64,512]{1,0:T(8,128)(2,1)S(1)}, bf16[64,512]{1,0:T(8,128)(2,1)S(1)}, u32[]{:S(2)}, u32[]{:S(2)}) collective-permute-start(bf16[64,512]{1,0:T(8,128)(2,1)S(1)} %add_convert_fusion.13), channel_id=1, source_target_pairs={{0,8},{2,10},{4,12},{6,14},{8,0},{10,2},{12,4},{14,6},{16,24},{18,... | collective-permute-start | bytes 196616 | tf_op jit(solution)/shard_map/ppermute | solution.py:256
  51.1 3.2 %collective-permute-done.4 = bf16[64,512]{1,0:T(8,128)(2,1)S(1)} collective-permute-done((bf16[64,512]{1,0:T(8,128)(2,1)S(1)}, bf16[64,512]{1,0:T(8,128)(2,1)S(1)}, u32[]{:S(2)}, u32[]{:S(2)}) %collective-permute-start.4) | collective-permute-done | bytes 65568 | tf_op jit(solution)/shard_map/ppermute | solution.py:256
  54.3 1.2 %collective-permute-start.6 = (bf16[128,512]{1,0:T(8,128)(2,1)S(1)}, bf16[128,512]{1,0:T(8,128)(2,1)S(1)}, u32[]{:S(2)}, u32[]{:S(2)}) collective-permute-start(bf16[128,512]{1,0:T(8,128)(2,1)S(1)} %pad_maximum_fusion.p0), channel_id=1, source_target_pairs={{0,4},{2,6},{4,0},{6,2},{8,12},{10,14},{12,8},{14,10},{16,20},{18,... | collective-permute-start | bytes 393224 | tf_op jit(solution)/shard_map/ppermute | solution.py:256
  55.6 0.0 collective-permute-done.21.refs_1_
  55.6 2.4 %shard_map.90 = (bf16[256,512]{1,0:T(8,128)(2,1)S(1)}, bf16[256,512]{1,0:T(8,128)(2,1)S(1)}) custom-call(bf16[1,3,512,512]{3,2,1,0:T(8,128)(2,1)} %w_hbm.7, bf16[256,512]{1,0:T(8,128)(2,1)S(1)} %get-tuple-element.36.refs_0_, bf16[256,512]{1,0:T(8,128)(2,1)S(1)} %collective-permute-done.21.refs_1_), custom_call_target="tpu_custom_call" | custom-call | tf_op jit(solution)/shard_map/pallas_call | solution.py:249
  58.0 0.6 collective-permute-start.22
  58.6 0.0 collective-permute-start.5
  58.6 0.8 %collective-permute-done.6.p2 = bf16[128,512]{1,0:T(8,128)(2,1)S(1)} collective-permute-done((bf16[128,512]{1,0:T(8,128)(2,1)S(1)}, bf16[128,512]{1,0:T(8,128)(2,1)S(1)}, u32[]{:S(2)}, u32[]{:S(2)}) %collective-permute-start.6) | collective-permute-done | bytes 131104 | tf_op jit(solution)/shard_map/ppermute | solution.py:256
  59.4 0.0 collective-permute-start.7
  59.4 0.5 collective-permute-done.5.p1
  59.9 0.8 %collective-permute-done.7.p3 = bf16[128,512]{1,0:T(8,128)(2,1)S(1)} collective-permute-done((bf16[128,512]{1,0:T(8,128)(2,1)S(1)}, bf16[128,512]{1,0:T(8,128)(2,1)S(1)}, u32[]{:S(2)}, u32[]{:S(2)}) %collective-permute-start.7) | collective-permute-done | bytes 131104 | tf_op jit(solution)/shard_map/ppermute | solution.py:256
  60.8 5.5 %shard_map.87 = (bf16[512,512]{1,0:T(8,128)(2,1)S(1)}, bf16[256,1024]{1,0:T(8,128)(2,1)S(1)}, f32[1,1024]{1,0:T(1,128)S(1)}) custom-call(bf16[128,512]{1,0:T(8,128)(2,1)S(1)} %pad_maximum_fusion.p0, bf16[128,512]{1,0:T(8,128)(2,1)S(1)} %collective-permute-done.5.p1, bf16[128,512]{1,0:T(8,128)(2,1)S(1)} %collective-permute-done.6.p2, ...), custom_call_target="tpu_custom_call" | custom-call | tf_op jit(solution)/shard_map/pallas_call | solution.py:249
  66.3 0.0 collective-permute-done.22.refs_1_
  66.3 1.9 %shard_map.91 = (bf16[256,1024]{1,0:T(8,128)(2,1)}, bf16[1,3,512,512]{3,2,1,0:T(8,128)(2,1)}) custom-call(bf16[256,1024]{1,0:T(8,128)(2,1)S(1)} %get-tuple-element.24.gate, f32[1,1024]{1,0:T(1,128)S(1)} %get-tuple-element.25.gain, bf16[512,512]{1,0:T(8,128)(2,1)S(1)} %shard_map.89.mine, bf16[512,512]{1,0:T(8,128)(2,1)S(1)} %get-tuple-element.35.two, ...), custom_call_target="tpu_custom_call" | custom-call | tf_op jit(solution)/shard_map/pallas_call | solution.py:249
  68.2 0.0 collective-permute-done.23.theirs
  68.2 0.8 %shard_map.92 = bf16[1,3,512,512]{3,2,1,0:T(8,128)(2,1)} custom-call(bf16[512,512]{1,0:T(8,128)(2,1)S(1)} %collective-permute-done.23.theirs, bf16[1,3,512,512]{3,2,1,0:T(8,128)(2,1)} %get-tuple-element.41.partial), custom_call_target="tpu_custom_call", output_to_operand_aliasing={{}: (1, {})} | custom-call | tf_op jit(solution)/shard_map/pallas_call | solution.py:249
  (11 shorter events, 0.3 us)
Async XLA Ops:
  4.8 1.7 %collective-permute-start.8 = (bf16[256,512]{1,0:T(8,128)(2,1)S(1)}, bf16[256,512]{1,0:T(8,128)(2,1)S(1)}, u32[]{:S(2)}, u32[]{:S(2)}) collective-permute-start(bf16[256,512]{1,0:T(8,128)(2,1)S(1)} %get-tuple-element.32), channel_id=1, source_target_pairs={{0,2},{2,0},{4,6},{6,4},{8,10},{10,8},{12,14},{14,12},{16,18},{18,... | collective-permute-start | bytes 786440 | tf_op jit(solution)/shard_map/ppermute | solution.py:256
  6.6 6.8 %collective-permute-start.9 = (bf16[128,512]{1,0:T(8,128)(2,1)S(1)}, bf16[128,512]{1,0:T(8,128)(2,1)S(1)}, u32[]{:S(2)}, u32[]{:S(2)}) collective-permute-start(bf16[128,512]{1,0:T(8,128)(2,1)S(1)} %get-tuple-element.45), channel_id=1, source_target_pairs={{0,8},{2,10},{4,12},{6,14},{8,0},{10,2},{12,4},{14,6},{16,24},{18,... | collective-permute-start | bytes 393224 | tf_op jit(solution)/shard_map/ppermute | solution.py:256
  9.6 5.5 %collective-permute-start.13 = (bf16[256,512]{1,0:T(8,128)(2,1)S(1)}, bf16[256,512]{1,0:T(8,128)(2,1)S(1)}, u32[]{:S(2)}, u32[]{:S(2)}) collective-permute-start(bf16[256,512]{1,0:T(8,128)(2,1)S(1)} %get-tuple-element.34), channel_id=1, source_target_pairs={{0,2},{2,0},{4,6},{6,4},{8,10},{10,8},{12,14},{14,12},{16,18},{18,... | collective-permute-start | bytes 786440 | tf_op jit(solution)/shard_map/ppermute | solution.py:256
  9.6 18.5 %collective-permute-start = (bf16[256,512]{1,0:T(8,128)(2,1)S(1)}, bf16[256,512]{1,0:T(8,128)(2,1)S(1)}, u32[]{:S(2)}, u32[]{:S(2)}) collective-permute-start(bf16[256,512]{1,0:T(8,128)(2,1)S(1)} %get-tuple-element.23), channel_id=1, source_target_pairs={{0,2},{2,0},{4,6},{6,4},{8,10},{10,8},{12,14},{14,12},{16,18},{18,... | collective-permute-start | bytes 786440 | tf_op jit(solution)/shard_map/ppermute | solution.py:256
  13.4 5.0 %collective-permute-start.10 = (bf16[64,512]{1,0:T(8,128)(2,1)S(1)}, bf16[64,512]{1,0:T(8,128)(2,1)S(1)}, u32[]{:S(2)}, u32[]{:S(2)}) collective-permute-start(bf16[64,512]{1,0:T(8,128)(2,1)S(1)} %add_convert_fusion.11), channel_id=1, source_target_pairs={{0,4},{2,6},{4,0},{6,2},{8,12},{10,14},{12,8},{14,10},{16,20},{18,... | collective-permute-start | bytes 196616 | tf_op jit(solution)/shard_map/ppermute | solution.py:256
  15.2 6.1 %collective-permute-start.14 = (bf16[128,512]{1,0:T(8,128)(2,1)S(1)}, bf16[128,512]{1,0:T(8,128)(2,1)S(1)}, u32[]{:S(2)}, u32[]{:S(2)}) collective-permute-start(bf16[128,512]{1,0:T(8,128)(2,1)S(1)} %add_convert_fusion.3), channel_id=1, source_target_pairs={{0,4},{2,6},{4,0},{6,2},{8,12},{10,14},{12,8},{14,10},{16,20},{18,... | collective-permute-start | bytes 393224 | tf_op jit(solution)/shard_map/ppermute | solution.py:256
  18.5 5.3 %collective-permute-start.11 = (bf16[64,512]{1,0:T(8,128)(2,1)S(1)}, bf16[64,512]{1,0:T(8,128)(2,1)S(1)}, u32[]{:S(2)}, u32[]{:S(2)}) collective-permute-start(bf16[64,512]{1,0:T(8,128)(2,1)S(1)} %add_convert_fusion.10), channel_id=1, source_target_pairs={{0,16},{2,18},{4,20},{6,22},{8,24},{10,26},{12,28},{14,30},{16,0},... | collective-permute-start | bytes 196616 | tf_op jit(solution)/shard_map/ppermute | solution.py:256
  21.4 5.0 %collective-permute-start.15 = (bf16[128,512]{1,0:T(8,128)(2,1)S(1)}, bf16[128,512]{1,0:T(8,128)(2,1)S(1)}, u32[]{:S(2)}, u32[]{:S(2)}) collective-permute-start(bf16[128,512]{1,0:T(8,128)(2,1)S(1)} %add_convert_fusion.2), channel_id=1, source_target_pairs={{0,8},{2,10},{4,12},{6,14},{8,0},{10,2},{12,4},{14,6},{16,24},{18,... | collective-permute-start | bytes 393224 | tf_op jit(solution)/shard_map/ppermute | solution.py:256
  23.9 5.3 %collective-permute-start.12 = (bf16[64,512]{1,0:T(8,128)(2,1)S(1)}, bf16[64,512]{1,0:T(8,128)(2,1)S(1)}, u32[]{:S(2)}, u32[]{:S(2)}) collective-permute-start(bf16[64,512]{1,0:T(8,128)(2,1)S(1)} %add_convert_fusion.9), channel_id=1, source_target_pairs={{0,4},{2,6},{4,0},{6,2},{8,12},{10,14},{12,8},{14,10},{16,20},{18,... | collective-permute-start | bytes 196616 | tf_op jit(solution)/shard_map/ppermute | solution.py:256
  26.5 7.4 %collective-permute-start.16 = (bf16[128,512]{1,0:T(8,128)(2,1)S(1)}, bf16[128,512]{1,0:T(8,128)(2,1)S(1)}, u32[]{:S(2)}, u32[]{:S(2)}) collective-permute-start(bf16[128,512]{1,0:T(8,128)(2,1)S(1)} %add_convert_fusion.1), channel_id=1, source_target_pairs={{0,16},{2,18},{4,20},{6,22},{8,24},{10,26},{12,28},{14,30},{16,0},... | collective-permute-start | bytes 393224 | tf_op jit(solution)/shard_map/ppermute | solution.py:256
  28.2 7.3 %collective-permute-start.1 = (bf16[128,512]{1,0:T(8,128)(2,1)S(1)}, bf16[128,512]{1,0:T(8,128)(2,1)S(1)}, u32[]{:S(2)}, u32[]{:S(2)}) collective-permute-start(bf16[128,512]{1,0:T(8,128)(2,1)S(1)} %get-tuple-element.47), channel_id=1, source_target_pairs={{0,4},{2,6},{4,0},{6,2},{8,12},{10,14},{12,8},{14,10},{16,20},{18,... | collective-permute-start | bytes 393224 | tf_op jit(solution)/shard_map/ppermute | solution.py:256
  34.0 6.3 %collective-permute-start.18 = (bf16[128,512]{1,0:T(8,128)(2,1)S(1)}, bf16[128,512]{1,0:T(8,128)(2,1)S(1)}, u32[]{:S(2)}, u32[]{:S(2)}) collective-permute-start(bf16[128,512]{1,0:T(8,128)(2,1)S(1)} %get-tuple-element.43), channel_id=1, source_target_pairs={{0,4},{2,6},{4,0},{6,2},{8,12},{10,14},{12,8},{14,10},{16,20},{18,... | collective-permute-start | bytes 393224 | tf_op jit(solution)/shard_map/ppermute | solution.py:256
  35.2 5.0 %collective-permute-start.17 = (bf16[128,512]{1,0:T(8,128)(2,1)S(1)}, bf16[128,512]{1,0:T(8,128)(2,1)S(1)}, u32[]{:S(2)}, u32[]{:S(2)}) collective-permute-start(bf16[128,512]{1,0:T(8,128)(2,1)S(1)} %get-tuple-element.50), channel_id=1, source_target_pairs={{0,8},{2,10},{4,12},{6,14},{8,0},{10,2},{12,4},{14,6},{16,24},{18,... | collective-permute-start | bytes 393224 | tf_op jit(solution)/shard_map/ppermute | solution.py:256
  35.5 5.4 %collective-permute-start.2 = (bf16[64,512]{1,0:T(8,128)(2,1)S(1)}, bf16[64,512]{1,0:T(8,128)(2,1)S(1)}, u32[]{:S(2)}, u32[]{:S(2)}) collective-permute-start(bf16[64,512]{1,0:T(8,128)(2,1)S(1)} %add_convert_fusion.15), channel_id=1, source_target_pairs={{0,8},{2,10},{4,12},{6,14},{8,0},{10,2},{12,4},{14,6},{16,24},{18,... | collective-permute-start | bytes 196616 | tf_op jit(solution)/shard_map/ppermute | solution.py:256
  37.4 6.6 %collective-permute-start.19 = (bf16[128,512]{1,0:T(8,128)(2,1)S(1)}, bf16[128,512]{1,0:T(8,128)(2,1)S(1)}, u32[]{:S(2)}, u32[]{:S(2)}) collective-permute-start(bf16[128,512]{1,0:T(8,128)(2,1)S(1)} %get-tuple-element.42), channel_id=1, source_target_pairs={{0,2},{2,0},{4,6},{6,4},{8,10},{10,8},{12,14},{14,12},{16,18},{18,... | collective-permute-start | bytes 393224 | tf_op jit(solution)/shard_map/ppermute | solution.py:256
  40.3 3.7 %collective-permute-start.20 = (bf16[128,512]{1,0:T(8,128)(2,1)S(1)}, bf16[128,512]{1,0:T(8,128)(2,1)S(1)}, u32[]{:S(2)}, u32[]{:S(2)}) collective-permute-start(bf16[128,512]{1,0:T(8,128)(2,1)S(1)} %get-tuple-element.48), channel_id=1, source_target_pairs={{0,2},{2,0},{4,6},{6,4},{8,10},{10,8},{12,14},{14,12},{16,18},{18,... | collective-permute-start | bytes 393224 | tf_op jit(solution)/shard_map/ppermute | solution.py:256
  41.0 8.8 %collective-permute-start.3 = (bf16[64,512]{1,0:T(8,128)(2,1)S(1)}, bf16[64,512]{1,0:T(8,128)(2,1)S(1)}, u32[]{:S(2)}, u32[]{:S(2)}) collective-permute-start(bf16[64,512]{1,0:T(8,128)(2,1)S(1)} %add_convert_fusion.14), channel_id=1, source_target_pairs={{0,16},{2,18},{4,20},{6,22},{8,24},{10,26},{12,28},{14,30},{16,0},... | collective-permute-start | bytes 196616 | tf_op jit(solution)/shard_map/ppermute | solution.py:256
  42.5 13.1 %collective-permute-start.21 = (bf16[256,512]{1,0:T(8,128)(2,1)S(1)}, bf16[256,512]{1,0:T(8,128)(2,1)S(1)}, u32[]{:S(2)}, u32[]{:S(2)}) collective-permute-start(bf16[256,512]{1,0:T(8,128)(2,1)S(1)} %get-tuple-element.37), channel_id=1, source_target_pairs={{0,1},{1,0},{2,3},{3,2},{4,5},{5,4},{6,7},{7,6},{8,9},{9,8},{10,11... | collective-permute-start | bytes 786440 | tf_op jit(solution)/shard_map/ppermute | solution.py:259
  49.7 18.5 %collective-permute-start.23 = (bf16[512,512]{1,0:T(8,128)(2,1)S(1)}, bf16[512,512]{1,0:T(8,128)(2,1)S(1)}, u32[]{:S(2)}, u32[]{:S(2)}) collective-permute-start(bf16[512,512]{1,0:T(8,128)(2,1)S(1)} %shard_map.89.mine), channel_id=1, source_target_pairs={{0,2},{2,0},{4,6},{6,4},{8,10},{10,8},{12,14},{14,12},{16,18},{18,... | collective-permute-start | bytes 1572872 | tf_op jit(solution)/shard_map/ppermute | solution.py:256
  49.8 4.5 %collective-permute-start.4 = (bf16[64,512]{1,0:T(8,128)(2,1)S(1)}, bf16[64,512]{1,0:T(8,128)(2,1)S(1)}, u32[]{:S(2)}, u32[]{:S(2)}) collective-permute-start(bf16[64,512]{1,0:T(8,128)(2,1)S(1)} %add_convert_fusion.13), channel_id=1, source_target_pairs={{0,8},{2,10},{4,12},{6,14},{8,0},{10,2},{12,4},{14,6},{16,24},{18,... | collective-permute-start | bytes 196616 | tf_op jit(solution)/shard_map/ppermute | solution.py:256
  54.3 5.1 %collective-permute-start.6 = (bf16[128,512]{1,0:T(8,128)(2,1)S(1)}, bf16[128,512]{1,0:T(8,128)(2,1)S(1)}, u32[]{:S(2)}, u32[]{:S(2)}) collective-permute-start(bf16[128,512]{1,0:T(8,128)(2,1)S(1)} %pad_maximum_fusion.p0), channel_id=1, source_target_pairs={{0,4},{2,6},{4,0},{6,2},{8,12},{10,14},{12,8},{14,10},{16,20},{18,... | collective-permute-start | bytes 393224 | tf_op jit(solution)/shard_map/ppermute | solution.py:256
  58.0 8.3 %collective-permute-start.22 = (bf16[256,512]{1,0:T(8,128)(2,1)S(1)}, bf16[256,512]{1,0:T(8,128)(2,1)S(1)}, u32[]{:S(2)}, u32[]{:S(2)}) collective-permute-start(bf16[256,512]{1,0:T(8,128)(2,1)S(1)} %get-tuple-element.39), channel_id=1, source_target_pairs={{0,1},{1,0},{2,3},{3,2},{4,5},{5,4},{6,7},{7,6},{8,9},{9,8},{10,11... | collective-permute-start | bytes 786440 | tf_op jit(solution)/shard_map/ppermute | solution.py:259
  58.6 1.3 %collective-permute-start.5 = (bf16[128,512]{1,0:T(8,128)(2,1)S(1)}, bf16[128,512]{1,0:T(8,128)(2,1)S(1)}, u32[]{:S(2)}, u32[]{:S(2)}) collective-permute-start(bf16[128,512]{1,0:T(8,128)(2,1)S(1)} %pad_maximum_fusion.p0), channel_id=1, source_target_pairs={{0,2},{2,0},{4,6},{6,4},{8,10},{10,8},{12,14},{14,12},{16,18},{18,... | collective-permute-start | bytes 393224 | tf_op jit(solution)/shard_map/ppermute | solution.py:256
  59.4 1.3 %collective-permute-start.7 = (bf16[128,512]{1,0:T(8,128)(2,1)S(1)}, bf16[128,512]{1,0:T(8,128)(2,1)S(1)}, u32[]{:S(2)}, u32[]{:S(2)}) collective-permute-start(bf16[128,512]{1,0:T(8,128)(2,1)S(1)} %collective-permute-done.6.p2), channel_id=1, source_target_pairs={{0,2},{2,0},{4,6},{6,4},{8,10},{10,8},{12,14},{14,12},{16,18},{18,... | collective-permute-start | bytes 393224 | tf_op jit(solution)/shard_map/ppermute | solution.py:256

commit v5 on v4

--- a/solution.py
+++ b/solution.py
@@ -10,6 +10,7 @@
 
 
 NS_STEPS = 5
+FIRST_STEPS = 4
 coef_a = 3.4445
 coef_b = -4.775
 coef_c = 2.0315
@@ -136,28 +137,22 @@
 
 def step(x):
     half = x.shape[0] // 2
-    x0, x1 = x[:half], x[half:]
     cat = jnp.concatenate
-    a00 = dot_nt(x0, x0).astype(BF)
-    a01 = dot_nt(x0, x1).astype(BF)
-    a11 = dot_nt(x1, x1).astype(BF)
-    a0 = cat([a00, a01], 1)
-    a1 = cat([a01.T, a11], 1)
-    b00 = polynomial(a00, dot_nt(a0, a0))
-    b01 = polynomial(a01, dot_nt(a0, a1))
-    b11 = polynomial(a11, dot_nt(a1, a1))
-    b0 = cat([b00, b01], 1)
-    b1 = cat([b01.T, b11], 1)
-    y0 = (coef_a * x0.astype(F32) + dot(b0, x)).astype(BF)
-    y1 = (coef_a * x1.astype(F32) + dot(b1, x)).astype(BF)
-    return cat([y0, y1], 0)
-
-
-def orthogonalize(*grads):
-    xs = [normalized(grad) for grad in grads]
-    for _ in range(NS_STEPS):
-        xs = [step(x) for x in xs]
-    return xs
+    gram = dot_nt(x, x).astype(BF)
+    upper, lower = gram[:half], gram[half:]
+    b01 = polynomial(upper[:, half:], dot(upper, gram[:, half:]))
+    b10 = b01.T
+    b00 = polynomial(upper[:, :half], dot(upper, gram[:, :half]))
+    b11 = polynomial(lower[:, half:], dot(lower, gram[:, half:]))
+    y0 = coef_a * x[:half].astype(F32) + dot(cat([b00, b01], 1), x)
+    y1 = coef_a * x[half:].astype(F32) + dot(cat([b10, b11], 1), x)
+    return cat([y0.astype(BF), y1.astype(BF)], 0)
+
+
+def steps(x, count):
+    for _ in range(count):
+        x = step(x)
+    return x
 
 
 def updated(weight, x):
@@ -165,14 +160,19 @@
     return (weight.astype(F32) - step_size * x.astype(F32)).astype(BF)
 
 
-def first_update_kernel(p0, p1, p2, p3, w_hbm, gate_hbm, gain_hbm, o_ref, gate, gain, w, whole, sems):
-    cw, *made = copies([(w_hbm.at[0, 2], w), (gate_hbm, gate), (gain_hbm, gain)], sems)
+def first_steps_kernel(p0, p1, p2, p3, gate_hbm, gain_hbm, o_ref, gate, gain, whole, sems):
+    made = copies([(gate_hbm, gate), (gain_hbm, gain)], sems)
     take_pieces((p0, p1, p2, p3), whole, PLANS["A"])
-    (x,) = orthogonalize(whole[...])
+    o_ref[...] = steps(normalized(whole[...]), FIRST_STEPS)
+    for copy in made:
+        copy.wait()
+
+
+def first_update_kernel(x_ref, w_hbm, o_ref, w, sems):
+    (cw,) = copies([(w_hbm.at[0, 2], w)], sems)
+    x = steps(x_ref[...], NS_STEPS - FIRST_STEPS)
     cw.wait()
     o_ref[...] = updated(w[...], x)
-    for copy in made:
-        copy.wait()
 
 
 def core():
@@ -191,7 +191,7 @@
     def _():
         take_pieces(pieces, whole, PLANS["C"])
 
-    (x,) = orthogonalize(whole[...])
+    x = steps(normalized(whole[...]), NS_STEPS)
     cw.wait()
     o_ref[...] = updated(w[...], x)
 
@@ -314,13 +314,20 @@
         return own[0], other[0], own[1], other[1]
 
     gains = gain.reshape(1, -1)
-    new_two, gate_here, gain_here = call(
+    x_two, gate_here, gain_here = call(
+        first_steps_kernel, 10,
+        out_shape=[matrix] + [jax.ShapeDtypeStruct(x.shape, x.dtype) for x in (gate, gains)],
+        in_specs=[VM] * 4 + [HBM] * 2,
+        out_specs=[VM] * 3,
+        scratch_shapes=[mat(BF), sems(2)],
+    )(*gathered(two), hbm(gate), hbm(gains))
+    new_two = call(
         first_update_kernel, 10,
-        out_shape=[matrix] + [jax.ShapeDtypeStruct(x.shape, x.dtype) for x in (gate, gains)],
-        in_specs=[VM] * 4 + [HBM] * 3,
-        out_specs=[VM] * 3,
-        scratch_shapes=[mat(BF), mat(BF), sems(3)],
-    )(*gathered(two), hbm(fast_weights), hbm(gate), hbm(gains))
+        out_shape=matrix,
+        in_specs=[VM, HBM],
+        out_specs=VM,
+        scratch_shapes=[mat(BF), sems(1)],
+    )(x_two, hbm(fast_weights))
     keep, got = [], []
     for b, c in zip(one, three):
         keep.append(jnp.where(core() == 0, b, c))

time: 69.3 us -> 69.2 us (level)
    pallas_call x7 -> x8, Pallas kernels: 20.5 us -> 20.3 us  [run(): pl.pallas_call(kernel, compiler_params=pltpu.CompilerParams(vmem_limit_by...]
where the time goes in v5:
time: 69.2 us; the launch traced here: 69 us
  starting transfers between devices  24.4 us (35%)
  waiting for transfers between devices  22.8 us (33%)
  Pallas kernels  20.3 us (29%)
  between operations  0.97 us (1%)
    ppermute x22, waiting for transfers between devices, swap(): return lax.ppermute(x, 'ctx', [(i, i ^ 1 << bit) for i in range(ctx)])  22.8 us
    ppermute x22, starting transfers between devices, swap(): return lax.ppermute(x, 'ctx', [(i, i ^ 1 << bit) for i in range(ctx)])  22.3 us
    pallas_call x8, Pallas kernels, run(): pl.pallas_call(kernel, compiler_params=pltpu.CompilerParams(vmem_limit_by...  20.3 us
    ppermute x2, starting transfers between devices, turn(): return lax.ppermute(x, 'head', [(i, (i + r) % heads) for i in range(heads)])  2.09 us
  transfers between devices with their start and end apart: 24, of which 12 were waited for; matrix products, arithmetic and copies ran while one was open for 1% of the time, Pallas kernels for 22%

profile of v5, /device:TPU:0, one launch (start us, length us, event | category | flops | bytes accessed | tf_op | source)
XLA Modules:
  0.0 69.0 jit_solution(5223772899327126985)
XLA Ops:
  0.6 2.9 %shard_map.86 = (bf16[256,512]{1,0:T(8,128)(2,1)S(1)}, bf16[256,512]{1,0:T(8,128)(2,1)S(1)}, f32[512,512]{1,0:T(8,128)S(1)}, f32[512,512]{1,0:T(8,128)S(1)}, bf1...) custom-call(bf16[512,512]{1,0:T(8,128)(2,1)} %k_hbm.1, ...), custom_call_target="tpu_custom_call" | custom-call | tf_op jit(solution)/shard_map/pallas_call | solution.py:249
  3.5 1.3 %shard_map.88 = (bf16[256,512]{1,0:T(8,128)(2,1)S(1)}, bf16[256,512]{1,0:T(8,128)(2,1)S(1)}, bf16[256,512]{1,0:T(8,128)(2,1)S(1)}, bf16[256,512]{1,0:T(8,128)(2,1)S(1)}) custom-call(bf16[512,512]{1,0:T(8,128)(2,1)S(1)} %get-tuple-element.26.k, bf16[512,512]{1,0:T(8,128)(2,1)S(1)} %get-tuple-element.27.w2, f32[512,512]{1,0:T(8,128)S(1)} %get-tuple-element.28.g1_ref, ...), custom_call_target="tpu_custom_call" | custom-call | tf_op jit(solution)/shard_map/pallas_call | solution.py:249
  4.8 0.6 collective-permute-start.8
  5.4 1.2 %collective-permute-done.8 = bf16[256,512]{1,0:T(8,128)(2,1)S(1)} collective-permute-done((bf16[256,512]{1,0:T(8,128)(2,1)S(1)}, bf16[256,512]{1,0:T(8,128)(2,1)S(1)}, u32[]{:S(2)}, u32[]{:S(2)}) %collective-permute-start.8) | collective-permute-done | bytes 262176 | tf_op jit(solution)/shard_map/ppermute | solution.py:256
  6.6 0.1 add_convert_fusion.6
  6.6 3.0 %collective-permute-start.9 = (bf16[128,512]{1,0:T(8,128)(2,1)S(1)}, bf16[128,512]{1,0:T(8,128)(2,1)S(1)}, u32[]{:S(2)}, u32[]{:S(2)}) collective-permute-start(bf16[128,512]{1,0:T(8,128)(2,1)S(1)} %get-tuple-element.45), channel_id=1, source_target_pairs={{0,8},{2,10},{4,12},{6,14},{8,0},{10,2},{12,4},{14,6},{16,24},{18,... | collective-permute-start | bytes 393224 | tf_op jit(solution)/shard_map/ppermute | solution.py:256
  9.6 0.0 collective-permute-start.13
  9.6 0.5 collective-permute-start
  10.1 3.3 %collective-permute-done.9 = bf16[128,512]{1,0:T(8,128)(2,1)S(1)} collective-permute-done((bf16[128,512]{1,0:T(8,128)(2,1)S(1)}, bf16[128,512]{1,0:T(8,128)(2,1)S(1)}, u32[]{:S(2)}, u32[]{:S(2)}) %collective-permute-start.9) | collective-permute-done | bytes 131104 | tf_op jit(solution)/shard_map/ppermute | solution.py:256
  13.4 1.7 %collective-permute-start.10 = (bf16[64,512]{1,0:T(8,128)(2,1)S(1)}, bf16[64,512]{1,0:T(8,128)(2,1)S(1)}, u32[]{:S(2)}, u32[]{:S(2)}) collective-permute-start(bf16[64,512]{1,0:T(8,128)(2,1)S(1)} %add_convert_fusion.11), channel_id=1, source_target_pairs={{0,4},{2,6},{4,0},{6,2},{8,12},{10,14},{12,8},{14,10},{16,20},{18,... | collective-permute-start | bytes 196616 | tf_op jit(solution)/shard_map/ppermute | solution.py:256
  15.2 0.0 collective-permute-done.13
  15.2 0.4 collective-permute-start.14
  15.6 2.8 %collective-permute-done.10 = bf16[64,512]{1,0:T(8,128)(2,1)S(1)} collective-permute-done((bf16[64,512]{1,0:T(8,128)(2,1)S(1)}, bf16[64,512]{1,0:T(8,128)(2,1)S(1)}, u32[]{:S(2)}, u32[]{:S(2)}) %collective-permute-start.10) | collective-permute-done | bytes 65568 | tf_op jit(solution)/shard_map/ppermute | solution.py:256
  18.5 2.8 %collective-permute-start.11 = (bf16[64,512]{1,0:T(8,128)(2,1)S(1)}, bf16[64,512]{1,0:T(8,128)(2,1)S(1)}, u32[]{:S(2)}, u32[]{:S(2)}) collective-permute-start(bf16[64,512]{1,0:T(8,128)(2,1)S(1)} %add_convert_fusion.10), channel_id=1, source_target_pairs={{0,16},{2,18},{4,20},{6,22},{8,24},{10,26},{12,28},{14,30},{16,0},... | collective-permute-start | bytes 196616 | tf_op jit(solution)/shard_map/ppermute | solution.py:256
  21.3 0.0 collective-permute-done.14
  21.3 0.1 add_convert_fusion.2
  21.4 1.6 %collective-permute-start.15 = (bf16[128,512]{1,0:T(8,128)(2,1)S(1)}, bf16[128,512]{1,0:T(8,128)(2,1)S(1)}, u32[]{:S(2)}, u32[]{:S(2)}) collective-permute-start(bf16[128,512]{1,0:T(8,128)(2,1)S(1)} %add_convert_fusion.2), channel_id=1, source_target_pairs={{0,8},{2,10},{4,12},{6,14},{8,0},{10,2},{12,4},{14,6},{16,24},{18,... | collective-permute-start | bytes 393224 | tf_op jit(solution)/shard_map/ppermute | solution.py:256
  23.0 0.8 %collective-permute-done.11 = bf16[64,512]{1,0:T(8,128)(2,1)S(1)} collective-permute-done((bf16[64,512]{1,0:T(8,128)(2,1)S(1)}, bf16[64,512]{1,0:T(8,128)(2,1)S(1)}, u32[]{:S(2)}, u32[]{:S(2)}) %collective-permute-start.11) | collective-permute-done | bytes 65568 | tf_op jit(solution)/shard_map/ppermute | solution.py:256
  23.9 1.3 %collective-permute-start.12 = (bf16[64,512]{1,0:T(8,128)(2,1)S(1)}, bf16[64,512]{1,0:T(8,128)(2,1)S(1)}, u32[]{:S(2)}, u32[]{:S(2)}) collective-permute-start(bf16[64,512]{1,0:T(8,128)(2,1)S(1)} %add_convert_fusion.9), channel_id=1, source_target_pairs={{0,4},{2,6},{4,0},{6,2},{8,12},{10,14},{12,8},{14,10},{16,20},{18,... | collective-permute-start | bytes 196616 | tf_op jit(solution)/shard_map/ppermute | solution.py:256
  25.2 1.2 %collective-permute-done.15 = bf16[128,512]{1,0:T(8,128)(2,1)S(1)} collective-permute-done((bf16[128,512]{1,0:T(8,128)(2,1)S(1)}, bf16[128,512]{1,0:T(8,128)(2,1)S(1)}, u32[]{:S(2)}, u32[]{:S(2)}) %collective-permute-start.15) | collective-permute-done | bytes 131104 | tf_op jit(solution)/shard_map/ppermute | solution.py:256
  26.5 1.7 %collective-permute-start.16 = (bf16[128,512]{1,0:T(8,128)(2,1)S(1)}, bf16[128,512]{1,0:T(8,128)(2,1)S(1)}, u32[]{:S(2)}, u32[]{:S(2)}) collective-permute-start(bf16[128,512]{1,0:T(8,128)(2,1)S(1)} %add_convert_fusion.1), channel_id=1, source_target_pairs={{0,16},{2,18},{4,20},{6,22},{8,24},{10,26},{12,28},{14,30},{16,0},... | collective-permute-start | bytes 393224 | tf_op jit(solution)/shard_map/ppermute | solution.py:256
  28.2 0.0 collective-permute-done
  28.2 0.1 add_convert_fusion.8
  28.2 0.9 %collective-permute-start.1 = (bf16[128,512]{1,0:T(8,128)(2,1)S(1)}, bf16[128,512]{1,0:T(8,128)(2,1)S(1)}, u32[]{:S(2)}, u32[]{:S(2)}) collective-permute-start(bf16[128,512]{1,0:T(8,128)(2,1)S(1)} %get-tuple-element.47), channel_id=1, source_target_pairs={{0,4},{2,6},{4,0},{6,2},{8,12},{10,14},{12,8},{14,10},{16,20},{18,... | collective-permute-start | bytes 393224 | tf_op jit(solution)/shard_map/ppermute | solution.py:256
  29.2 0.0 collective-permute-done.12
  29.2 4.7 %collective-permute-done.16 = bf16[128,512]{1,0:T(8,128)(2,1)S(1)} collective-permute-done((bf16[128,512]{1,0:T(8,128)(2,1)S(1)}, bf16[128,512]{1,0:T(8,128)(2,1)S(1)}, u32[]{:S(2)}, u32[]{:S(2)}) %collective-permute-start.16) | collective-permute-done | bytes 131104 | tf_op jit(solution)/shard_map/ppermute | solution.py:256
  33.9 0.1 broadcast_select_fusion.1
  34.0 1.2 %collective-permute-start.18 = (bf16[128,512]{1,0:T(8,128)(2,1)S(1)}, bf16[128,512]{1,0:T(8,128)(2,1)S(1)}, u32[]{:S(2)}, u32[]{:S(2)}) collective-permute-start(bf16[128,512]{1,0:T(8,128)(2,1)S(1)} %get-tuple-element.43), channel_id=1, source_target_pairs={{0,4},{2,6},{4,0},{6,2},{8,12},{10,14},{12,8},{14,10},{16,20},{18,... | collective-permute-start | bytes 393224 | tf_op jit(solution)/shard_map/ppermute | solution.py:256
  35.2 0.3 collective-permute-start.17
  35.5 0.0 collective-permute-done.1
  35.5 1.9 %collective-permute-start.2 = (bf16[64,512]{1,0:T(8,128)(2,1)S(1)}, bf16[64,512]{1,0:T(8,128)(2,1)S(1)}, u32[]{:S(2)}, u32[]{:S(2)}) collective-permute-start(bf16[64,512]{1,0:T(8,128)(2,1)S(1)} %add_convert_fusion.15), channel_id=1, source_target_pairs={{0,8},{2,10},{4,12},{6,14},{8,0},{10,2},{12,4},{14,6},{16,24},{18,... | collective-permute-start | bytes 196616 | tf_op jit(solution)/shard_map/ppermute | solution.py:256
  37.4 0.0 collective-permute-start.19
  37.4 2.8 %collective-permute-done.17 = bf16[128,512]{1,0:T(8,128)(2,1)S(1)} collective-permute-done((bf16[128,512]{1,0:T(8,128)(2,1)S(1)}, bf16[128,512]{1,0:T(8,128)(2,1)S(1)}, u32[]{:S(2)}, u32[]{:S(2)}) %collective-permute-start.17) | collective-permute-done | bytes 131104 | tf_op jit(solution)/shard_map/ppermute | solution.py:256
  40.2 0.0 collective-permute-done.18
  40.3 0.1 collective-permute-start.20
  40.3 0.6 collective-permute-done.2
  41.0 1.5 %collective-permute-start.3 = (bf16[64,512]{1,0:T(8,128)(2,1)S(1)}, bf16[64,512]{1,0:T(8,128)(2,1)S(1)}, u32[]{:S(2)}, u32[]{:S(2)}) collective-permute-start(bf16[64,512]{1,0:T(8,128)(2,1)S(1)} %add_convert_fusion.14), channel_id=1, source_target_pairs={{0,16},{2,18},{4,20},{6,22},{8,24},{10,26},{12,28},{14,30},{16,0},... | collective-permute-start | bytes 196616 | tf_op jit(solution)/shard_map/ppermute | solution.py:256
  42.5 1.5 %collective-permute-start.21 = (bf16[256,512]{1,0:T(8,128)(2,1)S(1)}, bf16[256,512]{1,0:T(8,128)(2,1)S(1)}, u32[]{:S(2)}, u32[]{:S(2)}) collective-permute-start(bf16[256,512]{1,0:T(8,128)(2,1)S(1)} %get-tuple-element.37), channel_id=1, source_target_pairs={{0,1},{1,0},{2,3},{3,2},{4,5},{5,4},{6,7},{7,6},{8,9},{9,8},{10,11... | collective-permute-start | bytes 786440 | tf_op jit(solution)/shard_map/ppermute | solution.py:259
  44.0 0.0 collective-permute-done.19.p1
  44.0 0.0 collective-permute-done.20.p3
  44.0 5.5 %shard_map.89.mine = bf16[512,512]{1,0:T(8,128)(2,1)S(1)} custom-call(bf16[128,512]{1,0:T(8,128)(2,1)S(1)} %get-tuple-element.51.p0, bf16[128,512]{1,0:T(8,128)(2,1)S(1)} %get-tuple-element.49.p2, bf16[128,512]{1,0:T(8,128)(2,1)S(1)} %collective-permute-done.19.p1, bf16[128,512]{1,0:T(8,128)(2,1)S(1)} %collective-permute-done.20.p3, ...), custom_call_target="tpu_custom_call" | custom-call | tf_op jit(solution)/shard_map/pallas_call | solution.py:249
  49.5 0.1 collective-permute-start.23
  49.5 0.0 collective-permute-done.3
  49.6 1.4 %collective-permute-start.4 = (bf16[64,512]{1,0:T(8,128)(2,1)S(1)}, bf16[64,512]{1,0:T(8,128)(2,1)S(1)}, u32[]{:S(2)}, u32[]{:S(2)}) collective-permute-start(bf16[64,512]{1,0:T(8,128)(2,1)S(1)} %add_convert_fusion.13), channel_id=1, source_target_pairs={{0,8},{2,10},{4,12},{6,14},{8,0},{10,2},{12,4},{14,6},{16,24},{18,... | collective-permute-start | bytes 196616 | tf_op jit(solution)/shard_map/ppermute | solution.py:256
  51.0 3.2 %collective-permute-done.4 = bf16[64,512]{1,0:T(8,128)(2,1)S(1)} collective-permute-done((bf16[64,512]{1,0:T(8,128)(2,1)S(1)}, bf16[64,512]{1,0:T(8,128)(2,1)S(1)}, u32[]{:S(2)}, u32[]{:S(2)}) %collective-permute-start.4) | collective-permute-done | bytes 65568 | tf_op jit(solution)/shard_map/ppermute | solution.py:256
  54.1 1.2 %collective-permute-start.6 = (bf16[128,512]{1,0:T(8,128)(2,1)S(1)}, bf16[128,512]{1,0:T(8,128)(2,1)S(1)}, u32[]{:S(2)}, u32[]{:S(2)}) collective-permute-start(bf16[128,512]{1,0:T(8,128)(2,1)S(1)} %pad_maximum_fusion.p0), channel_id=1, source_target_pairs={{0,4},{2,6},{4,0},{6,2},{8,12},{10,14},{12,8},{14,10},{16,20},{18,... | collective-permute-start | bytes 393224 | tf_op jit(solution)/shard_map/ppermute | solution.py:256
  55.4 0.0 collective-permute-done.21.refs_1_
  55.4 2.4 %shard_map.91 = (bf16[256,512]{1,0:T(8,128)(2,1)S(1)}, bf16[256,512]{1,0:T(8,128)(2,1)S(1)}) custom-call(bf16[1,3,512,512]{3,2,1,0:T(8,128)(2,1)} %w_hbm.7, bf16[256,512]{1,0:T(8,128)(2,1)S(1)} %get-tuple-element.36.refs_0_, bf16[256,512]{1,0:T(8,128)(2,1)S(1)} %collective-permute-done.21.refs_1_), custom_call_target="tpu_custom_call" | custom-call | tf_op jit(solution)/shard_map/pallas_call | solution.py:249
  57.8 0.6 collective-permute-start.22
  58.4 0.0 collective-permute-start.5
  58.4 0.8 %collective-permute-done.6.p2 = bf16[128,512]{1,0:T(8,128)(2,1)S(1)} collective-permute-done((bf16[128,512]{1,0:T(8,128)(2,1)S(1)}, bf16[128,512]{1,0:T(8,128)(2,1)S(1)}, u32[]{:S(2)}, u32[]{:S(2)}) %collective-permute-start.6) | collective-permute-done | bytes 131104 | tf_op jit(solution)/shard_map/ppermute | solution.py:256
  59.2 0.0 collective-permute-start.7
  59.2 0.5 collective-permute-done.5.p1
  59.7 0.8 %collective-permute-done.7.p3 = bf16[128,512]{1,0:T(8,128)(2,1)S(1)} collective-permute-done((bf16[128,512]{1,0:T(8,128)(2,1)S(1)}, bf16[128,512]{1,0:T(8,128)(2,1)S(1)}, u32[]{:S(2)}, u32[]{:S(2)}) %collective-permute-start.7) | collective-permute-done | bytes 131104 | tf_op jit(solution)/shard_map/ppermute | solution.py:256
  60.6 4.3 %shard_map.87 = (bf16[512,512]{1,0:T(8,128)(2,1)S(1)}, bf16[256,1024]{1,0:T(8,128)(2,1)S(1)}, f32[1,1024]{1,0:T(1,128)S(1)}) custom-call(bf16[128,512]{1,0:T(8,128)(2,1)S(1)} %pad_maximum_fusion.p0, bf16[128,512]{1,0:T(8,128)(2,1)S(1)} %collective-permute-done.5.p1, bf16[128,512]{1,0:T(8,128)(2,1)S(1)} %collective-permute-done.6.p2, ...), custom_call_target="tpu_custom_call" | custom-call | tf_op jit(solution)/shard_map/pallas_call | solution.py:249
  64.8 1.3 %shard_map.90.two = bf16[512,512]{1,0:T(8,128)(2,1)S(1)} custom-call(bf16[512,512]{1,0:T(8,128)(2,1)S(1)} %get-tuple-element.35.x_ref, bf16[1,3,512,512]{3,2,1,0:T(8,128)(2,1)} %w_hbm.7), custom_call_target="tpu_custom_call" | custom-call | tf_op jit(solution)/shard_map/pallas_call | solution.py:249
  66.2 0.0 collective-permute-done.22.refs_1_
  66.2 1.9 %shard_map.92 = (bf16[256,1024]{1,0:T(8,128)(2,1)}, bf16[1,3,512,512]{3,2,1,0:T(8,128)(2,1)}) custom-call(bf16[256,1024]{1,0:T(8,128)(2,1)S(1)} %get-tuple-element.24.gate, f32[1,1024]{1,0:T(1,128)S(1)} %get-tuple-element.25.gain, bf16[512,512]{1,0:T(8,128)(2,1)S(1)} %shard_map.89.mine, bf16[512,512]{1,0:T(8,128)(2,1)S(1)} %shard_map.90.two, ...), custom_call_target="tpu_custom_call" | custom-call | tf_op jit(solution)/shard_map/pallas_call | solution.py:249
  68.0 0.0 collective-permute-done.23.theirs
  68.1 0.8 %shard_map.93 = bf16[1,3,512,512]{3,2,1,0:T(8,128)(2,1)} custom-call(bf16[512,512]{1,0:T(8,128)(2,1)S(1)} %collective-permute-done.23.theirs, bf16[1,3,512,512]{3,2,1,0:T(8,128)(2,1)} %get-tuple-element.41.partial), custom_call_target="tpu_custom_call", output_to_operand_aliasing={{}: (1, {})} | custom-call | tf_op jit(solution)/shard_map/pallas_call | solution.py:249
  (11 shorter events, 0.3 us)
Async XLA Ops:
  4.8 1.7 %collective-permute-start.8 = (bf16[256,512]{1,0:T(8,128)(2,1)S(1)}, bf16[256,512]{1,0:T(8,128)(2,1)S(1)}, u32[]{:S(2)}, u32[]{:S(2)}) collective-permute-start(bf16[256,512]{1,0:T(8,128)(2,1)S(1)} %get-tuple-element.32), channel_id=1, source_target_pairs={{0,2},{2,0},{4,6},{6,4},{8,10},{10,8},{12,14},{14,12},{16,18},{18,... | collective-permute-start | bytes 786440 | tf_op jit(solution)/shard_map/ppermute | solution.py:256
  6.6 6.8 %collective-permute-start.9 = (bf16[128,512]{1,0:T(8,128)(2,1)S(1)}, bf16[128,512]{1,0:T(8,128)(2,1)S(1)}, u32[]{:S(2)}, u32[]{:S(2)}) collective-permute-start(bf16[128,512]{1,0:T(8,128)(2,1)S(1)} %get-tuple-element.45), channel_id=1, source_target_pairs={{0,8},{2,10},{4,12},{6,14},{8,0},{10,2},{12,4},{14,6},{16,24},{18,... | collective-permute-start | bytes 393224 | tf_op jit(solution)/shard_map/ppermute | solution.py:256
  9.6 5.5 %collective-permute-start.13 = (bf16[256,512]{1,0:T(8,128)(2,1)S(1)}, bf16[256,512]{1,0:T(8,128)(2,1)S(1)}, u32[]{:S(2)}, u32[]{:S(2)}) collective-permute-start(bf16[256,512]{1,0:T(8,128)(2,1)S(1)} %get-tuple-element.34), channel_id=1, source_target_pairs={{0,2},{2,0},{4,6},{6,4},{8,10},{10,8},{12,14},{14,12},{16,18},{18,... | collective-permute-start | bytes 786440 | tf_op jit(solution)/shard_map/ppermute | solution.py:256
  9.6 18.5 %collective-permute-start = (bf16[256,512]{1,0:T(8,128)(2,1)S(1)}, bf16[256,512]{1,0:T(8,128)(2,1)S(1)}, u32[]{:S(2)}, u32[]{:S(2)}) collective-permute-start(bf16[256,512]{1,0:T(8,128)(2,1)S(1)} %get-tuple-element.23), channel_id=1, source_target_pairs={{0,2},{2,0},{4,6},{6,4},{8,10},{10,8},{12,14},{14,12},{16,18},{18,... | collective-permute-start | bytes 786440 | tf_op jit(solution)/shard_map/ppermute | solution.py:256
  13.4 5.0 %collective-permute-start.10 = (bf16[64,512]{1,0:T(8,128)(2,1)S(1)}, bf16[64,512]{1,0:T(8,128)(2,1)S(1)}, u32[]{:S(2)}, u32[]{:S(2)}) collective-permute-start(bf16[64,512]{1,0:T(8,128)(2,1)S(1)} %add_convert_fusion.11), channel_id=1, source_target_pairs={{0,4},{2,6},{4,0},{6,2},{8,12},{10,14},{12,8},{14,10},{16,20},{18,... | collective-permute-start | bytes 196616 | tf_op jit(solution)/shard_map/ppermute | solution.py:256
  15.2 6.1 %collective-permute-start.14 = (bf16[128,512]{1,0:T(8,128)(2,1)S(1)}, bf16[128,512]{1,0:T(8,128)(2,1)S(1)}, u32[]{:S(2)}, u32[]{:S(2)}) collective-permute-start(bf16[128,512]{1,0:T(8,128)(2,1)S(1)} %add_convert_fusion.3), channel_id=1, source_target_pairs={{0,4},{2,6},{4,0},{6,2},{8,12},{10,14},{12,8},{14,10},{16,20},{18,... | collective-permute-start | bytes 393224 | tf_op jit(solution)/shard_map/ppermute | solution.py:256
  18.5 5.3 %collective-permute-start.11 = (bf16[64,512]{1,0:T(8,128)(2,1)S(1)}, bf16[64,512]{1,0:T(8,128)(2,1)S(1)}, u32[]{:S(2)}, u32[]{:S(2)}) collective-permute-start(bf16[64,512]{1,0:T(8,128)(2,1)S(1)} %add_convert_fusion.10), channel_id=1, source_target_pairs={{0,16},{2,18},{4,20},{6,22},{8,24},{10,26},{12,28},{14,30},{16,0},... | collective-permute-start | bytes 196616 | tf_op jit(solution)/shard_map/ppermute | solution.py:256
  21.4 5.0 %collective-permute-start.15 = (bf16[128,512]{1,0:T(8,128)(2,1)S(1)}, bf16[128,512]{1,0:T(8,128)(2,1)S(1)}, u32[]{:S(2)}, u32[]{:S(2)}) collective-permute-start(bf16[128,512]{1,0:T(8,128)(2,1)S(1)} %add_convert_fusion.2), channel_id=1, source_target_pairs={{0,8},{2,10},{4,12},{6,14},{8,0},{10,2},{12,4},{14,6},{16,24},{18,... | collective-permute-start | bytes 393224 | tf_op jit(solution)/shard_map/ppermute | solution.py:256
  23.9 5.3 %collective-permute-start.12 = (bf16[64,512]{1,0:T(8,128)(2,1)S(1)}, bf16[64,512]{1,0:T(8,128)(2,1)S(1)}, u32[]{:S(2)}, u32[]{:S(2)}) collective-permute-start(bf16[64,512]{1,0:T(8,128)(2,1)S(1)} %add_convert_fusion.9), channel_id=1, source_target_pairs={{0,4},{2,6},{4,0},{6,2},{8,12},{10,14},{12,8},{14,10},{16,20},{18,... | collective-permute-start | bytes 196616 | tf_op jit(solution)/shard_map/ppermute | solution.py:256
  26.5 7.4 %collective-permute-start.16 = (bf16[128,512]{1,0:T(8,128)(2,1)S(1)}, bf16[128,512]{1,0:T(8,128)(2,1)S(1)}, u32[]{:S(2)}, u32[]{:S(2)}) collective-permute-start(bf16[128,512]{1,0:T(8,128)(2,1)S(1)} %add_convert_fusion.1), channel_id=1, source_target_pairs={{0,16},{2,18},{4,20},{6,22},{8,24},{10,26},{12,28},{14,30},{16,0},... | collective-permute-start | bytes 393224 | tf_op jit(solution)/shard_map/ppermute | solution.py:256
  28.2 7.3 %collective-permute-start.1 = (bf16[128,512]{1,0:T(8,128)(2,1)S(1)}, bf16[128,512]{1,0:T(8,128)(2,1)S(1)}, u32[]{:S(2)}, u32[]{:S(2)}) collective-permute-start(bf16[128,512]{1,0:T(8,128)(2,1)S(1)} %get-tuple-element.47), channel_id=1, source_target_pairs={{0,4},{2,6},{4,0},{6,2},{8,12},{10,14},{12,8},{14,10},{16,20},{18,... | collective-permute-start | bytes 393224 | tf_op jit(solution)/shard_map/ppermute | solution.py:256
  34.0 6.3 %collective-permute-start.18 = (bf16[128,512]{1,0:T(8,128)(2,1)S(1)}, bf16[128,512]{1,0:T(8,128)(2,1)S(1)}, u32[]{:S(2)}, u32[]{:S(2)}) collective-permute-start(bf16[128,512]{1,0:T(8,128)(2,1)S(1)} %get-tuple-element.43), channel_id=1, source_target_pairs={{0,4},{2,6},{4,0},{6,2},{8,12},{10,14},{12,8},{14,10},{16,20},{18,... | collective-permute-start | bytes 393224 | tf_op jit(solution)/shard_map/ppermute | solution.py:256
  35.2 5.0 %collective-permute-start.17 = (bf16[128,512]{1,0:T(8,128)(2,1)S(1)}, bf16[128,512]{1,0:T(8,128)(2,1)S(1)}, u32[]{:S(2)}, u32[]{:S(2)}) collective-permute-start(bf16[128,512]{1,0:T(8,128)(2,1)S(1)} %get-tuple-element.50), channel_id=1, source_target_pairs={{0,8},{2,10},{4,12},{6,14},{8,0},{10,2},{12,4},{14,6},{16,24},{18,... | collective-permute-start | bytes 393224 | tf_op jit(solution)/shard_map/ppermute | solution.py:256
  35.5 5.4 %collective-permute-start.2 = (bf16[64,512]{1,0:T(8,128)(2,1)S(1)}, bf16[64,512]{1,0:T(8,128)(2,1)S(1)}, u32[]{:S(2)}, u32[]{:S(2)}) collective-permute-start(bf16[64,512]{1,0:T(8,128)(2,1)S(1)} %add_convert_fusion.15), channel_id=1, source_target_pairs={{0,8},{2,10},{4,12},{6,14},{8,0},{10,2},{12,4},{14,6},{16,24},{18,... | collective-permute-start | bytes 196616 | tf_op jit(solution)/shard_map/ppermute | solution.py:256
  37.4 6.6 %collective-permute-start.19 = (bf16[128,512]{1,0:T(8,128)(2,1)S(1)}, bf16[128,512]{1,0:T(8,128)(2,1)S(1)}, u32[]{:S(2)}, u32[]{:S(2)}) collective-permute-start(bf16[128,512]{1,0:T(8,128)(2,1)S(1)} %get-tuple-element.42), channel_id=1, source_target_pairs={{0,2},{2,0},{4,6},{6,4},{8,10},{10,8},{12,14},{14,12},{16,18},{18,... | collective-permute-start | bytes 393224 | tf_op jit(solution)/shard_map/ppermute | solution.py:256
  40.3 3.7 %collective-permute-start.20 = (bf16[128,512]{1,0:T(8,128)(2,1)S(1)}, bf16[128,512]{1,0:T(8,128)(2,1)S(1)}, u32[]{:S(2)}, u32[]{:S(2)}) collective-permute-start(bf16[128,512]{1,0:T(8,128)(2,1)S(1)} %get-tuple-element.48), channel_id=1, source_target_pairs={{0,2},{2,0},{4,6},{6,4},{8,10},{10,8},{12,14},{14,12},{16,18},{18,... | collective-permute-start | bytes 393224 | tf_op jit(solution)/shard_map/ppermute | solution.py:256
  41.0 8.6 %collective-permute-start.3 = (bf16[64,512]{1,0:T(8,128)(2,1)S(1)}, bf16[64,512]{1,0:T(8,128)(2,1)S(1)}, u32[]{:S(2)}, u32[]{:S(2)}) collective-permute-start(bf16[64,512]{1,0:T(8,128)(2,1)S(1)} %add_convert_fusion.14), channel_id=1, source_target_pairs={{0,16},{2,18},{4,20},{6,22},{8,24},{10,26},{12,28},{14,30},{16,0},... | collective-permute-start | bytes 196616 | tf_op jit(solution)/shard_map/ppermute | solution.py:256
  42.5 12.9 %collective-permute-start.21 = (bf16[256,512]{1,0:T(8,128)(2,1)S(1)}, bf16[256,512]{1,0:T(8,128)(2,1)S(1)}, u32[]{:S(2)}, u32[]{:S(2)}) collective-permute-start(bf16[256,512]{1,0:T(8,128)(2,1)S(1)} %get-tuple-element.37), channel_id=1, source_target_pairs={{0,1},{1,0},{2,3},{3,2},{4,5},{5,4},{6,7},{7,6},{8,9},{9,8},{10,11... | collective-permute-start | bytes 786440 | tf_op jit(solution)/shard_map/ppermute | solution.py:259
  49.5 18.6 %collective-permute-start.23 = (bf16[512,512]{1,0:T(8,128)(2,1)S(1)}, bf16[512,512]{1,0:T(8,128)(2,1)S(1)}, u32[]{:S(2)}, u32[]{:S(2)}) collective-permute-start(bf16[512,512]{1,0:T(8,128)(2,1)S(1)} %shard_map.89.mine), channel_id=1, source_target_pairs={{0,2},{2,0},{4,6},{6,4},{8,10},{10,8},{12,14},{14,12},{16,18},{18,... | collective-permute-start | bytes 1572872 | tf_op jit(solution)/shard_map/ppermute | solution.py:256
  49.6 4.5 %collective-permute-start.4 = (bf16[64,512]{1,0:T(8,128)(2,1)S(1)}, bf16[64,512]{1,0:T(8,128)(2,1)S(1)}, u32[]{:S(2)}, u32[]{:S(2)}) collective-permute-start(bf16[64,512]{1,0:T(8,128)(2,1)S(1)} %add_convert_fusion.13), channel_id=1, source_target_pairs={{0,8},{2,10},{4,12},{6,14},{8,0},{10,2},{12,4},{14,6},{16,24},{18,... | collective-permute-start | bytes 196616 | tf_op jit(solution)/shard_map/ppermute | solution.py:256
  54.1 5.1 %collective-permute-start.6 = (bf16[128,512]{1,0:T(8,128)(2,1)S(1)}, bf16[128,512]{1,0:T(8,128)(2,1)S(1)}, u32[]{:S(2)}, u32[]{:S(2)}) collective-permute-start(bf16[128,512]{1,0:T(8,128)(2,1)S(1)} %pad_maximum_fusion.p0), channel_id=1, source_target_pairs={{0,4},{2,6},{4,0},{6,2},{8,12},{10,14},{12,8},{14,10},{16,20},{18,... | collective-permute-start | bytes 393224 | tf_op jit(solution)/shard_map/ppermute | solution.py:256
  57.8 8.3 %collective-permute-start.22 = (bf16[256,512]{1,0:T(8,128)(2,1)S(1)}, bf16[256,512]{1,0:T(8,128)(2,1)S(1)}, u32[]{:S(2)}, u32[]{:S(2)}) collective-permute-start(bf16[256,512]{1,0:T(8,128)(2,1)S(1)} %get-tuple-element.39), channel_id=1, source_target_pairs={{0,1},{1,0},{2,3},{3,2},{4,5},{5,4},{6,7},{7,6},{8,9},{9,8},{10,11... | collective-permute-start | bytes 786440 | tf_op jit(solution)/shard_map/ppermute | solution.py:259
  58.4 1.3 %collective-permute-start.5 = (bf16[128,512]{1,0:T(8,128)(2,1)S(1)}, bf16[128,512]{1,0:T(8,128)(2,1)S(1)}, u32[]{:S(2)}, u32[]{:S(2)}) collective-permute-start(bf16[128,512]{1,0:T(8,128)(2,1)S(1)} %pad_maximum_fusion.p0), channel_id=1, source_target_pairs={{0,2},{2,0},{4,6},{6,4},{8,10},{10,8},{12,14},{14,12},{16,18},{18,... | collective-permute-start | bytes 393224 | tf_op jit(solution)/shard_map/ppermute | solution.py:256
  59.2 1.3 %collective-permute-start.7 = (bf16[128,512]{1,0:T(8,128)(2,1)S(1)}, bf16[128,512]{1,0:T(8,128)(2,1)S(1)}, u32[]{:S(2)}, u32[]{:S(2)}) collective-permute-start(bf16[128,512]{1,0:T(8,128)(2,1)S(1)} %collective-permute-done.6.p2), channel_id=1, source_target_pairs={{0,2},{2,0},{4,6},{6,4},{8,10},{10,8},{12,14},{14,12},{16,18},{18,... | collective-permute-start | bytes 393224 | tf_op jit(solution)/shard_map/ppermute | solution.py:256

commit v6 on v5

--- a/solution.py
+++ b/solution.py
@@ -179,8 +179,8 @@
     return lax.axis_index("ctx") & 1
 
 
-def pair_update_kernel(p0, p2, p1, p3, w_hbm, o_ref, w, whole, sems):
-    (cw,) = copies([(w_hbm.at[0, core()], w)], sems)
+def pair_update_kernel(p0, p2, p1, p3, w_hbm, two, o_ref, o_hbm, w, whole, sems):
+    cw, c2 = copies([(w_hbm.at[0, core()], w), (two, o_hbm.at[0, 2])], sems)
     pieces = (p0, p1, p2, p3)
 
     @pl.when(core() == 0)
@@ -194,6 +194,7 @@
     x = steps(normalized(whole[...]), NS_STEPS)
     cw.wait()
     o_ref[...] = updated(w[...], x)
+    c2.wait()
 
 
 def last_kernel(theirs, partial, o_hbm, sems):
@@ -216,9 +217,10 @@
         out[...] = (dot(h, w2[...]) * scale).astype(BF)
 
 
-def norm_kernel(heads, gate, gain, mine, two, *refs):
+def norm_kernel(heads, gate, gain, mine, partial, *refs):
+    del partial
     reads, (out, o_hbm, sems) = refs[:heads], refs[heads:]
-    made = copies([(mine, o_hbm.at[0, core()]), (two, o_hbm.at[0, 2])], sems)
+    made = copies([(mine, o_hbm.at[0, core()])], sems)
     width = reads[0].shape[-1]
     me = lax.axis_index("head")
     for r, read in enumerate(reads):
@@ -333,13 +335,13 @@
         keep.append(jnp.where(core() == 0, b, c))
         give = lax.select_n(jnp.broadcast_to(core() == 0, b.shape), b, c)
         got.append(swap(give, 0))
-    mine = call(
+    mine, new_weights = call(
         pair_update_kernel, 10,
-        out_shape=matrix,
-        in_specs=[VM] * 4 + [HBM],
-        out_specs=VM,
-        scratch_shapes=[mat(BF), mat(BF), sems(1)],
-    )(*keep, *got, hbm(fast_weights))
+        out_shape=[matrix, jax.ShapeDtypeStruct(fast_weights.shape, BF)],
+        in_specs=[VM] * 4 + [HBM, VM],
+        out_specs=[VM, HBM],
+        scratch_shapes=[mat(BF), mat(BF), sems(2)],
+    )(*keep, *got, hbm(fast_weights), new_two)
     theirs = swap(mine, 0)
 
     reads = call(
@@ -356,10 +358,11 @@
             jax.ShapeDtypeStruct(queries.shape, BF),
             jax.ShapeDtypeStruct(fast_weights.shape, BF),
         ],
-        in_specs=[VM] * (4 + heads),
+        in_specs=[VM] * 3 + [HBM] + [VM] * heads,
         out_specs=[VM, HBM],
-        scratch_shapes=[sems(2)],
-    )(gate_here, gain_here, mine, new_two, *back)
+        scratch_shapes=[sems(1)],
+        input_output_aliases={3: 1},
+    )(gate_here, gain_here, mine, new_weights, *back)
     new_weights = call(
         last_kernel, 4,
         out_shape=jax.ShapeDtypeStruct(fast_weights.shape, BF),

time: 69.2 us -> 69.5 us (level)
  starting transfers between devices: 24.4 us -> 29.2 us
  waiting for transfers between devices: 22.8 us -> 18.5 us
    ppermute x22, waiting for transfers between devices: 22.8 us -> 10.4 us  [swap(): return lax.ppermute(x, 'ctx', [(i, i ^ 1 << bit) for i in range(ctx)])]
    ppermute x2, waiting for transfers between devices: 0.01 us -> 8.08 us  [turn(): return lax.ppermute(x, 'head', [(i, (i + r) % heads) for i in range(heads)])]
    ppermute x22, starting transfers between devices: 22.3 us -> 27.1 us  [swap(): return lax.ppermute(x, 'ctx', [(i, i ^ 1 << bit) for i in range(ctx)])]
  transfers between devices with their start and end apart: 24 -> 24, of which waited for: 12 -> 10; matrix products, arithmetic and copies ran while one was open for 1% -> 1% of each run, Pallas kernels for 22% -> 22%
where the time goes in v6:
time: 69.5 us; the launch traced here: 69.4 us
  starting transfers between devices  29.2 us (42%)
  Pallas kernels  20.2 us (29%)
  waiting for transfers between devices  18.5 us (27%)
  between operations  0.97 us (1%)
    ppermute x22, starting transfers between devices, swap(): return lax.ppermute(x, 'ctx', [(i, i ^ 1 << bit) for i in range(ctx)])  27.1 us
    pallas_call x8, Pallas kernels, run(): pl.pallas_call(kernel, compiler_params=pltpu.CompilerParams(vmem_limit_by...  20.2 us
    ppermute x22, waiting for transfers between devices, swap(): return lax.ppermute(x, 'ctx', [(i, i ^ 1 << bit) for i in range(ctx)])  10.4 us
    ppermute x2, waiting for transfers between devices, turn(): return lax.ppermute(x, 'head', [(i, (i + r) % heads) for i in range(heads)])  8.08 us
    ppermute x2, starting transfers between devices, turn(): return lax.ppermute(x, 'head', [(i, (i + r) % heads) for i in range(heads)])  2.16 us
  transfers between devices with their start and end apart: 24, of which 10 were waited for; matrix products, arithmetic and copies ran while one was open for 1% of the time, Pallas kernels for 22%

profile of v6, /device:TPU:0, one launch (start us, length us, event | category | flops | bytes accessed | tf_op | source)
XLA Modules:
  0.0 69.4 jit_solution(9179246160222419723)
XLA Ops:
  0.6 2.9 %shard_map.86 = (bf16[256,512]{1,0:T(8,128)(2,1)S(1)}, bf16[256,512]{1,0:T(8,128)(2,1)S(1)}, f32[512,512]{1,0:T(8,128)S(1)}, f32[512,512]{1,0:T(8,128)S(1)}, bf1...) custom-call(bf16[512,512]{1,0:T(8,128)(2,1)} %k_hbm.1, ...), custom_call_target="tpu_custom_call" | custom-call | tf_op jit(solution)/shard_map/pallas_call | solution.py:251
  3.5 1.3 %shard_map.88 = (bf16[256,512]{1,0:T(8,128)(2,1)S(1)}, bf16[256,512]{1,0:T(8,128)(2,1)S(1)}, bf16[256,512]{1,0:T(8,128)(2,1)S(1)}, bf16[256,512]{1,0:T(8,128)(2,1)S(1)}) custom-call(bf16[512,512]{1,0:T(8,128)(2,1)S(1)} %get-tuple-element.28.k, bf16[512,512]{1,0:T(8,128)(2,1)S(1)} %get-tuple-element.29.w2, f32[512,512]{1,0:T(8,128)S(1)} %get-tuple-element.30.g1_ref, ...), custom_call_target="tpu_custom_call" | custom-call | tf_op jit(solution)/shard_map/pallas_call | solution.py:251
  4.8 0.6 collective-permute-start.13
  5.4 0.1 collective-permute-start.8
  5.5 0.4 collective-permute-start
  5.9 0.7 collective-permute-done.13
  6.6 2.9 %collective-permute-start.14 = (bf16[128,512]{1,0:T(8,128)(2,1)S(1)}, bf16[128,512]{1,0:T(8,128)(2,1)S(1)}, u32[]{:S(2)}, u32[]{:S(2)}) collective-permute-start(bf16[128,512]{1,0:T(8,128)(2,1)S(1)} %add_convert_fusion.3), channel_id=1, source_target_pairs={{0,4},{2,6},{4,0},{6,2},{8,12},{10,14},{12,8},{14,10},{16,20},{18,... | collective-permute-start | bytes 393224 | tf_op jit(solution)/shard_map/ppermute | solution.py:258
  9.5 0.0 collective-permute-done.8
  9.5 0.1 add_convert_fusion.6
  9.6 1.6 %collective-permute-start.9 = (bf16[128,512]{1,0:T(8,128)(2,1)S(1)}, bf16[128,512]{1,0:T(8,128)(2,1)S(1)}, u32[]{:S(2)}, u32[]{:S(2)}) collective-permute-start(bf16[128,512]{1,0:T(8,128)(2,1)S(1)} %get-tuple-element.49), channel_id=1, source_target_pairs={{0,8},{2,10},{4,12},{6,14},{8,0},{10,2},{12,4},{14,6},{16,24},{18,... | collective-permute-start | bytes 393224 | tf_op jit(solution)/shard_map/ppermute | solution.py:258
  11.2 0.0 collective-permute-done
  11.2 0.1 add_convert_fusion.8
  11.3 0.6 collective-permute-start.1
  11.9 1.5 %collective-permute-done.14 = bf16[128,512]{1,0:T(8,128)(2,1)S(1)} collective-permute-done((bf16[128,512]{1,0:T(8,128)(2,1)S(1)}, bf16[128,512]{1,0:T(8,128)(2,1)S(1)}, u32[]{:S(2)}, u32[]{:S(2)}) %collective-permute-start.14) | collective-permute-done | bytes 131104 | tf_op jit(solution)/shard_map/ppermute | solution.py:258
  13.4 0.1 add_convert_fusion.2
  13.4 2.6 %collective-permute-start.15 = (bf16[128,512]{1,0:T(8,128)(2,1)S(1)}, bf16[128,512]{1,0:T(8,128)(2,1)S(1)}, u32[]{:S(2)}, u32[]{:S(2)}) collective-permute-start(bf16[128,512]{1,0:T(8,128)(2,1)S(1)} %add_convert_fusion.2), channel_id=1, source_target_pairs={{0,8},{2,10},{4,12},{6,14},{8,0},{10,2},{12,4},{14,6},{16,24},{18,... | collective-permute-start | bytes 393224 | tf_op jit(solution)/shard_map/ppermute | solution.py:258
  16.1 0.3 collective-permute-done.1
  16.4 1.7 %collective-permute-start.2 = (bf16[64,512]{1,0:T(8,128)(2,1)S(1)}, bf16[64,512]{1,0:T(8,128)(2,1)S(1)}, u32[]{:S(2)}, u32[]{:S(2)}) collective-permute-start(bf16[64,512]{1,0:T(8,128)(2,1)S(1)} %add_convert_fusion.15), channel_id=1, source_target_pairs={{0,8},{2,10},{4,12},{6,14},{8,0},{10,2},{12,4},{14,6},{16,24},{18,... | collective-permute-start | bytes 196616 | tf_op jit(solution)/shard_map/ppermute | solution.py:258
  18.0 0.0 collective-permute-done.9
  18.1 1.6 %collective-permute-start.10 = (bf16[64,512]{1,0:T(8,128)(2,1)S(1)}, bf16[64,512]{1,0:T(8,128)(2,1)S(1)}, u32[]{:S(2)}, u32[]{:S(2)}) collective-permute-start(bf16[64,512]{1,0:T(8,128)(2,1)S(1)} %add_convert_fusion.11), channel_id=1, source_target_pairs={{0,4},{2,6},{4,0},{6,2},{8,12},{10,14},{12,8},{14,10},{16,20},{18,... | collective-permute-start | bytes 196616 | tf_op jit(solution)/shard_map/ppermute | solution.py:258
  19.6 1.1 %collective-permute-done.2 = bf16[64,512]{1,0:T(8,128)(2,1)S(1)} collective-permute-done((bf16[64,512]{1,0:T(8,128)(2,1)S(1)}, bf16[64,512]{1,0:T(8,128)(2,1)S(1)}, u32[]{:S(2)}, u32[]{:S(2)}) %collective-permute-start.2) | collective-permute-done | bytes 65568 | tf_op jit(solution)/shard_map/ppermute | solution.py:258
  20.7 2.7 %collective-permute-start.3 = (bf16[64,512]{1,0:T(8,128)(2,1)S(1)}, bf16[64,512]{1,0:T(8,128)(2,1)S(1)}, u32[]{:S(2)}, u32[]{:S(2)}) collective-permute-start(bf16[64,512]{1,0:T(8,128)(2,1)S(1)} %add_convert_fusion.14), channel_id=1, source_target_pairs={{0,16},{2,18},{4,20},{6,22},{8,24},{10,26},{12,28},{14,30},{16,0},... | collective-permute-start | bytes 196616 | tf_op jit(solution)/shard_map/ppermute | solution.py:258
  23.4 0.0 collective-permute-done.10
  23.4 1.6 %collective-permute-start.11 = (bf16[64,512]{1,0:T(8,128)(2,1)S(1)}, bf16[64,512]{1,0:T(8,128)(2,1)S(1)}, u32[]{:S(2)}, u32[]{:S(2)}) collective-permute-start(bf16[64,512]{1,0:T(8,128)(2,1)S(1)} %add_convert_fusion.10), channel_id=1, source_target_pairs={{0,16},{2,18},{4,20},{6,22},{8,24},{10,26},{12,28},{14,30},{16,0},... | collective-permute-start | bytes 196616 | tf_op jit(solution)/shard_map/ppermute | solution.py:258
  25.1 1.2 %collective-permute-done.3 = bf16[64,512]{1,0:T(8,128)(2,1)S(1)} collective-permute-done((bf16[64,512]{1,0:T(8,128)(2,1)S(1)}, bf16[64,512]{1,0:T(8,128)(2,1)S(1)}, u32[]{:S(2)}, u32[]{:S(2)}) %collective-permute-start.3) | collective-permute-done | bytes 65568 | tf_op jit(solution)/shard_map/ppermute | solution.py:258
  26.3 2.2 %collective-permute-start.4 = (bf16[64,512]{1,0:T(8,128)(2,1)S(1)}, bf16[64,512]{1,0:T(8,128)(2,1)S(1)}, u32[]{:S(2)}, u32[]{:S(2)}) collective-permute-start(bf16[64,512]{1,0:T(8,128)(2,1)S(1)} %add_convert_fusion.13), channel_id=1, source_target_pairs={{0,8},{2,10},{4,12},{6,14},{8,0},{10,2},{12,4},{14,6},{16,24},{18,... | collective-permute-start | bytes 196616 | tf_op jit(solution)/shard_map/ppermute | solution.py:258
  28.5 0.0 collective-permute-done.15
  28.5 4.0 %collective-permute-start.16 = (bf16[128,512]{1,0:T(8,128)(2,1)S(1)}, bf16[128,512]{1,0:T(8,128)(2,1)S(1)}, u32[]{:S(2)}, u32[]{:S(2)}) collective-permute-start(bf16[128,512]{1,0:T(8,128)(2,1)S(1)} %add_convert_fusion.1), channel_id=1, source_target_pairs={{0,16},{2,18},{4,20},{6,22},{8,24},{10,26},{12,28},{14,30},{16,0},... | collective-permute-start | bytes 393224 | tf_op jit(solution)/shard_map/ppermute | solution.py:258
  32.5 0.0 collective-permute-done.11
  32.6 1.6 %collective-permute-start.12 = (bf16[64,512]{1,0:T(8,128)(2,1)S(1)}, bf16[64,512]{1,0:T(8,128)(2,1)S(1)}, u32[]{:S(2)}, u32[]{:S(2)}) collective-permute-start(bf16[64,512]{1,0:T(8,128)(2,1)S(1)} %add_convert_fusion.9), channel_id=1, source_target_pairs={{0,4},{2,6},{4,0},{6,2},{8,12},{10,14},{12,8},{14,10},{16,20},{18,... | collective-permute-start | bytes 196616 | tf_op jit(solution)/shard_map/ppermute | solution.py:258
  34.2 0.0 collective-permute-done.4
  34.2 0.5 collective-permute-start.6
  34.7 2.6 %collective-permute-done.12 = bf16[64,512]{1,0:T(8,128)(2,1)S(1)} collective-permute-done((bf16[64,512]{1,0:T(8,128)(2,1)S(1)}, bf16[64,512]{1,0:T(8,128)(2,1)S(1)}, u32[]{:S(2)}, u32[]{:S(2)}) %collective-permute-start.12) | collective-permute-done | bytes 65568 | tf_op jit(solution)/shard_map/ppermute | solution.py:258
  37.4 0.0 collective-permute-done.16
  37.4 0.1 broadcast_select_fusion.1
  37.5 0.1 collective-permute-start.17
  37.5 1.4 %collective-permute-start.18 = (bf16[128,512]{1,0:T(8,128)(2,1)S(1)}, bf16[128,512]{1,0:T(8,128)(2,1)S(1)}, u32[]{:S(2)}, u32[]{:S(2)}) collective-permute-start(bf16[128,512]{1,0:T(8,128)(2,1)S(1)} %get-tuple-element.47), channel_id=1, source_target_pairs={{0,4},{2,6},{4,0},{6,2},{8,12},{10,14},{12,8},{14,10},{16,20},{18,... | collective-permute-start | bytes 393224 | tf_op jit(solution)/shard_map/ppermute | solution.py:258
  39.0 0.0 collective-permute-start.5
  39.0 0.5 collective-permute-start.19
  39.5 0.2 collective-permute-done.6.p2
  39.7 0.0 collective-permute-start.7
  39.7 2.8 %collective-permute-done.17 = bf16[128,512]{1,0:T(8,128)(2,1)S(1)} collective-permute-done((bf16[128,512]{1,0:T(8,128)(2,1)S(1)}, bf16[128,512]{1,0:T(8,128)(2,1)S(1)}, u32[]{:S(2)}, u32[]{:S(2)}) %collective-permute-start.17) | collective-permute-done | bytes 131104 | tf_op jit(solution)/shard_map/ppermute | solution.py:258
  42.5 0.1 collective-permute-done.18
  42.6 0.1 collective-permute-start.20
  42.7 1.6 %collective-permute-start.21 = (bf16[256,512]{1,0:T(8,128)(2,1)S(1)}, bf16[256,512]{1,0:T(8,128)(2,1)S(1)}, u32[]{:S(2)}, u32[]{:S(2)}) collective-permute-start(bf16[256,512]{1,0:T(8,128)(2,1)S(1)} %get-tuple-element.41), channel_id=1, source_target_pairs={{0,1},{1,0},{2,3},{3,2},{4,5},{5,4},{6,7},{7,6},{8,9},{9,8},{10,11... | collective-permute-start | bytes 786440 | tf_op jit(solution)/shard_map/ppermute | solution.py:261
  44.3 0.0 collective-permute-done.5.p1
  44.3 0.0 collective-permute-done.7.p3
  44.3 4.3 %shard_map.87 = (bf16[512,512]{1,0:T(8,128)(2,1)S(1)}, bf16[256,1024]{1,0:T(8,128)(2,1)S(1)}, f32[1,1024]{1,0:T(1,128)S(1)}) custom-call(bf16[128,512]{1,0:T(8,128)(2,1)S(1)} %pad_maximum_fusion.p0, bf16[128,512]{1,0:T(8,128)(2,1)S(1)} %collective-permute-done.5.p1, bf16[128,512]{1,0:T(8,128)(2,1)S(1)} %collective-permute-done.6.p2, ...), custom_call_target="tpu_custom_call" | custom-call | tf_op jit(solution)/shard_map/pallas_call | solution.py:251
  48.5 1.3 %shard_map.89.two = bf16[512,512]{1,0:T(8,128)(2,1)S(1)} custom-call(bf16[512,512]{1,0:T(8,128)(2,1)S(1)} %get-tuple-element.37.x_ref, bf16[1,3,512,512]{3,2,1,0:T(8,128)(2,1)} %w_hbm.7), custom_call_target="tpu_custom_call" | custom-call | tf_op jit(solution)/shard_map/pallas_call | solution.py:251
  49.9 0.0 collective-permute-done.19.p1
  49.9 0.0 collective-permute-done.20.p3
  49.9 5.5 %shard_map.90 = (bf16[512,512]{1,0:T(8,128)(2,1)S(1)}, bf16[1,3,512,512]{3,2,1,0:T(8,128)(2,1)}) custom-call(bf16[128,512]{1,0:T(8,128)(2,1)S(1)} %get-tuple-element.55.p0, bf16[128,512]{1,0:T(8,128)(2,1)S(1)} %get-tuple-element.53.p2, bf16[128,512]{1,0:T(8,128)(2,1)S(1)} %collective-permute-done.19.p1, bf16[128,512]{1,0:T(8,128)(2,1)S(1)} %collective-permute-done.20.p3, ...), custom_call_target="tpu_custom_call" | custom-call | tf_op jit(solution)/shard_map/pallas_call | solution.py:251
  55.4 0.2 collective-permute-start.23
  55.6 0.0 collective-permute-done.21.refs_1_
  55.6 2.4 %shard_map.91 = (bf16[256,512]{1,0:T(8,128)(2,1)S(1)}, bf16[256,512]{1,0:T(8,128)(2,1)S(1)}) custom-call(bf16[1,3,512,512]{3,2,1,0:T(8,128)(2,1)} %w_hbm.7, bf16[256,512]{1,0:T(8,128)(2,1)S(1)} %get-tuple-element.40.refs_0_, bf16[256,512]{1,0:T(8,128)(2,1)S(1)} %collective-permute-done.21.refs_1_), custom_call_target="tpu_custom_call" | custom-call | tf_op jit(solution)/shard_map/pallas_call | solution.py:251
  58.0 0.6 collective-permute-start.22
  58.6 8.1 %collective-permute-done.22.refs_1_ = bf16[256,512]{1,0:T(8,128)(2,1)S(1)} collective-permute-done((bf16[256,512]{1,0:T(8,128)(2,1)S(1)}, bf16[256,512]{1,0:T(8,128)(2,1)S(1)}, u32[]{:S(2)}, u32[]{:S(2)}) %collective-permute-start.22) | collective-permute-done | bytes 262176 | tf_op jit(solution)/shard_map/ppermute | solution.py:261
  66.7 1.7 %shard_map.92 = (bf16[256,1024]{1,0:T(8,128)(2,1)}, bf16[1,3,512,512]{3,2,1,0:T(8,128)(2,1)}) custom-call(bf16[256,1024]{1,0:T(8,128)(2,1)S(1)} %get-tuple-element.26.gate, f32[1,1024]{1,0:T(1,128)S(1)} %get-tuple-element.27.gain, bf16[512,512]{1,0:T(8,128)(2,1)S(1)} %get-tuple-element.38.mine, ...), custom_call_target="tpu_custom_call", output_to_operand_aliasing={{1}: (3, {})} | custom-call | tf_op jit(solution)/shard_map/pallas_call | solution.py:251
  68.4 0.0 collective-permute-done.23.theirs
  68.4 0.8 %shard_map.93 = bf16[1,3,512,512]{3,2,1,0:T(8,128)(2,1)} custom-call(bf16[512,512]{1,0:T(8,128)(2,1)S(1)} %collective-permute-done.23.theirs, bf16[1,3,512,512]{3,2,1,0:T(8,128)(2,1)} %get-tuple-element.45.partial), custom_call_target="tpu_custom_call", output_to_operand_aliasing={{}: (1, {})} | custom-call | tf_op jit(solution)/shard_map/pallas_call | solution.py:251
  (11 shorter events, 0.3 us)
Async XLA Ops:
  4.8 1.7 %collective-permute-start.13 = (bf16[256,512]{1,0:T(8,128)(2,1)S(1)}, bf16[256,512]{1,0:T(8,128)(2,1)S(1)}, u32[]{:S(2)}, u32[]{:S(2)}) collective-permute-start(bf16[256,512]{1,0:T(8,128)(2,1)S(1)} %get-tuple-element.36), channel_id=1, source_target_pairs={{0,2},{2,0},{4,6},{6,4},{8,10},{10,8},{12,14},{14,12},{16,18},{18,... | collective-permute-start | bytes 786440 | tf_op jit(solution)/shard_map/ppermute | solution.py:258
  5.4 4.1 %collective-permute-start.8 = (bf16[256,512]{1,0:T(8,128)(2,1)S(1)}, bf16[256,512]{1,0:T(8,128)(2,1)S(1)}, u32[]{:S(2)}, u32[]{:S(2)}) collective-permute-start(bf16[256,512]{1,0:T(8,128)(2,1)S(1)} %get-tuple-element.34), channel_id=1, source_target_pairs={{0,2},{2,0},{4,6},{6,4},{8,10},{10,8},{12,14},{14,12},{16,18},{18,... | collective-permute-start | bytes 786440 | tf_op jit(solution)/shard_map/ppermute | solution.py:258
  5.5 5.8 %collective-permute-start = (bf16[256,512]{1,0:T(8,128)(2,1)S(1)}, bf16[256,512]{1,0:T(8,128)(2,1)S(1)}, u32[]{:S(2)}, u32[]{:S(2)}) collective-permute-start(bf16[256,512]{1,0:T(8,128)(2,1)S(1)} %get-tuple-element.25), channel_id=1, source_target_pairs={{0,2},{2,0},{4,6},{6,4},{8,10},{10,8},{12,14},{14,12},{16,18},{18,... | collective-permute-start | bytes 786440 | tf_op jit(solution)/shard_map/ppermute | solution.py:258
  6.6 6.8 %collective-permute-start.14 = (bf16[128,512]{1,0:T(8,128)(2,1)S(1)}, bf16[128,512]{1,0:T(8,128)(2,1)S(1)}, u32[]{:S(2)}, u32[]{:S(2)}) collective-permute-start(bf16[128,512]{1,0:T(8,128)(2,1)S(1)} %add_convert_fusion.3), channel_id=1, source_target_pairs={{0,4},{2,6},{4,0},{6,2},{8,12},{10,14},{12,8},{14,10},{16,20},{18,... | collective-permute-start | bytes 393224 | tf_op jit(solution)/shard_map/ppermute | solution.py:258
  9.6 8.4 %collective-permute-start.9 = (bf16[128,512]{1,0:T(8,128)(2,1)S(1)}, bf16[128,512]{1,0:T(8,128)(2,1)S(1)}, u32[]{:S(2)}, u32[]{:S(2)}) collective-permute-start(bf16[128,512]{1,0:T(8,128)(2,1)S(1)} %get-tuple-element.49), channel_id=1, source_target_pairs={{0,8},{2,10},{4,12},{6,14},{8,0},{10,2},{12,4},{14,6},{16,24},{18,... | collective-permute-start | bytes 393224 | tf_op jit(solution)/shard_map/ppermute | solution.py:258
  11.3 5.0 %collective-permute-start.1 = (bf16[128,512]{1,0:T(8,128)(2,1)S(1)}, bf16[128,512]{1,0:T(8,128)(2,1)S(1)}, u32[]{:S(2)}, u32[]{:S(2)}) collective-permute-start(bf16[128,512]{1,0:T(8,128)(2,1)S(1)} %get-tuple-element.51), channel_id=1, source_target_pairs={{0,4},{2,6},{4,0},{6,2},{8,12},{10,14},{12,8},{14,10},{16,20},{18,... | collective-permute-start | bytes 393224 | tf_op jit(solution)/shard_map/ppermute | solution.py:258
  13.4 15.0 %collective-permute-start.15 = (bf16[128,512]{1,0:T(8,128)(2,1)S(1)}, bf16[128,512]{1,0:T(8,128)(2,1)S(1)}, u32[]{:S(2)}, u32[]{:S(2)}) collective-permute-start(bf16[128,512]{1,0:T(8,128)(2,1)S(1)} %add_convert_fusion.2), channel_id=1, source_target_pairs={{0,8},{2,10},{4,12},{6,14},{8,0},{10,2},{12,4},{14,6},{16,24},{18,... | collective-permute-start | bytes 393224 | tf_op jit(solution)/shard_map/ppermute | solution.py:258
  16.4 4.3 %collective-permute-start.2 = (bf16[64,512]{1,0:T(8,128)(2,1)S(1)}, bf16[64,512]{1,0:T(8,128)(2,1)S(1)}, u32[]{:S(2)}, u32[]{:S(2)}) collective-permute-start(bf16[64,512]{1,0:T(8,128)(2,1)S(1)} %add_convert_fusion.15), channel_id=1, source_target_pairs={{0,8},{2,10},{4,12},{6,14},{8,0},{10,2},{12,4},{14,6},{16,24},{18,... | collective-permute-start | bytes 196616 | tf_op jit(solution)/shard_map/ppermute | solution.py:258
  18.1 5.4 %collective-permute-start.10 = (bf16[64,512]{1,0:T(8,128)(2,1)S(1)}, bf16[64,512]{1,0:T(8,128)(2,1)S(1)}, u32[]{:S(2)}, u32[]{:S(2)}) collective-permute-start(bf16[64,512]{1,0:T(8,128)(2,1)S(1)} %add_convert_fusion.11), channel_id=1, source_target_pairs={{0,4},{2,6},{4,0},{6,2},{8,12},{10,14},{12,8},{14,10},{16,20},{18,... | collective-permute-start | bytes 196616 | tf_op jit(solution)/shard_map/ppermute | solution.py:258
  20.7 5.5 %collective-permute-start.3 = (bf16[64,512]{1,0:T(8,128)(2,1)S(1)}, bf16[64,512]{1,0:T(8,128)(2,1)S(1)}, u32[]{:S(2)}, u32[]{:S(2)}) collective-permute-start(bf16[64,512]{1,0:T(8,128)(2,1)S(1)} %add_convert_fusion.14), channel_id=1, source_target_pairs={{0,16},{2,18},{4,20},{6,22},{8,24},{10,26},{12,28},{14,30},{16,0},... | collective-permute-start | bytes 196616 | tf_op jit(solution)/shard_map/ppermute | solution.py:258
  23.4 9.1 %collective-permute-start.11 = (bf16[64,512]{1,0:T(8,128)(2,1)S(1)}, bf16[64,512]{1,0:T(8,128)(2,1)S(1)}, u32[]{:S(2)}, u32[]{:S(2)}) collective-permute-start(bf16[64,512]{1,0:T(8,128)(2,1)S(1)} %add_convert_fusion.10), channel_id=1, source_target_pairs={{0,16},{2,18},{4,20},{6,22},{8,24},{10,26},{12,28},{14,30},{16,0},... | collective-permute-start | bytes 196616 | tf_op jit(solution)/shard_map/ppermute | solution.py:258
  26.3 7.9 %collective-permute-start.4 = (bf16[64,512]{1,0:T(8,128)(2,1)S(1)}, bf16[64,512]{1,0:T(8,128)(2,1)S(1)}, u32[]{:S(2)}, u32[]{:S(2)}) collective-permute-start(bf16[64,512]{1,0:T(8,128)(2,1)S(1)} %add_convert_fusion.13), channel_id=1, source_target_pairs={{0,8},{2,10},{4,12},{6,14},{8,0},{10,2},{12,4},{14,6},{16,24},{18,... | collective-permute-start | bytes 196616 | tf_op jit(solution)/shard_map/ppermute | solution.py:258
  28.5 8.8 %collective-permute-start.16 = (bf16[128,512]{1,0:T(8,128)(2,1)S(1)}, bf16[128,512]{1,0:T(8,128)(2,1)S(1)}, u32[]{:S(2)}, u32[]{:S(2)}) collective-permute-start(bf16[128,512]{1,0:T(8,128)(2,1)S(1)} %add_convert_fusion.1), channel_id=1, source_target_pairs={{0,16},{2,18},{4,20},{6,22},{8,24},{10,26},{12,28},{14,30},{16,0},... | collective-permute-start | bytes 393224 | tf_op jit(solution)/shard_map/ppermute | solution.py:258
  32.6 4.8 %collective-permute-start.12 = (bf16[64,512]{1,0:T(8,128)(2,1)S(1)}, bf16[64,512]{1,0:T(8,128)(2,1)S(1)}, u32[]{:S(2)}, u32[]{:S(2)}) collective-permute-start(bf16[64,512]{1,0:T(8,128)(2,1)S(1)} %add_convert_fusion.9), channel_id=1, source_target_pairs={{0,4},{2,6},{4,0},{6,2},{8,12},{10,14},{12,8},{14,10},{16,20},{18,... | collective-permute-start | bytes 196616 | tf_op jit(solution)/shard_map/ppermute | solution.py:258
  34.2 5.5 %collective-permute-start.6 = (bf16[128,512]{1,0:T(8,128)(2,1)S(1)}, bf16[128,512]{1,0:T(8,128)(2,1)S(1)}, u32[]{:S(2)}, u32[]{:S(2)}) collective-permute-start(bf16[128,512]{1,0:T(8,128)(2,1)S(1)} %pad_maximum_fusion.p0), channel_id=1, source_target_pairs={{0,4},{2,6},{4,0},{6,2},{8,12},{10,14},{12,8},{14,10},{16,20},{18,... | collective-permute-start | bytes 393224 | tf_op jit(solution)/shard_map/ppermute | solution.py:258
  37.5 5.0 %collective-permute-start.17 = (bf16[128,512]{1,0:T(8,128)(2,1)S(1)}, bf16[128,512]{1,0:T(8,128)(2,1)S(1)}, u32[]{:S(2)}, u32[]{:S(2)}) collective-permute-start(bf16[128,512]{1,0:T(8,128)(2,1)S(1)} %get-tuple-element.54), channel_id=1, source_target_pairs={{0,8},{2,10},{4,12},{6,14},{8,0},{10,2},{12,4},{14,6},{16,24},{18,... | collective-permute-start | bytes 393224 | tf_op jit(solution)/shard_map/ppermute | solution.py:258
  37.5 5.0 %collective-permute-start.18 = (bf16[128,512]{1,0:T(8,128)(2,1)S(1)}, bf16[128,512]{1,0:T(8,128)(2,1)S(1)}, u32[]{:S(2)}, u32[]{:S(2)}) collective-permute-start(bf16[128,512]{1,0:T(8,128)(2,1)S(1)} %get-tuple-element.47), channel_id=1, source_target_pairs={{0,4},{2,6},{4,0},{6,2},{8,12},{10,14},{12,8},{14,10},{16,20},{18,... | collective-permute-start | bytes 393224 | tf_op jit(solution)/shard_map/ppermute | solution.py:258
  39.0 5.3 %collective-permute-start.5 = (bf16[128,512]{1,0:T(8,128)(2,1)S(1)}, bf16[128,512]{1,0:T(8,128)(2,1)S(1)}, u32[]{:S(2)}, u32[]{:S(2)}) collective-permute-start(bf16[128,512]{1,0:T(8,128)(2,1)S(1)} %pad_maximum_fusion.p0), channel_id=1, source_target_pairs={{0,2},{2,0},{4,6},{6,4},{8,10},{10,8},{12,14},{14,12},{16,18},{18,... | collective-permute-start | bytes 393224 | tf_op jit(solution)/shard_map/ppermute | solution.py:258
  39.0 10.9 %collective-permute-start.19 = (bf16[128,512]{1,0:T(8,128)(2,1)S(1)}, bf16[128,512]{1,0:T(8,128)(2,1)S(1)}, u32[]{:S(2)}, u32[]{:S(2)}) collective-permute-start(bf16[128,512]{1,0:T(8,128)(2,1)S(1)} %get-tuple-element.46), channel_id=1, source_target_pairs={{0,2},{2,0},{4,6},{6,4},{8,10},{10,8},{12,14},{14,12},{16,18},{18,... | collective-permute-start | bytes 393224 | tf_op jit(solution)/shard_map/ppermute | solution.py:258
  39.7 4.6 %collective-permute-start.7 = (bf16[128,512]{1,0:T(8,128)(2,1)S(1)}, bf16[128,512]{1,0:T(8,128)(2,1)S(1)}, u32[]{:S(2)}, u32[]{:S(2)}) collective-permute-start(bf16[128,512]{1,0:T(8,128)(2,1)S(1)} %collective-permute-done.6.p2), channel_id=1, source_target_pairs={{0,2},{2,0},{4,6},{6,4},{8,10},{10,8},{12,14},{14,12},{16,18},{18,... | collective-permute-start | bytes 393224 | tf_op jit(solution)/shard_map/ppermute | solution.py:258
  42.6 7.3 %collective-permute-start.20 = (bf16[128,512]{1,0:T(8,128)(2,1)S(1)}, bf16[128,512]{1,0:T(8,128)(2,1)S(1)}, u32[]{:S(2)}, u32[]{:S(2)}) collective-permute-start(bf16[128,512]{1,0:T(8,128)(2,1)S(1)} %get-tuple-element.52), channel_id=1, source_target_pairs={{0,2},{2,0},{4,6},{6,4},{8,10},{10,8},{12,14},{14,12},{16,18},{18,... | collective-permute-start | bytes 393224 | tf_op jit(solution)/shard_map/ppermute | solution.py:258
  42.7 12.9 %collective-permute-start.21 = (bf16[256,512]{1,0:T(8,128)(2,1)S(1)}, bf16[256,512]{1,0:T(8,128)(2,1)S(1)}, u32[]{:S(2)}, u32[]{:S(2)}) collective-permute-start(bf16[256,512]{1,0:T(8,128)(2,1)S(1)} %get-tuple-element.41), channel_id=1, source_target_pairs={{0,1},{1,0},{2,3},{3,2},{4,5},{5,4},{6,7},{7,6},{8,9},{9,8},{10,11... | collective-permute-start | bytes 786440 | tf_op jit(solution)/shard_map/ppermute | solution.py:261
  55.4 13.0 %collective-permute-start.23 = (bf16[512,512]{1,0:T(8,128)(2,1)S(1)}, bf16[512,512]{1,0:T(8,128)(2,1)S(1)}, u32[]{:S(2)}, u32[]{:S(2)}) collective-permute-start(bf16[512,512]{1,0:T(8,128)(2,1)S(1)} %get-tuple-element.38.mine), channel_id=1, source_target_pairs={{0,2},{2,0},{4,6},{6,4},{8,10},{10,8},{12,14},{14,12},{16,18},{18,... | collective-permute-start | bytes 1572872 | tf_op jit(solution)/shard_map/ppermute | solution.py:258
  58.0 8.7 %collective-permute-start.22 = (bf16[256,512]{1,0:T(8,128)(2,1)S(1)}, bf16[256,512]{1,0:T(8,128)(2,1)S(1)}, u32[]{:S(2)}, u32[]{:S(2)}) collective-permute-start(bf16[256,512]{1,0:T(8,128)(2,1)S(1)} %get-tuple-element.43), channel_id=1, source_target_pairs={{0,1},{1,0},{2,3},{3,2},{4,5},{5,4},{6,7},{7,6},{8,9},{9,8},{10,11... | collective-permute-start | bytes 786440 | tf_op jit(solution)/shard_map/ppermute | solution.py:261
